TPU v7x, 32 devices: a whole 2x2x4 slice. The times are simulated.
32 devices in a mesh: dp: 8 (over z, x), fsdp: 4 (over y, core).
Axes of the slice: x: 2, y: 2, z: 4, core: 2. Of those that a mesh axis runs over, the one named last changes fastest.
Arguments:
- tokens: bfloat16 [8, 1, 64, 64, 768], P('dp', None, 'fsdp'), may hold values from -6 to 6
- cotangent: bfloat16 [8, 1, 64, 64, 768], P('dp', None, 'fsdp'), may hold values from -6 to 6
- size_tags: int32 [8, 1], P('dp'), may hold values from 0 to 1
- step_ids: int32 [8, 1, 4], P('dp'), may hold values from 0 to 999
- ada_weight: bfloat16 [768, 4608], P(('dp', 'fsdp')), may hold values from -0.3125 to 0.3125
- ada_bias: bfloat16 [4608], P(('dp', 'fsdp')), may hold values from -3 to 3
- attn_kernel: bfloat16 [9, 768], P(None, ('dp', 'fsdp')), may hold values from -2 to 2
- attn_shift: bfloat16 [768], P(('dp', 'fsdp')), may hold values from -3 to 3
- qkv_weight: bfloat16 [768, 2304], P(('dp', 'fsdp')), may hold values from -0.21875 to 0.21875
- qv_bias: bfloat16 [2, 768], P(None, ('dp', 'fsdp')), may hold values from -3 to 3
- out_weight: bfloat16 [768, 768], P(('dp', 'fsdp')), may hold values from -1.75 to 1.75
- out_bias: bfloat16 [768], P(('dp', 'fsdp')), may hold values from -3 to 3
- up_weight: bfloat16 [768, 3072], P(('dp', 'fsdp')), may hold values from -0.21875 to 0.21875
- up_bias: bfloat16 [3072], P(('dp', 'fsdp')), may hold values from -3 to 3
- ffn_kernel: bfloat16 [9, 3072], P(None, ('dp', 'fsdp')), may hold values from -2 to 2
- ffn_shift: bfloat16 [3072], P(('dp', 'fsdp')), may hold values from -3 to 3
- down_weight: bfloat16 [3072, 768], P(('dp', 'fsdp')), may hold values from -0.109375 to 0.109375
- down_bias: bfloat16 [768], P(('dp', 'fsdp')), may hold values from -3 to 3
Outputs:
- block_out: bfloat16 [8, 1, 64, 64, 768], P('dp', None, 'fsdp')
- grad_tokens: bfloat16 [8, 1, 64, 64, 768], P('dp', None, 'fsdp')
- grad_ada_weight: float32 [768, 4608], P(('dp', 'fsdp'))
- grad_ada_bias: float32 [4608], P(('dp', 'fsdp'))
- grad_attn_kernel: float32 [9, 768], P(None, ('dp', 'fsdp'))
- grad_attn_shift: float32 [768], P(('dp', 'fsdp'))
- grad_qkv_weight: float32 [768, 2304], P(('dp', 'fsdp'))
- grad_qv_bias: float32 [2, 768], P(None, ('dp', 'fsdp'))
- grad_out_weight: float32 [768, 768], P(('dp', 'fsdp'))
- grad_out_bias: float32 [768], P(('dp', 'fsdp'))
- grad_up_weight: float32 [768, 3072], P(('dp', 'fsdp'))
- grad_up_bias: float32 [3072], P(('dp', 'fsdp'))
- grad_ffn_kernel: float32 [9, 3072], P(None, ('dp', 'fsdp'))
- grad_ffn_shift: float32 [3072], P(('dp', 'fsdp'))
- grad_down_weight: float32 [3072, 768], P(('dp', 'fsdp'))
- grad_down_bias: float32 [768], P(('dp', 'fsdp'))
Inputs may be any that keep to these rules, and one draw needn't show every extreme that they name: `size_tags`: 1 where a canvas holds one item of 64 x 64 tokens, 0 where its four quadrants are four items.
All inputs are finite; a program needn't handle non-finite values.
Results may differ from a plain program's by a relative error of at most 0.018.
Values may be sent and summed in bfloat16 or wider, within the bound.
No kernel may reach another device: no remote copies, remote signals or barrier semaphores. Data moves between devices by JAX's collectives and lax.ppermute only.
A program may use at most 384 MiB of HBM per device.

v0:
```python
from functools import partial
import math

import jax
import jax.numpy as jnp
from jax import lax
from jax.sharding import PartitionSpec as P

HEADS = 12
HDIM = 64


def with_halo(cells, sides, width):
    for axis, dim in sides:
        count = lax.axis_size(axis)
        ends = count - 1
        head = lax.slice_in_dim(cells, 0, width, axis=dim)
        tail = lax.slice_in_dim(cells, cells.shape[dim] - width, cells.shape[dim], axis=dim)
        cells = jnp.concatenate(
            [
                lax.ppermute(tail, axis, [(i, (i + 1) % count) for i in range(ends)]),
                cells,
                lax.ppermute(head, axis, [((i + 1) % count, i) for i in range(ends)]),
            ],
            axis=dim,
        )
    return cells


def layer_norm(values):
    centre = values - jnp.mean(values, axis=-1, keepdims=True)
    spread = jnp.mean(centre * centre, axis=-1, keepdims=True)
    return centre * lax.rsqrt(spread + 1e-06)


def embed_steps(chosen, width):
    half_width = width // 2
    frequency = jnp.exp(-math.log(10000.0) * jnp.arange(half_width, dtype=jnp.float32) / half_width)
    angles = chosen.astype(jnp.float32)[..., None] * frequency
    return jnp.concatenate([jnp.cos(angles), jnp.sin(angles)], axis=-1)


def spread_cols(vector, grid):
    return jnp.repeat(vector, grid // 2, axis=1)[:, None, :, :]


def per_quadrant(values):
    canvases, row_count, col_count, channels = values.shape
    return values.reshape(canvases, row_count, 2, col_count // 2, channels).sum(axis=(1, 3))


def tap_masks(big_item, first_row, row_count, grid):
    rows_here = first_row + jnp.arange(row_count)
    cols_here = jnp.arange(grid)
    row_masks = []
    col_masks = []
    for offset in (-1, 0, 1):
        row_same = (rows_here + offset >= grid // 2) == (rows_here >= grid // 2)
        col_same = (cols_here + offset >= grid // 2) == (cols_here >= grid // 2)
        row_masks.append(jnp.logical_or(big_item[:, None], row_same[None, :]).astype(jnp.float32))
        col_masks.append(jnp.logical_or(big_item[:, None], col_same[None, :]).astype(jnp.float32))
    return (row_masks, col_masks)


def with_rims(values):
    padded = with_halo(values, (("fsdp", 1),), 1)
    return jnp.pad(padded, ((0, 0), (0, 0), (1, 1), (0, 0)))


def apply_taps(padded, kernel, row_masks, col_masks, direction, row_count, grid):
    summed = jnp.zeros((padded.shape[0], row_count, grid, padded.shape[3]), jnp.float32)
    for row_off in (-1, 0, 1):
        for col_off in (-1, 0, 1):
            tap_index = (row_off + 1) * 3 + col_off + 1
            start_row = 1 + direction * row_off
            start_col = 1 + direction * col_off
            window = padded[
                :, start_row : start_row + row_count, start_col : start_col + grid, :
            ].astype(jnp.float32)
            gate_mask = (
                row_masks[direction * row_off + 1][:, :, None, None]
                * col_masks[direction * col_off + 1][:, None, :, None]
            )
            summed = summed + window * gate_mask * kernel[tap_index].astype(jnp.float32)
    return summed


def kernel_grads(padded, grads_out, row_masks, col_masks, row_count, grid):
    tap_rows = []
    for row_off in (-1, 0, 1):
        for col_off in (-1, 0, 1):
            window = padded[
                :, 1 + row_off : 1 + row_off + row_count, 1 + col_off : 1 + col_off + grid, :
            ].astype(jnp.float32)
            gate_mask = (
                row_masks[row_off + 1][:, :, None, None] * col_masks[col_off + 1][:, None, :, None]
            )
            tap_rows.append(jnp.sum(window * grads_out * gate_mask, axis=(0, 1, 2)))
    return jnp.stack(tap_rows)


def to_groups(values, row_count, grid):
    canvases, channels = (values.shape[0], values.shape[-1])
    shaped = values.reshape(canvases, row_count // 2, 2, grid // 2, 2, channels)
    return shaped.transpose(0, 2, 4, 1, 3, 5).reshape(canvases, 4, row_count * grid // 4, channels)


def from_groups(values, row_count, grid):
    canvases, channels = (values.shape[0], values.shape[-1])
    shaped = values.reshape(canvases, 2, 2, row_count // 2, grid // 2, channels)
    return shaped.transpose(0, 3, 1, 4, 2, 5).reshape(canvases, row_count, grid, channels)


def split_heads(values):
    return values.reshape(values.shape[0], values.shape[1], HEADS, values.shape[2] // HEADS)


def masked_scores(query_heads, key_heads, allowed):
    scores = jnp.einsum(
        "pqhd,pkhd->phqk", query_heads, key_heads, preferred_element_type=jnp.float32
    ) * HDIM ** (-0.5)
    return jnp.where(allowed[None, None], scores, -1e30)


def attend_forward(queries, keys_all, values_all, allowed):
    query_heads = split_heads(queries)
    scores = masked_scores(query_heads, split_heads(keys_all), allowed)
    row_top = jnp.max(scores, axis=-1, keepdims=True)
    log_total = row_top + jnp.log(jnp.sum(jnp.exp(scores - row_top), axis=-1, keepdims=True))
    weights_low = jnp.exp(scores - log_total).astype(jnp.bfloat16)
    attended = jnp.einsum(
        "phqk,pkhd->pqhd", weights_low, split_heads(values_all), preferred_element_type=jnp.float32
    )
    return (attended.astype(jnp.bfloat16).reshape(queries.shape), log_total)


def attend_backward(queries, keys_all, values_all, allowed, log_total, grad_attended):
    query_heads = split_heads(queries)
    key_heads = split_heads(keys_all)
    grad_heads = split_heads(grad_attended)
    weights = jnp.exp(masked_scores(query_heads, key_heads, allowed) - log_total)
    weights_low = weights.astype(jnp.bfloat16)
    grad_weights = jnp.einsum(
        "pqhd,pkhd->phqk", grad_heads, split_heads(values_all), preferred_element_type=jnp.float32
    )
    centred = jnp.sum(weights * grad_weights, axis=-1, keepdims=True)
    grad_scores = (weights * (grad_weights - centred)).astype(jnp.bfloat16)
    grad_query = jnp.einsum(
        "phqk,pkhd->pqhd", grad_scores, key_heads, preferred_element_type=jnp.float32
    ) * HDIM ** (-0.5)
    grad_key = jnp.einsum(
        "phqk,pqhd->pkhd", grad_scores, query_heads, preferred_element_type=jnp.float32
    ) * HDIM ** (-0.5)
    grad_value = jnp.einsum(
        "phqk,pqhd->pkhd", weights_low, grad_heads, preferred_element_type=jnp.float32
    )
    key_count = keys_all.shape[1]
    pair_grad = jnp.concatenate(
        [grad_key.reshape(4, key_count, -1), grad_value.reshape(4, key_count, -1)], axis=-1
    )
    return (grad_query.astype(jnp.bfloat16).reshape(queries.shape), pair_grad, centred)


def contract_rows(left_side, right_side):
    return lax.dot_general(
        left_side, right_side, (((0,), (0,)), ((), ())), preferred_element_type=jnp.float32
    )


def contract_cols(left_side, right_side):
    return lax.dot_general(
        left_side, right_side, (((1,), (1,)), ((), ())), preferred_element_type=jnp.float32
    )


def per_device(
    tokens,
    cotangent,
    size_tags,
    step_ids,
    ada_weight,
    ada_bias,
    attn_kernel,
    attn_shift,
    qkv_weight,
    qv_bias,
    out_weight,
    out_bias,
    up_weight,
    up_bias,
    ffn_kernel,
    ffn_shift,
    down_weight,
    down_bias,
):
    canvases, row_count, grid, width = (
        tokens.shape[1],
        tokens.shape[2],
        tokens.shape[3],
        tokens.shape[4],
    )
    token_count = canvases * row_count * grid
    fsdp_index = lax.axis_index("fsdp")
    first_row = fsdp_index * row_count
    row_half = (first_row >= grid // 2).astype(jnp.int32)
    big_item = size_tags[0] == 1
    row_masks, col_masks = tap_masks(big_item, first_row, row_count, grid)
    (
        ada_full,
        ada_bias_full,
        attn_kernel_full,
        attn_shift_full,
        qkv_full,
        qv_bias_full,
        out_full,
        out_bias_full,
    ) = (
        lax.all_gather(ada_weight, ("dp", "fsdp"), axis=0, tiled=True),
        lax.all_gather(ada_bias, ("dp", "fsdp"), axis=0, tiled=True),
        lax.all_gather(attn_kernel, ("dp", "fsdp"), axis=1, tiled=True),
        lax.all_gather(attn_shift, ("dp", "fsdp"), axis=0, tiled=True),
        lax.all_gather(qkv_weight, ("dp", "fsdp"), axis=0, tiled=True),
        lax.all_gather(qv_bias, ("dp", "fsdp"), axis=1, tiled=True),
        lax.all_gather(out_weight, ("dp", "fsdp"), axis=0, tiled=True),
        lax.all_gather(out_bias, ("dp", "fsdp"), axis=0, tiled=True),
    )
    step_rows = step_ids[0]
    chosen = jnp.where(big_item[:, None], step_rows[:, :1], step_rows)
    embedded = (
        jax.nn.silu(embed_steps(chosen, width)).astype(jnp.bfloat16).reshape(canvases * 4, width)
    )
    modulation = jnp.dot(
        embedded, ada_full, preferred_element_type=jnp.float32
    ) + ada_bias_full.astype(jnp.float32)
    modulation = modulation.reshape(canvases, 4, 6 * width)
    local_mod = lax.dynamic_slice_in_dim(modulation, 2 * row_half, 2, axis=1)
    shift_one, scale_one, gate_one, shift_two, scale_two, gate_two = [
        spread_cols(local_mod[:, :, piece_index * width : (piece_index + 1) * width], grid)
        for piece_index in range(6)
    ]
    inputs_float = tokens[0].astype(jnp.float32)
    normed_one = layer_norm(inputs_float)
    first = (normed_one * (1.0 + scale_one) + shift_one).astype(jnp.bfloat16)
    first_rims = with_rims(first)
    mixed = (
        apply_taps(first_rims, attn_kernel_full, row_masks, col_masks, 1, row_count, grid)
        + attn_shift_full.astype(jnp.float32)
    ).astype(jnp.bfloat16)
    bias_row = jnp.concatenate(
        [
            qv_bias_full[0].astype(jnp.float32),
            jnp.zeros((width,), jnp.float32),
            qv_bias_full[1].astype(jnp.float32),
        ]
    )
    projected = (
        jnp.dot(mixed.reshape(token_count, width), qkv_full, preferred_element_type=jnp.float32)
        + bias_row
    )
    grouped = to_groups(
        projected.astype(jnp.bfloat16).reshape(canvases, row_count, grid, 3 * width),
        row_count,
        grid,
    )
    queries = grouped[..., :width]
    pair_all = lax.all_gather(grouped[..., width:], "fsdp", axis=2, tiled=True)
    keys_all = pair_all[..., :width]
    values_all = pair_all[..., width:]
    group_rows = row_count // 2
    query_rows = (fsdp_index * group_rows + jnp.arange(group_rows) >= grid // 4).astype(jnp.int32)
    group_cols = (jnp.arange(grid // 2) >= grid // 4).astype(jnp.int32)
    query_quad = (2 * query_rows[:, None] + group_cols[None, :]).reshape(-1)
    key_rows = (jnp.arange(grid // 2) >= grid // 4).astype(jnp.int32)
    key_quad = (2 * key_rows[:, None] + group_cols[None, :]).reshape(-1)
    same_quad = query_quad[:, None] == key_quad[None, :]
    attended_list = []
    lse_list = []
    for canvas_index in range(canvases):
        allowed = jnp.logical_or(big_item[canvas_index], same_quad)
        attended_one, log_total = attend_forward(
            queries[canvas_index], keys_all[canvas_index], values_all[canvas_index], allowed
        )
        attended_list.append(attended_one)
        lse_list.append(log_total)
    merged = from_groups(jnp.stack(attended_list), row_count, grid).reshape(token_count, width)
    branch_one = (
        jnp.dot(merged, out_full, preferred_element_type=jnp.float32)
        + out_bias_full.astype(jnp.float32)
    ).reshape(canvases, row_count, grid, width)
    hidden_state = inputs_float + gate_one * branch_one
    up_full, up_bias_full, ffn_kernel_full, ffn_shift_full, down_full, down_bias_full = (
        lax.all_gather(up_weight, ("dp", "fsdp"), axis=0, tiled=True),
        lax.all_gather(up_bias, ("dp", "fsdp"), axis=0, tiled=True),
        lax.all_gather(ffn_kernel, ("dp", "fsdp"), axis=1, tiled=True),
        lax.all_gather(ffn_shift, ("dp", "fsdp"), axis=0, tiled=True),
        lax.all_gather(down_weight, ("dp", "fsdp"), axis=0, tiled=True),
        lax.all_gather(down_bias, ("dp", "fsdp"), axis=0, tiled=True),
    )
    hidden_units = up_full.shape[1]
    normed_two = layer_norm(hidden_state)
    second = (normed_two * (1.0 + scale_two) + shift_two).astype(jnp.bfloat16)
    expanded = (
        jnp.dot(second.reshape(token_count, width), up_full, preferred_element_type=jnp.float32)
        + up_bias_full.astype(jnp.float32)
    ).astype(jnp.bfloat16)
    expanded_rims = with_rims(expanded.reshape(canvases, row_count, grid, hidden_units))
    convolved = apply_taps(
        expanded_rims, ffn_kernel_full, row_masks, col_masks, 1, row_count, grid
    ) + ffn_shift_full.astype(jnp.float32)
    activated = (
        jax.nn.gelu(convolved, approximate=True)
        .astype(jnp.bfloat16)
        .reshape(token_count, hidden_units)
    )
    branch_two = (
        jnp.dot(activated, down_full, preferred_element_type=jnp.float32)
        + down_bias_full.astype(jnp.float32)
    ).reshape(canvases, row_count, grid, width)
    result = (hidden_state + gate_two * branch_two).astype(jnp.bfloat16)[None]
    back_attn_kernel, back_qkv, back_out, back_up, back_ffn_kernel, back_down = (
        lax.all_gather(attn_kernel, ("dp", "fsdp"), axis=1, tiled=True),
        lax.all_gather(qkv_weight, ("dp", "fsdp"), axis=0, tiled=True),
        lax.all_gather(out_weight, ("dp", "fsdp"), axis=0, tiled=True),
        lax.all_gather(up_weight, ("dp", "fsdp"), axis=0, tiled=True),
        lax.all_gather(ffn_kernel, ("dp", "fsdp"), axis=1, tiled=True),
        lax.all_gather(down_weight, ("dp", "fsdp"), axis=0, tiled=True),
    )
    grad_out = cotangent[0].astype(jnp.float32)
    grad_gate_two = per_quadrant(grad_out * branch_two)
    grad_branch_two = (gate_two * grad_out).astype(jnp.bfloat16).reshape(token_count, width)
    grad_down = contract_rows(activated, grad_branch_two)
    grad_down_bias = jnp.sum(grad_branch_two.astype(jnp.float32), axis=0)
    grad_activated = contract_cols(grad_branch_two, back_down).reshape(convolved.shape)
    unused_gelu, gelu_pull = jax.vjp(partial(jax.nn.gelu, approximate=True), convolved)
    grad_convolved = gelu_pull(grad_activated)[0].astype(jnp.bfloat16)
    grad_conv_float = grad_convolved.astype(jnp.float32)
    grad_ffn_shift = jnp.sum(grad_conv_float, axis=(0, 1, 2))
    grad_ffn_kernel = kernel_grads(
        expanded_rims, grad_conv_float, row_masks, col_masks, row_count, grid
    )
    grad_expanded = (
        apply_taps(
            with_rims(grad_convolved), back_ffn_kernel, row_masks, col_masks, -1, row_count, grid
        )
        .astype(jnp.bfloat16)
        .reshape(token_count, hidden_units)
    )
    grad_up = contract_rows(second.reshape(token_count, width), grad_expanded)
    grad_up_bias = jnp.sum(grad_expanded.astype(jnp.float32), axis=0)
    grad_second = contract_cols(grad_expanded, back_up).reshape(canvases, row_count, grid, width)
    grad_scale_two = per_quadrant(grad_second * normed_two)
    grad_shift_two = per_quadrant(grad_second)
    unused_two, norm_pull_two = jax.vjp(layer_norm, hidden_state)
    grad_hidden = grad_out + norm_pull_two(grad_second * (1.0 + scale_two))[0]
    grad_gate_one = per_quadrant(grad_hidden * branch_one)
    grad_branch_one = (gate_one * grad_hidden).astype(jnp.bfloat16).reshape(token_count, width)
    grad_out_weight = contract_rows(merged, grad_branch_one)
    grad_out_bias = jnp.sum(grad_branch_one.astype(jnp.float32), axis=0)
    grad_merged = contract_cols(grad_branch_one, back_out).astype(jnp.bfloat16)
    grad_grouped = to_groups(grad_merged.reshape(canvases, row_count, grid, width), row_count, grid)
    query_grads = []
    pair_parts = []
    centre_list = []
    for canvas_index in range(canvases):
        allowed = jnp.logical_or(big_item[canvas_index], same_quad)
        grad_query, pair_grad, centred = attend_backward(
            queries[canvas_index],
            keys_all[canvas_index],
            values_all[canvas_index],
            allowed,
            lse_list[canvas_index],
            grad_grouped[canvas_index],
        )
        query_grads.append(grad_query)
        pair_parts.append(pair_grad)
        centre_list.append(centred)
    pair_summed = lax.psum_scatter(
        jnp.stack(pair_parts).astype(jnp.bfloat16), "fsdp", scatter_dimension=2, tiled=True
    )
    grad_projected = from_groups(
        jnp.concatenate([jnp.stack(query_grads), pair_summed], axis=-1), row_count, grid
    ).reshape(token_count, 3 * width)
    grad_qkv = contract_rows(mixed.reshape(token_count, width), grad_projected)
    grad_projected_float = grad_projected.astype(jnp.float32)
    grad_qv_bias = jnp.stack(
        [
            jnp.sum(grad_projected_float[:, :width], axis=0),
            jnp.sum(grad_projected_float[:, 2 * width :], axis=0),
        ]
    )
    grad_mixed = (
        contract_cols(grad_projected, back_qkv)
        .astype(jnp.bfloat16)
        .reshape(canvases, row_count, grid, width)
    )
    grad_mixed_float = grad_mixed.astype(jnp.float32)
    grad_attn_shift = jnp.sum(grad_mixed_float, axis=(0, 1, 2))
    grad_attn_kernel = kernel_grads(
        first_rims, grad_mixed_float, row_masks, col_masks, row_count, grid
    )
    grad_first = apply_taps(
        with_rims(grad_mixed), back_attn_kernel, row_masks, col_masks, -1, row_count, grid
    )
    grad_scale_one = per_quadrant(grad_first * normed_one)
    grad_shift_one = per_quadrant(grad_first)
    unused_one, norm_pull_one = jax.vjp(layer_norm, inputs_float)
    grad_inputs = grad_hidden + norm_pull_one(grad_first * (1.0 + scale_one))[0]
    grad_tokens = grad_inputs.astype(jnp.bfloat16)[None]
    local_grad = jnp.concatenate(
        [
            grad_shift_one,
            grad_scale_one,
            grad_gate_one,
            grad_shift_two,
            grad_scale_two,
            grad_gate_two,
        ],
        axis=-1,
    )
    full_grad = lax.dynamic_update_slice_in_dim(
        jnp.zeros((canvases, 4, 6 * width), jnp.float32), local_grad, 2 * row_half, axis=1
    )
    full_grad = full_grad.reshape(canvases * 4, 6 * width)
    grad_ada = jnp.dot(embedded.astype(jnp.float32).T, full_grad, precision=lax.Precision.HIGHEST)
    grad_ada_bias = jnp.sum(full_grad, axis=0)
    shards = tuple(
        (
            lax.psum_scatter(grad_ada, ("dp", "fsdp"), scatter_dimension=0, tiled=True),
            lax.psum_scatter(grad_ada_bias, ("dp", "fsdp"), scatter_dimension=0, tiled=True),
            lax.psum_scatter(grad_attn_kernel, ("dp", "fsdp"), scatter_dimension=1, tiled=True),
            lax.psum_scatter(grad_attn_shift, ("dp", "fsdp"), scatter_dimension=0, tiled=True),
            lax.psum_scatter(grad_qkv, ("dp", "fsdp"), scatter_dimension=0, tiled=True),
            lax.psum_scatter(grad_qv_bias, ("dp", "fsdp"), scatter_dimension=1, tiled=True),
            lax.psum_scatter(grad_out_weight, ("dp", "fsdp"), scatter_dimension=0, tiled=True),
            lax.psum_scatter(grad_out_bias, ("dp", "fsdp"), scatter_dimension=0, tiled=True),
            lax.psum_scatter(grad_up, ("dp", "fsdp"), scatter_dimension=0, tiled=True),
            lax.psum_scatter(grad_up_bias, ("dp", "fsdp"), scatter_dimension=0, tiled=True),
            lax.psum_scatter(grad_ffn_kernel, ("dp", "fsdp"), scatter_dimension=1, tiled=True),
            lax.psum_scatter(grad_ffn_shift, ("dp", "fsdp"), scatter_dimension=0, tiled=True),
            lax.psum_scatter(grad_down, ("dp", "fsdp"), scatter_dimension=0, tiled=True),
            lax.psum_scatter(grad_down_bias, ("dp", "fsdp"), scatter_dimension=0, tiled=True),
        )
    )
    return (result, grad_tokens) + shards


def solution(mesh):
    placed = (
        P("dp", None, "fsdp", None, None),
        P("dp", None, "fsdp", None, None),
        P("dp", None),
        P("dp", None, None),
        P(("dp", "fsdp"), None),
        P(("dp", "fsdp")),
        P(None, ("dp", "fsdp")),
        P(("dp", "fsdp")),
        P(("dp", "fsdp"), None),
        P(None, ("dp", "fsdp")),
        P(("dp", "fsdp"), None),
        P(("dp", "fsdp")),
        P(("dp", "fsdp"), None),
        P(("dp", "fsdp")),
        P(None, ("dp", "fsdp")),
        P(("dp", "fsdp")),
        P(("dp", "fsdp"), None),
        P(("dp", "fsdp")),
    )
    return jax.shard_map(
        per_device,
        mesh=mesh,
        in_specs=placed,
        out_specs=(
            P("dp", None, "fsdp", None, None),
            P("dp", None, "fsdp", None, None),
            P(("dp", "fsdp"), None),
            P(("dp", "fsdp")),
            P(None, ("dp", "fsdp")),
            P(("dp", "fsdp")),
            P(("dp", "fsdp"), None),
            P(None, ("dp", "fsdp")),
            P(("dp", "fsdp"), None),
            P(("dp", "fsdp")),
            P(("dp", "fsdp"), None),
            P(("dp", "fsdp")),
            P(None, ("dp", "fsdp")),
            P(("dp", "fsdp")),
            P(("dp", "fsdp"), None),
            P(("dp", "fsdp")),
        ),
        check_vma=False,
    )
```

profile of v0, /device:TPU:0, one launch (start us, length us, event | category | flops | bytes accessed | tf_op | source)
XLA Modules:
  0.0 1714.4 jit_solution(11760897133954389206)
XLA Ops:
  14.5 43.2 %all-reduce.19 = (bf16[3072]{0:T(1024)(128)(2,1)S(1)}, bf16[4608]{0:T(1024)(128)(2,1)S(1)}, bf16[768]{0:T(1024)(128)(2,1)S(1)}, bf16[768]{0:T(1024)(128)(2,1)S(1...) all-reduce(bf16[3072]{0:T(1024)(128)(2,1)S(1)} %dynamic-update-slic, ...), channel_id=1, replica_groups=mesh['dp'=8,'fsdp'=4] {'dp','fsdp'}, use_global_device_ids=true, to_apply=%add.7 | all-reduce | flops 13056 | bytes 52224
  57.6 40.6 %all-gather.1 = bf16[32,24,2]{1,2,0:T(2,128)(2,1)S(1)} all-gather(bf16[1,24,2]{1,2,0:T(2,128)(2,1)} %bitcast.402), channel_id=1, replica_groups=mesh['dp'=8,'fsdp'=4] {'dp','fsdp'}, dimensions={0}, use_global_device_ids=true | all-gather | bytes 3168 | tf_op jit(solution)/shard_map/all_gather | solution.py:223
  98.3 37.5 %all-gather = bf16[32,24,9]{1,2,0:T(8,128)(2,1)S(1)} all-gather(bf16[1,24,9]{1,2,0:T(8,128)(2,1)} %bitcast.399), channel_id=1, replica_groups=mesh['dp'=8,'fsdp'=4] {'dp','fsdp'}, dimensions={0}, use_global_device_ids=true | all-gather | bytes 14256 | tf_op jit(solution)/shard_map/all_gather | solution.py:220
  140.2 4.0 fusion.185
  154.5 6.4 fusion.82
  160.9 8.0 add_convert_fusion.1
  168.9 10.2 reshape_reshape.15
  179.1 3.2 copy.69
  189.0 41.1 %all-gather.2 = bf16[32,96,9]{1,2,0:T(8,128)(2,1)S(1)} all-gather(bf16[1,96,9]{1,2,0:T(8,128)(2,1)S(1)} %bitcast.400), channel_id=1, replica_groups=mesh['dp'=8,'fsdp'=4] {'dp','fsdp'}, dimensions={0}, use_global_device_ids=true | all-gather | bytes 57024 | tf_op jit(solution)/shard_map/all_gather | solution.py:294
  235.6 33.7 %all-gather.14.cloned.1.call-done = bf16[1,4,1024,1536]{3,2,1,0:T(8,128)(2,1)} async-done(((bf16[1,4,256,1536]{3,2,1,0:T(8,128)(2,1)}), bf16[1,4,1024,1536]{3,2,1,0:T(8,128)(2,1)}) %all-gather.14.cloned.1.call-update) | async-done | bytes 12582928 | tf_op jit(solution)/shard_map/all_gather | solution.py:266
  269.3 10.4 fusion.193
  279.7 8.6 copy.72
  288.3 8.6 copy.70
  297.0 21.1 %fusion = (f32[4,12,256]{2,1,0:T(8,128)S(1)}, f32[4,12,256,1024]{3,2,1,0:T(8,128)}) fusion(pred[256,1024]{1,0:T(8,128)(4,1)S(1)} %compare_or_fusion, bf16[4,256,12,64]{1,3,2,0:T(8,128)(2,1)S(1)} %bitcast.340, bf16[4,1024,12,64]{1,3,2,0:T(8,128)(2,1)} %bitcast.315), kind=kOutput, calls=%fused_computation.16 | convolution fusion | flops 1648349184 | bytes 58507264 | tf_op jit(solution)/shard_map/pqhd,pkhd->phqk/dot_general | solution.py:119
  318.0 22.0 %exponential_reduce_fusion = f32[4,12,256]{2,1,0:T(8,128)S(1)} fusion(f32[4,12,256,1024]{3,2,1,0:T(8,128)} %get-tuple-element.121, f32[4,12,256]{2,1,0:T(8,128)S(1)} %get-tuple-element.120, pred[256,1024]{1,0:T(8,128)(4,1)S(1)} %compare_or_fusion), kind=kLoop, calls=%fused_computation.3 | loop fusion | flops 50319360 | bytes 50692096 | tf_op jit(solution)/shard_map/reduce_sum | solution.py:129
  340.1 21.2 %fusion.153 = bf16[4,256,12,64]{1,3,2,0:T(8,128)(2,1)S(1)} fusion(bf16[4,1024,12,64]{1,3,2,0:T(8,128)(2,1)} %bitcast.336, f32[4,12,256,1024]{3,2,1,0:T(8,128)} %get-tuple-element.121, f32[4,12,256]{2,1,0:T(8,128)S(1)} %log_add_fusion, pred[256,1024]{1,0:T(8,128)(4,1)S(1)} %compare_or_fusion), kind=kOutput, calls=%fused_computation.255 | convolution fusion | flops 1661730816 | bytes 58507264 | tf_op jit(solution)/shard_map/phqk,pkhd->pqhd/dot_general | solution.py:131
  361.3 4.7 copy.73
  366.0 6.1 reshape_stack_reshape.3
  375.1 11.7 reshape_reshape.16
  395.7 4.2 fusion.103
  400.0 7.5 add_convert_fusion
  413.5 3.5 select_maximum_fusion.2
  420.1 30.0 %multiply_convert_fusion.2 = (bf16[1,16,64,3072]{3,2,1,0:T(8,128)(2,1)}, f32[1,16,64,3072]{3,2,1,0:T(8,128)}) fusion(f32[3072]{0:T(1024)} %convert_element_type.839, f32[3072]{0:T(1024)} %bitcast.372, f32[16,64]{1,0:T(8,128)} %copy-done.58, bf16[1,18,66,3072]{3,2,1,0:T(8,128)(2,1)S(1)} %select_maximum_fusion.2, f32[3072]{0:T(1024)} %bitcast.374, ...), kind=kLoop, calls=%fused_computation.90 | loop fusion | flops 147849216 | bytes 63860736 | tf_op jit(solution)/shard_map/convert_element_type | solution.py:312
  450.2 5.7 all-gather.20.cloned.1.call-done
  456.6 23.2 %convert_reduce_fusion = (f32[3072]{0:T(1024)}, f32[3072]{0:T(1024)}, f32[3072]{0:T(1024)}, f32[3072]{0:T(1024)}, bf16[1,16,64,3072]{3,2,1,0:T(8,128)(2,1)S(1)}) fusion(f32[16,64]{1,0:T(8,128)} %copy-done.73, bf16[1024,3072]{1,0:T(8,128)(2,1)} %copy-done.12, f32[16,64]{1,0:T(8,128)} %copy-done.69, bf16[1,16,64,3072]{3,2,1,0:T(8,128)(2,1)} %bitcast.323, ...), kind=kOutput, calls=%fused_computation.5 | convolution fusion | flops 4947431424 | bytes 38793216 | tf_op jit(solution)/shard_map/dot_general | solution.py:171
  486.8 3.9 select_maximum_fusion
  490.8 24.0 %convert_reduce_fusion.1 = (f32[3072]{0:T(1024)}, bf16[1,16,64,3072]{3,2,1,0:T(8,128)(2,1)S(1)}) fusion(f32[3072]{0:T(1024)S(1)} %bitcast.373, f32[16,64]{1,0:T(8,128)S(1)} %get-tuple-element.111, bf16[1,18,66,3072]{3,2,1,0:T(8,128)(2,1)S(1)} %select_maximum_fusion, f32[3072]{0:T(1024)S(1)} %bitcast.375, f32[16,64]{1,0:T(8,128)S(1)} %copy-done.70, ...), kind=kLoop, calls=%fused_computation.88 | loop fusion | flops 125826048 | bytes 51277824 | tf_op jit(solution)/shard_map/reduce_sum | solution.py:349
  514.9 5.1 fusion.198
  522.9 3.8 fusion.191
  531.5 4.1 reshape_squeeze_reshape.3
  535.6 4.4 copy.77
  540.0 23.0 %convolution_convert_fusion = bf16[4,12,64,1024]{3,2,1,0:T(8,128)(2,1)} fusion(bf16[4,256,12,64]{1,3,2,0:T(8,128)(2,1)S(1)} %copy.77, f32[4,12,256,1024]{3,2,1,0:T(8,128)} %get-tuple-element.121, f32[4,12,256]{2,1,0:T(8,128)S(1)} %log_add_fusion, pred[256,1024]{1,0:T(8,128)(4,1)S(1)} %compare_or_fusion), kind=kOutput, calls=%fused_computation.141 | convolution fusion | flops 1664090112 | bytes 58507264 | tf_op jit(solution)/shard_map/phqk,pqhd->pkhd/dot_general | solution.py:154
  563.0 38.4 %multiply_reduce_fusion = (f32[4,12,256]{2,1,0:T(8,128)S(1)}, f32[4,12,256,1024]{3,2,1,0:T(8,128)}) fusion(f32[4,12,256,1024]{3,2,1,0:T(8,128)} %get-tuple-element.121, f32[4,12,256]{2,1,0:T(8,128)S(1)} %log_add_fusion, pred[256,1024]{1,0:T(8,128)(4,1)S(1)} %compare_or_fusion, bf16[4,256,12,64]{1,3,2,0:T(8,128)(2,1)S(1)} %copy.77, ...), kind=kOutput, calls=%fused_computation.1 | convolution fusion | flops 1673515008 | bytes 108888064 | tf_op jit(solution)/shard_map/pqhd,pkhd->phqk/dot_general | solution.py:143
  601.4 8.5 copy.81
  610.0 40.7 %multiply_convert_fusion = bf16[4,12,256,1024]{3,2,1,0:T(8,128)(2,1)} fusion(f32[4,12,256,1024]{3,2,1,0:T(8,128)} %get-tuple-element.123, f32[4,12,256,1024]{3,2,1,0:T(8,128)} %get-tuple-element.121, f32[4,12,256]{2,1,0:T(8,128)S(1)} %get-tuple-element.122, f32[4,12,256]{2,1,0:T(8,128)S(1)} %log_add_fusion, pred[256,1024]{1,0:T(8,128)(4,1)S(1)} %compare_or_fusion), kind=kLoop, calls=%fused_computation | loop fusion | flops 75497472 | bytes 126189568 | tf_op jit(solution)/shard_map/convert_element_type | solution.py:147
  650.7 15.3 multiply_convert_fusion.1
  665.9 8.6 copy.80
  674.6 10.4 pad_maximum_fusion
  687.5 25.9 %fusion.52 = (f32[3072]{0:T(1024)S(1)}, f32[3072]{0:T(1024)S(1)}, f32[3072]{0:T(1024)S(1)}, f32[3072]{0:T(1024)S(1)}, f32[3072]{0:T(1024)S(1)}, /*index=5*/f32[3072]{0:T(1024)S(1)}) fusion(bf16[1,16,64,3072]{3,2,1,0:T(8,128)(2,1)} %copy-done.10, f32[16,64]{1,0:T(8,128)S(1)} %copy-done.59, bf16[1,18,66,3072]{3,2,1,0:T(8,128)(2,1)} %copy-done, ...), kind=kLoop, calls=%fused_computation.81 | loop fusion | flops 78624768 | bytes 44138496 | tf_op jit(solution)/shard_map/reduce_sum | solution.py:98
  715.4 10.1 convolution_add_fusion.1
  725.7 15.7 fusion.154
  742.2 6.1 copy.78
  748.3 6.3 concatenate.85
  754.6 6.0 multiply_reduce_fusion.2
  760.7 29.7 %reduce-scatter.12.cloned.1.call-done = bf16[1,4,256,1536]{3,2,1,0:T(8,128)(2,1)} async-done(((bf16[1,4,1024,1536]{3,2,1,0:T(8,128)(2,1)}), bf16[1,4,256,1536]{3,2,1,0:T(8,128)(2,1)}) %reduce-scatter.12.cloned.1.call-update) | async-done | bytes 3145744 | tf_op jit(solution)/shard_map/reduce_scatter | solution.py:377
  790.3 4.8 maximum_bitcast_fusion
  795.1 9.4 copy.82
  804.5 10.6 reshape_reshape.18
  815.2 3.2 convert_element_type.882
  820.7 6.5 fusion.128
  846.9 8.2 fusion.140
  860.1 4.8 fusion.200
  865.1 10.2 fusion.64
  877.9 11.4 fusion.61
  889.6 9.6 fusion.199
  899.9 9.8 fusion.183
  909.7 4.8 add_convert_fusion.3
  918.0 6.0 fusion.152
  924.0 100.7 %all-reduce.22.cloned.1.call-done = (f32[4608]{0:T(1024)}, f32[9,768]{1,0:T(8,128)}, f32[768]{0:T(1024)}, f32[2,768]{1,0:T(2,128)}, f32[768]{0:T(1024)}, /*index=5*/f32[3072]{0:T(1024)}, f32[3072]{0:T(1024)}, f32[768]{0:T(1024)}) async-done(((f32[4608]{0:T(1024)}, f32[9,768]{1,0:T(8,128)}, f32[768]{0:T(1024)}, f32[2,768]{1,0:T(2,128)}, f32[768]{0:T(1024)}, /*index=5*/f32[3072]{0:T(1024)}, f32[3072]{0:T(1024)}, ...) | async-done | bytes 86032
  1035.0 96.0 %reduce-scatter.18.cloned.1.call-done = f32[24,768]{1,0:T(8,128)} async-done(((f32[768,768]{1,0:T(8,128)}), f32[24,768]{1,0:T(8,128)}) %reduce-scatter.18.cloned.1.call-update) | async-done | bytes 73744 | tf_op jit(solution)/shard_map/reduce_scatter | solution.py:434
  1131.0 141.7 %reduce-scatter.22.cloned.1.call-done = f32[96,768]{1,0:T(8,128)} async-done(((f32[3072,768]{1,0:T(8,128)}), f32[96,768]{1,0:T(8,128)}) %reduce-scatter.22.cloned.1.call-update) | async-done | bytes 294928 | tf_op jit(solution)/shard_map/reduce_scatter | solution.py:440
  1272.7 141.5 %reduce-scatter.20.cloned.1.call-done = f32[24,3072]{1,0:T(8,128)} async-done(((f32[768,3072]{1,0:T(8,128)}), f32[24,3072]{1,0:T(8,128)}) %reduce-scatter.20.cloned.1.call-update) | async-done | bytes 294928 | tf_op jit(solution)/shard_map/reduce_scatter | solution.py:436
  1414.2 124.8 %reduce-scatter.16.cloned.1.call-done = f32[24,2304]{1,0:T(8,128)} async-done(((f32[768,2304]{1,0:T(8,128)}), f32[24,2304]{1,0:T(8,128)}) %reduce-scatter.16.cloned.1.call-update) | async-done | bytes 221200 | tf_op jit(solution)/shard_map/reduce_scatter | solution.py:432
  1539.0 168.4 %reduce-scatter.14.cloned.1.call-done = f32[24,4608]{1,0:T(8,128)} async-done(((f32[768,4608]{1,0:T(8,128)}), f32[24,4608]{1,0:T(8,128)}) %reduce-scatter.14.cloned.1.call-update) | async-done | bytes 442384 | tf_op jit(solution)/shard_map/reduce_scatter | solution.py:428
  (479 shorter events, 118.3 us)
Async XLA Ops:
  7.2 131.7 %copy-start.1 = (bf16[1,1,16,64,768]{4,3,2,1,0:T(8,128)(2,1)S(1)}, bf16[1,1,16,64,768]{4,3,2,1,0:T(8,128)(2,1)}, u32[]{:S(2)}) copy-start(bf16[1,1,16,64,768]{4,3,2,1,0:T(8,128)(2,1)} %param.18) | copy-start | bytes 4718596
  7.2 133.0 %all-gather.10.cloned.1.call-start = ((), (), s32[]{:S(2)}) async-start(), calls=%async_computation.7 | async-start | bytes 7299072 | tf_op jit(solution)/shard_map/all_gather | solution.py:218
  7.9 152.9 %all-gather.12.cloned.1.call-start = ((), (), s32[]{:S(2)}) async-start(), calls=%async_computation.8 | async-start | bytes 3649536 | tf_op jit(solution)/shard_map/all_gather | solution.py:222
  8.7 260.6 %all-gather.14.cloned.1.call-start = ((), (), s32[]{:S(2)}) async-start(), calls=%async_computation.9 | async-start | bytes 15728640 | tf_op jit(solution)/shard_map/all_gather | solution.py:266
  136.2 16.9 copy-start.110
  136.2 16.9 copy-start.112
  136.2 16.9 copy-start.114
  136.3 16.9 copy-start.116
  136.3 16.9 copy-start.118
  136.3 16.9 copy-start.120
  136.3 16.9 copy-start.122
  136.3 16.9 copy-start.124
  136.3 16.9 copy-start.126
  140.1 13.2 copy-start.50
  140.1 13.2 copy-start.54
  140.1 13.2 copy-start.58
  140.1 13.2 copy-start.62
  140.1 13.2 copy-start.69
  140.1 13.2 copy-start.73
  140.2 13.2 copy-start.77
  140.2 350.5 %copy-start.46 = (f32[16,64]{1,0:T(8,128)}, f32[16,64]{1,0:T(8,128)S(1)}, u32[]{:S(2)}) copy-start(f32[16,64]{1,0:T(8,128)S(1)} %get-tuple-element.114) | copy-start | bytes 12292
  145.8 3.9 collective-permute-start
  148.1 4.2 collective-permute-start.1
  186.3 200.5 %all-gather.16.cloned.1.call-start = ((), (), s32[]{:S(2)}) async-start(), calls=%async_computation.10 | async-start | bytes 1216512 | tf_op jit(solution)/shard_map/all_gather | solution.py:224
  186.9 213.1 %all-gather.18.cloned.1.call-start = ((), (), s32[]{:S(2)}) async-start(), calls=%async_computation.11 | async-start | bytes 4866048 | tf_op jit(solution)/shard_map/all_gather | solution.py:292
  187.5 268.4 %all-gather.20.cloned.1.call-start = ((), (), s32[]{:S(2)}) async-start(), calls=%async_computation.12 | async-start | bytes 4866048 | tf_op jit(solution)/shard_map/all_gather | solution.py:296
  188.0 602.3 %reduce-scatter.12.cloned.1.call-start = ((), (), s32[]{:S(2)}) async-start(), calls=%async_computation.13 | async-start | bytes 15728640 | tf_op jit(solution)/shard_map/reduce_scatter | solution.py:377
  235.6 61.4 %copy-start.25 = (bf16[1,4,256,768]{2,3,1,0:T(8,128)(2,1)}, bf16[1,4,256,768]{2,3,1,0:T(8,128)(2,1)S(1)}, u32[]{:S(2)}) copy-start(bf16[1,4,256,768]{2,3,1,0:T(8,128)(2,1)S(1)} %copy.71) | copy-start | bytes 4718596
  399.9 11.2 copy-start.45
  407.4 9.6 copy-start.12
  407.5 4.3 collective-permute-start.2
  409.8 3.7 collective-permute-start.3
  456.6 23.2 %copy-start.34 = (f32[2,32,768]{2,1,0:T(8,128)}, f32[2,32,768]{2,1,0:T(8,128)S(1)}, u32[]{:S(2)}) copy-start(f32[2,32,768]{2,1,0:T(8,128)S(1)} %broadcast_in_dim.88) | copy-start | bytes 589828
  479.8 10.9 copy-start.10
  479.9 3.9 collective-permute-start.4
  482.2 8.5 copy-start.51
  482.2 8.5 copy-start.55
  482.2 8.5 copy-start.59
  482.2 8.5 copy-start.63
  482.2 8.5 copy-start.70
  482.2 8.5 copy-start.74
  482.2 8.5 copy-start.78
  482.2 8.5 copy-start.86
  482.2 8.5 copy-start.87
  482.3 4.5 collective-permute-start.5
  486.8 28.1 %slice-start = ((s8[4718592]{0:T(1024)(128)(4,1)}), s8[4194304]{0:T(1024)(128)(4,1)S(1)}, s32[]{:S(2)}) async-start(s8[4718592]{0:T(1024)(128)(4,1)} %bitcast.403), calls=%async_computation.21 | async-start | bytes 8388608
  490.8 24.1 %slice-start.1 = ((s8[4718592]{0:T(1024)(128)(4,1)}), s8[524288]{0:T(1024)(128)(4,1)S(1)}, s32[]{:S(2)}) async-start(s8[4718592]{0:T(1024)(128)(4,1)} %bitcast.403), calls=%async_computation.22 | async-start | bytes 1048576
  522.8 202.7 %copy-start.84 = (f32[16,64]{1,0:T(8,128)}, f32[16,64]{1,0:T(8,128)S(1)}, u32[]{:S(2)}) copy-start(f32[16,64]{1,0:T(8,128)S(1)} %multiply_reduce_fusion.3) | copy-start | bytes 12292
  609.9 40.7 %copy-start.26 = (bf16[1,4,256,768]{2,3,1,0:T(8,128)(2,1)S(1)}, bf16[1,4,256,768]{2,3,1,0:T(8,128)(2,1)}, u32[]{:S(2)}) copy-start(bf16[1,4,256,768]{2,3,1,0:T(8,128)(2,1)} %copy-done.25) | copy-start | bytes 4718596
  685.0 229.5 %reduce-scatter.24.cloned.1.call-start = ((), (), s32[]{:S(2)}) async-start(), calls=%async_computation.19 | async-start | bytes 1622016
  687.5 26.0 %copy-start.139 = (f32[3072]{0:T(1024)S(1)}, f32[3072]{0:T(1024)}, u32[]{:S(2)}) copy-start(f32[3072]{0:T(1024)} %get-tuple-element.29) | copy-start | bytes 36868
  687.5 26.0 %copy-start.140 = (f32[3072]{0:T(1024)S(1)}, f32[3072]{0:T(1024)}, u32[]{:S(2)}) copy-start(f32[3072]{0:T(1024)} %get-tuple-element.30) | copy-start | bytes 36868
  687.5 26.0 %copy-start.141 = (f32[3072]{0:T(1024)S(1)}, f32[3072]{0:T(1024)}, u32[]{:S(2)}) copy-start(f32[3072]{0:T(1024)} %get-tuple-element.31) | copy-start | bytes 36868
  715.3 309.3 %all-reduce.22.cloned.1.call-start = ((), (), s32[]{:S(2)}) async-start(), calls=%async_computation.20 | async-start | bytes 225280
  715.4 10.2 copy-start.102
  725.7 15.8 copy-start.9
  835.6 9.4 collective-permute-start.6
  837.8 7.2 collective-permute-start.7
  846.9 9.9 copy-start.83
  860.1 270.9 %reduce-scatter.18.cloned.1.call-start = ((), (), s32[]{:S(2)}) async-start(), calls=%async_computation.16 | async-start | bytes 2433024 | tf_op jit(solution)/shard_map/reduce_scatter | solution.py:434
  865.0 407.7 %reduce-scatter.22.cloned.1.call-start = ((), (), s32[]{:S(2)}) async-start(), calls=%async_computation.18 | async-start | bytes 9732096 | tf_op jit(solution)/shard_map/reduce_scatter | solution.py:440
  875.3 538.9 %reduce-scatter.20.cloned.1.call-start = ((), (), s32[]{:S(2)}) async-start(), calls=%async_computation.17 | async-start | bytes 9732096 | tf_op jit(solution)/shard_map/reduce_scatter | solution.py:436
  889.3 649.7 %reduce-scatter.16.cloned.1.call-start = ((), (), s32[]{:S(2)}) async-start(), calls=%async_computation.15 | async-start | bytes 7299072 | tf_op jit(solution)/shard_map/reduce_scatter | solution.py:432
  899.2 808.2 %reduce-scatter.14.cloned.1.call-start = ((), (), s32[]{:S(2)}) async-start(), calls=%async_computation.14 | async-start | bytes 14598144 | tf_op jit(solution)/shard_map/reduce_scatter | solution.py:428
  (105 other events, 436.3 us)
Sparse Core Ops, SparseCore 0:
  10.9 74.8 all-gather.9
  88.7 59.0 all-gather.11
  186.4 82.8 all-gather.13
  272.1 53.8 all-gather.15
  328.7 62.4 all-gather.17
  394.0 61.8 all-gather.19
  685.1 105.1 reduce-scatter.11
  795.6 97.9 reduce-scatter.23
  900.0 124.6 all-reduce.21
  1030.4 100.5 reduce-scatter.17
  1137.5 135.2 reduce-scatter.21
  1279.1 135.1 reduce-scatter.19
  1420.5 118.5 reduce-scatter.15
  1545.5 161.8 reduce-scatter.13
where the time goes:
time: 1720 us; the launch traced here: 1710 us
  waiting for transfers between devices  853 us (50%)
  matrix products  250 us (15%)
  other arithmetic  233 us (14%)
  local copies, waits for them, and re-layouts  184 us (11%)
  blocking collectives  162 us (9%)
  between operations  17.4 us (1%)
    reduce_scatter x1, waiting for transfers between devices, per_device(): lax.psum_scatter(grad_ada, ('dp', 'fsdp'), scatter_dimension=0, tiled=True)  168 us
    reduce_scatter x1, waiting for transfers between devices, per_device(): lax.psum_scatter(grad_down, ('dp', 'fsdp'), scatter_dimension=0, tiled=True)  142 us
    reduce_scatter x1, waiting for transfers between devices, per_device(): lax.psum_scatter(grad_up, ('dp', 'fsdp'), scatter_dimension=0, tiled=True)  141 us
    reduce_scatter x1, waiting for transfers between devices, per_device(): lax.psum_scatter(grad_qkv, ('dp', 'fsdp'), scatter_dimension=0, tiled=True)  125 us
    unnamed x16, waiting for transfers between devices  104 us
    reduce_scatter x1, waiting for transfers between devices, per_device(): lax.psum_scatter(grad_out_weight, ('dp', 'fsdp'), scatter_dimension=0, ti...  96 us
    unnamed x1, blocking collectives  43.2 us
    all_gather x1, blocking collectives, per_device(): lax.all_gather(ffn_kernel, ('dp', 'fsdp'), axis=1, tiled=True)  41.1 us
  transfers between devices with their start and end apart: 22, of which 12 were waited for; matrix products, arithmetic and copies ran while one was open for 24% of the time, Pallas kernels for 0%

commit v1 on v0

v1 whole, which is shorter than its diff:
```python
import functools
import math

import jax
import jax.numpy as jnp
from jax import lax
from jax.experimental import pallas as pl
from jax.experimental.pallas import tpu as pltpu
from jax.sharding import PartitionSpec as P

HEADS = 12
HDIM = 64
EVERY = ("dp", "fsdp")
F32 = jnp.float32
BF16 = jnp.bfloat16


def bits_of(axis):
    size = lax.axis_size(axis)
    count = size.bit_length() - 1
    assert 1 << count == size, axis
    return [(axis, 1 << k) for k in range(count)]


def my_bit(axis, bit):
    return (lax.axis_index(axis) // bit) % 2


def swap(value, axis, bit):
    size = lax.axis_size(axis)
    return lax.ppermute(value, axis, [(i, i ^ bit) for i in range(size)])


def by_bit(mine, other, flag, dim, join=jnp.stack):
    low = jnp.where(flag == 0, mine, other)
    high = jnp.where(flag == 0, other, mine)
    return join([low, high], axis=dim)


def halves(value, flag, dim):
    half = value.shape[dim] // 2
    keep = lax.dynamic_slice_in_dim(value, flag * half, half, axis=dim)
    give = lax.dynamic_slice_in_dim(value, (1 - flag) * half, half, axis=dim)
    return keep, give


def gather_small(value, bits):
    order = bits[::-1]
    for step, (axis, bit) in enumerate(order):
        value = by_bit(value, swap(value, axis, bit), my_bit(axis, bit), step)
    return value.reshape((1 << len(order),) + value.shape[len(order):])


def scatter_small(value, bits):
    sizes = [2] * len(bits)
    value = value.reshape(sizes + [value.shape[0] >> len(bits)] + list(value.shape[1:]))
    for step, (axis, bit) in enumerate(bits):
        dim = len(bits) - 1 - step
        flag = my_bit(axis, bit)
        keep, give = halves(value, flag, dim)
        value = keep + swap(give, axis, bit)
    return value.reshape(value.shape[len(bits):])


def exchange(blocks, axis):
    bits = bits_of(axis)
    value = blocks.reshape([2] * len(bits) + list(blocks.shape[1:]))
    for step, (name, bit) in enumerate(bits):
        dim = len(bits) - 1 - step
        flag = my_bit(name, bit)
        keep, give = halves(value, flag, dim)
        other = swap(give, name, bit)
        value = by_bit(keep, other, flag, dim, jnp.concatenate)
    return value.reshape(blocks.shape)


def with_halo(cells, axis, dim, width):
    count = lax.axis_size(axis)
    ends = count - 1
    head = lax.slice_in_dim(cells, 0, width, axis=dim)
    tail = lax.slice_in_dim(cells, cells.shape[dim] - width, cells.shape[dim], axis=dim)
    above = lax.ppermute(tail, axis, [(i, i + 1) for i in range(ends)])
    below = lax.ppermute(head, axis, [(i + 1, i) for i in range(ends)])
    return above, below


def layer_norm(values):
    centre = values - jnp.mean(values, axis=-1, keepdims=True)
    spread = jnp.mean(centre * centre, axis=-1, keepdims=True)
    rate = lax.rsqrt(spread + 1e-06)
    return centre * rate, rate


def layer_norm_back(grad, normed, rate):
    mean_grad = jnp.mean(grad, axis=-1, keepdims=True)
    mean_both = jnp.mean(grad * normed, axis=-1, keepdims=True)
    return rate * (grad - mean_grad - normed * mean_both)


def split_cols(values):
    shape = values.shape
    shaped = values.reshape(shape[:-2] + (shape[-2] // 2, 2, shape[-1]))
    return jnp.swapaxes(shaped, -3, -2)


def join_cols(values):
    shape = values.shape
    return jnp.swapaxes(values, -3, -2).reshape(shape[:-3] + (2 * shape[-2], shape[-1]))


def side_cells(cells, big):
    half = cells.shape[3]
    even, odd = cells[:, :, 0], cells[:, :, 1]
    spot = jnp.arange(half)[None, None, :, None]
    same = big[:, None, None, None]
    pad = ((0, 0), (0, 0), (1, 1), (0, 0))
    odd_down = jnp.pad(odd, pad)[:, :, :half] * jnp.where(spot == half // 2, same, 1.0)
    even_up = jnp.pad(even, pad)[:, :, 2:] * jnp.where(spot == half // 2 - 1, same, 1.0)
    left = jnp.stack([odd_down, even], axis=2)
    right = jnp.stack([odd, even_up], axis=2)
    return left, right


def conv(cells, kernel, big):
    cells = cells.astype(F32)
    rows = cells.shape[1] - 2
    left, right = side_cells(cells, big)
    total = 0.0
    for down in range(3):
        for across, part in enumerate((left, cells, right)):
            total = total + part[:, down : down + rows] * kernel[3 * down + across]
    return total


def tap_grads(cells, grads, big):
    cells = cells.astype(F32)
    rows = cells.shape[1] - 2
    left, right = side_cells(cells, big)
    sums = []
    for down in range(3):
        for part in (left, cells, right):
            sums.append(jnp.sum(part[:, down : down + rows] * grads, axis=(0, 1, 2, 3)))
    return jnp.stack(sums)


def item_sums(values):
    half = values.shape[3] // 2
    shaped = values.reshape(values.shape[:3] + (2, half, values.shape[-1]))
    return shaped.sum(axis=(1, 2, 4))


def spread_items(piece, grid):
    return jnp.repeat(piece, grid // 4, axis=1)[:, None, None]


def contract_rows(left_side, right_side):
    return lax.dot_general(
        left_side, right_side, (((0,), (0,)), ((), ())), preferred_element_type=F32
    )


def contract_cols(left_side, right_side):
    return lax.dot_general(
        left_side, right_side, (((1,), (1,)), ((), ())), preferred_element_type=F32
    )


def matmul(left_side, right_side):
    return jnp.dot(left_side, right_side, preferred_element_type=F32)


GELU_C = math.sqrt(2.0 / math.pi)
GELU_A = 0.044715


def shifted(values, mask, step):
    lead = values.shape[0] * 8
    flat = values.reshape(lead, values.shape[2])
    return pltpu.roll(flat, step % lead, axis=0).reshape(values.shape) * mask


def conv_row(load, taps):
    even_sum = odd_sum = None
    for down in range(3):
        even, odd, odd_down, even_up = load(down)
        left, centre, right = taps[3 * down : 3 * down + 3]
        even_part = left * odd_down + centre * even + right * odd
        odd_part = left * even + centre * odd + right * even_up
        even_sum = even_part if even_sum is None else even_sum + even_part
        odd_sum = odd_part if odd_sum is None else odd_sum + odd_part
    return even_sum, odd_sum


def ffn_body(canvases, rows, half, lanes, flag_ref, second_ref, grad_ref, up_ref, up_bias_ref, kernel_ref, shift_ref,
             down_ref, branch_ref, grad_second_ref, grad_up_ref, grad_down_ref, sums_ref,
             cells, cells_side, grads, grads_side, active, grad_cells, second_t):
    step = pl.program_id(0)
    width = second_ref.shape[1]
    block = up_ref.shape[1]
    grid = 2 * half
    group = half // 8
    tile = 256
    ext = rows + 4
    mid = rows + 2
    own = rows * grid

    @pl.when(step == 0)
    def _():
        branch_ref[...] = jnp.zeros_like(branch_ref)
        grad_second_ref[...] = jnp.zeros_like(grad_second_ref)
        for c in range(canvases):
            start = (c * ext + 2) * grid
            second_t[:, c * own : (c + 1) * own] = second_ref[start : start + own, :].T

    spot = lax.broadcasted_iota(jnp.int32, (group, 8, lanes), 0) * 8 + lax.broadcasted_iota(jnp.int32, (group, 8, lanes), 1)

    def masks(c):
        big = flag_ref[c, 0]
        down_mask = jnp.where(spot == 0, 0.0, jnp.where(spot == half // 2, big, 1.0))
        up_mask = jnp.where(spot == half - 1, 0.0, jnp.where(spot == half // 2 - 1, big, 1.0))
        return down_mask, up_mask

    @pl.loop(0, block // tile)
    def _(n):
        cols = pl.ds(pl.multiple_of(n * tile, tile), tile)
        product = matmul(second_ref[...], up_ref[:, cols]) + up_bias_ref[:, cols]
        cells[:, :, cols] = product.reshape(-1, 8, tile)
        weight = down_ref[pl.ds(pl.multiple_of(n * tile, tile), tile), :]
        grads[:, :, cols] = contract_cols(grad_ref[...], weight).reshape(-1, 8, tile)

    for c in range(canvases):
        @pl.when(flag_ref[c, 1] == 0)
        def _():
            cells[pl.ds(c * ext * grid // 8, 2 * grid // 8)] = jnp.zeros((2 * grid // 8, 8, block), F32)

        @pl.when(flag_ref[c, 2] == 0)
        def _():
            cells[pl.ds(((c + 1) * ext - 2) * grid // 8, 2 * grid // 8)] = jnp.zeros((2 * grid // 8, 8, block), F32)

    chunks = block // lanes
    per_row = grid // 8

    for c in range(canvases):
        down_mask, up_mask = masks(c)

        @pl.loop(0, ext)
        def _(r):
            base = (c * ext + r) * per_row
            for k in range(chunks):
                cols = slice(k * lanes, (k + 1) * lanes)
                even = cells[pl.ds(base, group), :, cols]
                odd = cells[pl.ds(base + group, group), :, cols]
                cells_side[pl.ds(base, group), :, cols] = shifted(odd, down_mask, 1)
                cells_side[pl.ds(base + group, group), :, cols] = shifted(even, up_mask, -1)

        @pl.loop(0, chunks)
        def _(k):
            cols = pl.ds(pl.multiple_of(k * lanes, lanes), lanes)
            taps = [kernel_ref[pl.ds(t, 1), cols][None] for t in range(9)]
            taps = [jnp.broadcast_to(t, (1, 8, lanes)) for t in taps]
            shift = jnp.broadcast_to(shift_ref[:, cols][None], (1, 8, lanes))

            @pl.loop(0, mid)
            def _(r):
                def load(down):
                    base = (c * ext + r + down) * per_row
                    return (cells[pl.ds(base, group), :, cols], cells[pl.ds(base + group, group), :, cols],
                            cells_side[pl.ds(base, group), :, cols], cells_side[pl.ds(base + group, group), :, cols])

                sums = conv_row(load, taps)
                here = (c * mid + r) * per_row
                outs = []
                for side in range(2):
                    v = sums[side] + shift
                    square = v * v
                    t = jnp.tanh(v * (GELU_C + (GELU_C * GELU_A) * square))
                    gate = 0.5 + 0.5 * t
                    slope = gate + (v * (2 * GELU_C + (6 * GELU_C * GELU_A) * square)) * (gate - gate * gate)
                    spots = pl.ds(here + side * group, group)
                    active[spots, :, cols] = (v * gate).astype(BF16)
                    outs.append(grads[spots, :, cols] * slope)
                    grads[spots, :, cols] = outs[-1]
                grads_side[pl.ds(here, group), :, cols] = shifted(outs[1], down_mask, 1)
                grads_side[pl.ds(here + group, group), :, cols] = shifted(outs[0], up_mask, -1)

        for row, flag in ((0, 1), (mid - 1, 2)):
            @pl.when(flag_ref[c, flag] == 0)
            def _():
                spots = pl.ds((c * mid + row) * per_row, per_row)
                grads[spots] = jnp.zeros((per_row, 8, block), F32)
                grads_side[spots] = jnp.zeros((per_row, 8, block), F32)

        @pl.loop(0, chunks)
        def _(k):
            cols = pl.ds(pl.multiple_of(k * lanes, lanes), lanes)
            taps = [kernel_ref[pl.ds(8 - t, 1), cols][None] for t in range(9)]
            taps = [jnp.broadcast_to(t, (1, 8, lanes)) for t in taps]

            def row_step(r, sums):
                def load_grads(down):
                    base = (c * mid + r + down) * per_row
                    return (grads[pl.ds(base, group), :, cols], grads[pl.ds(base + group, group), :, cols],
                            grads_side[pl.ds(base, group), :, cols], grads_side[pl.ds(base + group, group), :, cols])

                back_even, back_odd = conv_row(load_grads, taps)
                here = (c * rows + r) * per_row
                grad_cells[pl.ds(here, group), :, cols] = back_even.astype(BF16)
                grad_cells[pl.ds(here + group, group), :, cols] = back_odd.astype(BF16)
                mine = (c * mid + r + 1) * per_row
                g_even = grads[pl.ds(mine, group), :, cols]
                g_odd = grads[pl.ds(mine + group, group), :, cols]
                new = []
                for down in range(3):
                    base = (c * ext + r + 1 + down) * per_row
                    even = cells[pl.ds(base, group), :, cols]
                    odd = cells[pl.ds(base + group, group), :, cols]
                    odd_down = cells_side[pl.ds(base, group), :, cols]
                    even_up = cells_side[pl.ds(base + group, group), :, cols]
                    for for_even, for_odd in ((odd_down, even), (even, odd), (odd, even_up)):
                        new.append(jnp.sum(for_even * g_even + for_odd * g_odd, axis=0))
                new.append(jnp.sum(g_even + g_odd, axis=0))
                new.append(jnp.sum(back_even + back_odd, axis=0))
                return tuple(s + v for s, v in zip(sums, new))

            zero = jnp.zeros((8, lanes), F32)
            sums = lax.fori_loop(0, rows, row_step, (zero,) * 11)
            for t in range(11):
                total = jnp.sum(sums[t], axis=0, keepdims=True)
                if c == 0:
                    sums_ref[pl.ds(t, 1), cols] = total
                else:
                    sums_ref[pl.ds(t, 1), cols] += total

    for c in range(canvases):
        mine = slice(c * own, (c + 1) * own)
        act_rows = pl.ds((c * mid + 1) * per_row, rows * per_row)
        own_grad = grad_ref[(c * mid + 1) * grid : (c * mid + 1) * grid + own, :]

        @pl.loop(0, width // tile)
        def _(n):
            cols = pl.ds(pl.multiple_of(n * tile, tile), tile)
            branch_ref[mine, cols] += matmul(active[act_rows].reshape(own, block), down_ref[:, cols])
            weight = up_ref[pl.ds(pl.multiple_of(n * tile, tile), tile), :]
            spots = pl.ds(c * rows * per_row, rows * per_row)
            grad_second_ref[mine, cols] += contract_cols(grad_cells[spots].reshape(own, block), weight)

        @pl.loop(0, block // tile)
        def _(n):
            cols = pl.ds(pl.multiple_of(n * tile, tile), tile)
            part = contract_rows(active[act_rows, :, cols].reshape(own, tile), own_grad)
            if canvases == 1:
                grad_down_ref[cols, :] = part.astype(grad_down_ref.dtype)
            elif c == 0:
                grad_down_ref[cols, :] = part.astype(grad_down_ref.dtype)
            else:
                grad_down_ref[cols, :] += part.astype(grad_down_ref.dtype)

    @pl.loop(0, block // tile)
    def _(n):
        cols = pl.ds(pl.multiple_of(n * tile, tile), tile)
        grad_up_ref[:, cols] = matmul(second_t[...], grad_cells[:, :, cols].reshape(-1, tile)).astype(grad_up_ref.dtype)


def feed_forward(flags, second, grad_two, up, up_bias, kernel, shift, down, canvases, rows, half):
    width, hidden = up.shape
    block, lanes = 768, 128
    grid = 2 * half
    ext, mid, own = [canvases * n * grid for n in (rows + 4, rows + 2, rows)]
    kernel = jnp.pad(kernel, ((0, 7), (0, 0)))
    body = functools.partial(ffn_body, canvases, rows, half, lanes)
    fixed = lambda shape: pl.BlockSpec(shape, lambda i: (0, 0), pipeline_mode=pl.Buffered(1))
    cols = lambda n: pl.BlockSpec((n, block), lambda i: (0, i))
    return pl.pallas_call(
        body,
        grid=(hidden // block,),
        in_specs=[
            pl.BlockSpec(memory_space=pltpu.SMEM),
            fixed((ext, width)),
            fixed((mid, width)),
            cols(width),
            cols(1),
            cols(16),
            cols(1),
            pl.BlockSpec((block, width), lambda i: (i, 0)),
        ],
        out_specs=[
            pl.BlockSpec((own, width), lambda i: (0, 0)),
            pl.BlockSpec((own, width), lambda i: (0, 0)),
            cols(width),
            pl.BlockSpec((block, width), lambda i: (i, 0)),
            cols(16),
        ],
        out_shape=[
            jax.ShapeDtypeStruct((own, width), F32),
            jax.ShapeDtypeStruct((own, width), F32),
            jax.ShapeDtypeStruct((width, hidden), BF16),
            jax.ShapeDtypeStruct((hidden, width), BF16 if canvases == 1 else F32),
            jax.ShapeDtypeStruct((16, hidden), F32),
        ],
        scratch_shapes=[
            pltpu.VMEM((ext // 8, 8, block), F32),
            pltpu.VMEM((ext // 8, 8, block), F32),
            pltpu.VMEM((mid // 8, 8, block), F32),
            pltpu.VMEM((mid // 8, 8, block), F32),
            pltpu.VMEM((mid // 8, 8, block), BF16),
            pltpu.VMEM((own // 8, 8, block), BF16),
            pltpu.VMEM((width, own), BF16),
        ],
        compiler_params=pltpu.CompilerParams(vmem_limit_bytes=60 << 20, dimension_semantics=("arbitrary",)),
        cost_estimate=pl.CostEstimate(flops=36 * own * width * hidden // 3, bytes_accessed=40 << 20, transcendentals=own * hidden),
        name="feed_forward",
    )(flags, second, grad_two, up, up_bias[None], kernel, shift[None], down)


def one_head(pair, head):
    lane = lax.broadcasted_iota(jnp.int32, pair.shape, 1)
    return jnp.where((lane < HDIM) == (head == 0), pair, jnp.zeros_like(pair))


def attend_forward_body(tile, query_ref, key_ref, value_ref, query_item_ref, key_item_ref, out_ref, lse_ref, key_wide):
    tokens = query_ref.shape[0]
    pair = query_ref.shape[1]
    scale = HDIM ** -0.5
    key_wide[:, :pair] = key_ref[...]
    key_wide[:, pair:] = key_item_ref[...]

    @pl.loop(0, tokens // tile)
    def _(n):
        spots = pl.ds(pl.multiple_of(n * tile, tile), tile)
        query = query_ref[spots, :] * jnp.asarray(scale, BF16)
        outs = []
        for head in range(2):
            wide = jnp.concatenate([one_head(query, head), query_item_ref[spots, :]], axis=1)
            scores = contract_cols(wide, key_wide[...])
            top = jnp.max(scores, axis=1, keepdims=True)
            weights = jnp.exp(scores - top)
            total = jnp.sum(weights, axis=1, keepdims=True)
            outs.append(matmul(weights.astype(BF16), value_ref[...]) / total)
            lse = jnp.broadcast_to(top + jnp.log(total), (tile, 128))
            lse_ref[0, pl.ds(head, 1), spots] = lse.T[:1]
        lane = lax.broadcasted_iota(jnp.int32, outs[0].shape, 1)
        out_ref[spots, :] = jnp.where(lane < HDIM, outs[0], outs[1]).astype(BF16)


def attend_forward(projected, query_item, key_item):
    tokens = projected.shape[0]
    width = projected.shape[1] // 3
    pair = 2 * HDIM
    pairs = width // pair
    block = lambda k: pl.BlockSpec((tokens, pair), lambda i: (0, i + k * pairs))
    fixed = pl.BlockSpec((tokens, 128), lambda i: (0, 0))
    return pl.pallas_call(
        functools.partial(attend_forward_body, 256),
        grid=(pairs,),
        in_specs=[block(0), block(1), block(2), fixed, fixed],
        out_specs=[block(0), pl.BlockSpec((1, 8, tokens), lambda i: (i, 0, 0))],
        out_shape=[jax.ShapeDtypeStruct((tokens, width), BF16), jax.ShapeDtypeStruct((pairs, 8, tokens), F32)],
        scratch_shapes=[pltpu.VMEM((tokens, 2 * pair), BF16)],
        compiler_params=pltpu.CompilerParams(vmem_limit_bytes=40 << 20, dimension_semantics=("arbitrary",)),
        cost_estimate=pl.CostEstimate(flops=8 * tokens * tokens * width, bytes_accessed=8 << 20, transcendentals=tokens * tokens * width // HDIM),
        name="attend_forward",
    )(projected, projected, projected, query_item, key_item)


def attend_backward_body(tile, query_ref, key_ref, value_ref, query_item_ref, key_item_ref, grad_ref, out_ref, lse_ref,
                         result_ref, key_wide, key_t, query_t):
    tokens = query_ref.shape[0]
    pair = query_ref.shape[1]
    scale = HDIM ** -0.5
    key_wide[:, :pair] = key_ref[...]
    key_wide[:, pair:] = key_item_ref[...]
    key_t[...] = key_ref[...].T

    grad_key = [jnp.zeros((), F32)] * 2
    result_ref[1] = jnp.zeros_like(result_ref[1])
    result_ref[2] = jnp.zeros_like(result_ref[2])

    @pl.loop(0, tokens // tile)
    def _(n):
        spots = pl.ds(pl.multiple_of(n * tile, tile), tile)
        query = query_ref[spots, :] * jnp.asarray(scale, BF16)
        grad = grad_ref[spots, :]
        both = (grad.astype(F32) * out_ref[spots, :].astype(F32)).T
        keys_new = []
        values_new = []
        queries_new = []
        for head in range(2):
            own = slice(head * HDIM, (head + 1) * HDIM)
            centre = jnp.sum(both[own], axis=0, keepdims=True)
            wide = jnp.concatenate([one_head(query, head), query_item_ref[spots, :]], axis=1)
            weights = jnp.exp(contract_cols(key_wide[...], wide) - lse_ref[0, pl.ds(head, 1), spots])
            grad_weights = contract_cols(value_ref[...], one_head(grad, head))
            grad_scores = (weights * (grad_weights - centre)).astype(BF16)
            values_new.append(matmul(weights.astype(BF16), grad))
            keys_new.append(matmul(grad_scores, query))
            queries_new.append(matmul(key_t[...], grad_scores)[own])
        lane = lax.broadcasted_iota(jnp.int32, keys_new[0].shape, 1)
        result_ref[1] += jnp.where(lane < HDIM, keys_new[0], keys_new[1])
        result_ref[2] += jnp.where(lane < HDIM, values_new[0], values_new[1])
        query_t[:, spots] = jnp.concatenate(queries_new, axis=0)

    result_ref[0] = query_t[...].T * scale


def attend_backward_wrap(tile, query_ref, key_ref, value_ref, query_item_ref, key_item_ref, grad_ref, out_ref, lse_ref,
                         final_ref, sums_ref, result, key_wide, key_t, query_t):
    attend_backward_body(tile, query_ref, key_ref, value_ref, query_item_ref, key_item_ref, grad_ref, out_ref, lse_ref,
                         result, key_wide, key_t, query_t)
    final_ref[...] = result[...].astype(BF16)
    for k in range(3):
        sums_ref[k] = jnp.sum(result[k].reshape(-1, 8, result.shape[2]), axis=0)


def attend_backward(projected, query_item, key_item, grad, out, lse):
    tokens = projected.shape[0]
    width = projected.shape[1] // 3
    pair = 2 * HDIM
    pairs = width // pair
    block = lambda k: pl.BlockSpec((tokens, pair), lambda i: (0, i + k * pairs))
    fixed = pl.BlockSpec((tokens, 128), lambda i: (0, 0))
    return pl.pallas_call(
        functools.partial(attend_backward_wrap, 256),
        grid=(pairs,),
        in_specs=[block(0), block(1), block(2), fixed, fixed, block(0), block(0), pl.BlockSpec((1, 8, tokens), lambda i: (i, 0, 0))],
        out_specs=[pl.BlockSpec((3, tokens, pair), lambda i: (0, 0, i)), pl.BlockSpec((3, 8, pair), lambda i: (0, 0, i))],
        out_shape=[jax.ShapeDtypeStruct((3, tokens, width), BF16), jax.ShapeDtypeStruct((3, 8, width), F32)],
        scratch_shapes=[pltpu.VMEM((3, tokens, pair), F32), pltpu.VMEM((tokens, 2 * pair), BF16), pltpu.VMEM((pair, tokens), BF16), pltpu.VMEM((pair, tokens), F32)],
        compiler_params=pltpu.CompilerParams(vmem_limit_bytes=48 << 20, dimension_semantics=("arbitrary",)),
        cost_estimate=pl.CostEstimate(flops=20 * tokens * tokens * width, bytes_accessed=12 << 20, transcendentals=tokens * tokens * width // HDIM),
        name="attend_backward",
    )(projected, projected, projected, query_item, key_item, grad, out, lse)


def to_units(cells):
    canvases, rows, two, half, width = cells.shape
    shaped = cells.reshape(canvases, rows // 2, 2, two, half, width)
    return shaped.transpose(0, 2, 3, 1, 4, 5).reshape(canvases * 4, rows // 2, half, width)


def from_units(blocks, canvases):
    units, count, half, width = blocks.shape
    shaped = blocks.reshape(canvases, 2, 2, count, half, width)
    return shaped.transpose(0, 3, 1, 2, 4, 5).reshape(canvases, 2 * count, 2, half, width)


def unit_to_rows(values, half, rows, canvases):
    width = values.shape[-1]
    own = rows // 2
    padded = jnp.pad(values.reshape(half, half, width), ((1, 1), (0, 0), (0, 0)))
    blocks = jnp.stack(
        [padded[own * k : own * k + own + 2] for k in range(half // own)]
    )
    return from_units(exchange(blocks, "fsdp"), canvases)


def rows_to_unit(cells):
    blocks = exchange(to_units(cells), "fsdp")
    return blocks.reshape(-1, cells.shape[-1])


def per_device(
    tokens,
    cotangent,
    size_tags,
    step_ids,
    ada_weight,
    ada_bias,
    attn_kernel,
    attn_shift,
    qkv_weight,
    qv_bias,
    out_weight,
    out_bias,
    up_weight,
    up_bias,
    ffn_kernel,
    ffn_shift,
    down_weight,
    down_bias,
):
    canvases, rows, grid, width = tokens.shape[1:]
    half = grid // 2
    n_dp, n_fsdp = lax.axis_size("dp"), lax.axis_size("fsdp")
    count = n_dp * n_fsdp
    assert canvases * 4 == n_fsdp and rows * n_fsdp == grid
    fsdp_index = lax.axis_index("fsdp")
    every_bit = bits_of("fsdp") + bits_of("dp")
    hidden_units = up_weight.shape[1]
    shard = width // count
    ff_shard = hidden_units // count

    first_pair = lax.all_gather(
        jnp.concatenate([qkv_weight, out_weight], axis=1), EVERY, axis=0, tiled=True
    )
    qkv_full, out_full = first_pair[:, : 3 * width], first_pair[:, 3 * width :]
    up_rows = up_weight.reshape(shard, ff_shard * count // width, width).transpose(1, 0, 2)
    up_rows = up_rows.reshape(ff_shard, width)
    second_pair = lax.all_gather(
        jnp.concatenate([up_rows, down_weight], axis=0)[None], EVERY, axis=0, tiled=True
    )
    up_full = second_pair[:, :ff_shard].reshape(count, ff_shard // shard, shard, width)
    up_full = up_full.transpose(0, 2, 1, 3).reshape(width, hidden_units)
    down_full = second_pair[:, ff_shard:].reshape(hidden_units, width)

    parts = [
        ada_bias,
        attn_kernel,
        attn_shift,
        qv_bias,
        out_bias,
        up_bias,
        ffn_kernel,
        ffn_shift,
        down_bias,
        size_tags,
        step_ids,
    ]
    packed = gather_small(
        jnp.concatenate([part.astype(F32).reshape(-1) for part in parts]), every_bit
    )
    pieces = []
    start = 0
    for part in parts:
        size = math.prod(part.shape)
        pieces.append(packed[:, start : start + size])
        start += size
    whole = [
        piece.reshape((count,) + part.shape).swapaxes(0, 1).reshape(part.shape[0], -1)
        if part.ndim == 2
        else piece.reshape(-1)
        for piece, part in zip(pieces[:9], parts[:9])
    ]
    (
        ada_bias_full,
        attn_kernel_full,
        attn_shift_full,
        qv_bias_full,
        out_bias_full,
        up_bias_full,
        ffn_kernel_full,
        ffn_shift_full,
        down_bias_full,
    ) = whole
    tags = pieces[9].reshape(n_dp, n_fsdp, canvases)[:, 0].reshape(n_dp * canvases)
    steps = pieces[10].reshape(n_dp, n_fsdp, canvases, 4)[:, 0].reshape(n_dp * canvases, 4)

    chosen = jnp.where(tags[:, None] == 1, steps[:, :1], steps).reshape(-1)
    device = lax.axis_index("dp") * n_fsdp + fsdp_index
    feature = device * shard + jnp.arange(shard)
    half_width = width // 2
    frequency = jnp.exp(
        -math.log(10000.0) * (feature % half_width).astype(F32) / half_width
    )
    angles = chosen[:, None] * frequency
    embedded = jnp.where(feature < half_width, jnp.cos(angles), jnp.sin(angles))
    embedded = jax.nn.silu(embedded).astype(BF16)
    modulation = matmul(embedded, ada_weight)
    for axis, bit in bits_of("fsdp"):
        keep, give = halves(modulation, my_bit(axis, bit), 1)
        modulation = keep + swap(give, axis, bit)
    for axis, bit in bits_of("dp")[::-1]:
        keep, give = halves(modulation, my_bit(axis, bit), 0)
        modulation = keep + swap(give, axis, bit)
    for axis, bit in bits_of("fsdp")[::-1]:
        modulation = by_bit(
            modulation, swap(modulation, axis, bit), my_bit(axis, bit), 1, jnp.concatenate
        )
    modulation = (modulation + ada_bias_full).reshape(canvases, 4, 6 * width)
    first_row = fsdp_index * rows
    row_half = (first_row >= half).astype(jnp.int32)
    local_mod = lax.dynamic_slice_in_dim(modulation, 2 * row_half, 2, axis=1)
    shift_one, scale_one, gate_one, shift_two, scale_two, gate_two = [
        spread_items(local_mod[:, :, k * width : (k + 1) * width], grid) for k in range(6)
    ]

    big_item = size_tags[0] == 1
    big = big_item.astype(F32)
    edge = jnp.concatenate(
        [tokens[0][:, -2:], cotangent[0][:, -1:]], axis=1
    ), jnp.concatenate([tokens[0][:, :2], cotangent[0][:, :1]], axis=1)
    ends = n_fsdp - 1
    above = lax.ppermute(edge[0], "fsdp", [(i, i + 1) for i in range(ends)])
    below = lax.ppermute(edge[1], "fsdp", [(i + 1, i) for i in range(ends)])
    inputs = split_cols(jnp.concatenate([above[:, :2], tokens[0], below[:, :2]], axis=1))
    grad_out = split_cols(jnp.concatenate([above[:, 2:], cotangent[0], below[:, 2:]], axis=1))
    inputs = inputs.astype(F32)
    grad_out = grad_out.astype(F32)
    crosses_top = jnp.logical_and(first_row == half, jnp.logical_not(big_item))
    crosses_end = jnp.logical_and(first_row + rows == half, jnp.logical_not(big_item))
    top_ok = jnp.where(jnp.logical_or(fsdp_index == 0, crosses_top), 0.0, 1.0)
    end_ok = jnp.where(jnp.logical_or(fsdp_index == n_fsdp - 1, crosses_end), 0.0, 1.0)

    def keep_item(cells, extra):
        spot = jnp.arange(cells.shape[1])[None, :]
        flag = jnp.where(spot < extra, top_ok[:, None], 1.0)
        flag = jnp.where(spot >= cells.shape[1] - extra, end_ok[:, None], flag)
        return jnp.where(flag[:, :, None, None, None] > 0, cells, jnp.zeros_like(cells))

    normed_one, rate_one = layer_norm(inputs[:, 1:-1])
    first = keep_item((normed_one * (1.0 + scale_one) + shift_one).astype(BF16), 1)
    mixed = (conv(first, attn_kernel_full, big) + attn_shift_full).astype(BF16)
    mixed_unit = rows_to_unit(mixed)
    bias_row = jnp.concatenate([qv_bias_full[0], jnp.zeros((width,), F32), qv_bias_full[1]])
    projected = (matmul(mixed_unit, qkv_full) + bias_row).astype(BF16)
    unit_canvas = fsdp_index // 4
    unit_big = jnp.take(big_item, unit_canvas)
    side = (jnp.arange(half) >= half // 2).astype(jnp.int32)
    quad = (2 * side[:, None] + side[None, :]).reshape(-1)
    lane = jnp.arange(128)[None]
    hot = quad[:, None] == lane
    query_item = hot.astype(BF16)
    open_keys = jnp.logical_or(unit_big, jnp.logical_or(hot, lane >= 4))
    key_item = jnp.where(open_keys, 0.0, -1e30).astype(BF16)
    attended_unit, lse = attend_forward(projected, query_item, key_item)
    attended = unit_to_rows(attended_unit, half, rows, canvases)
    flat = attended.reshape(-1, width)
    branch_one = (matmul(flat, out_full) + out_bias_full).reshape(attended.shape)
    hidden = inputs + gate_one * branch_one
    normed_two, rate_two = layer_norm(hidden)
    second = (normed_two * (1.0 + scale_two) + shift_two).astype(BF16)

    own_shape = (canvases, rows, 2, half, width)
    grad_two_ext = (gate_two * grad_out).astype(BF16)
    grad_branch_two = grad_two_ext[:, 1:-1].reshape(-1, width)
    flags = jnp.stack([big, top_ok, end_ok], axis=1)
    branch_two, grad_second, grad_up, grad_down, ff_sums = feed_forward(
        flags,
        second.reshape(-1, width),
        grad_two_ext.reshape(-1, width),
        up_full,
        up_bias_full,
        ffn_kernel_full,
        ffn_shift_full,
        down_full,
        canvases,
        rows,
        half,
    )
    branch_two = (branch_two + down_bias_full).reshape(own_shape)
    grad_second = grad_second.reshape(own_shape)
    grad_ffn_kernel, grad_ffn_shift, grad_up_bias = ff_sums[:9], ff_sums[9], ff_sums[10]
    grad_up_rows = grad_up.astype(BF16).reshape(count, shard, ff_shard // shard, width)
    grad_up_rows = grad_up_rows.transpose(0, 2, 1, 3).reshape(count, ff_shard, width)
    ff_grads = jnp.concatenate(
        [grad_up_rows, grad_down.astype(BF16).reshape(count, ff_shard, width)], axis=1
    )
    ff_grads = lax.psum_scatter(ff_grads, EVERY, scatter_dimension=0, tiled=True)[0]
    grad_up = ff_grads[:ff_shard].reshape(ff_shard // shard, shard, width)
    grad_up = grad_up.transpose(1, 0, 2).reshape(shard, hidden_units).astype(F32)
    grad_down = ff_grads[ff_shard:].astype(F32)

    grad_own = grad_out[:, 1:-1]
    hidden_own = hidden[:, 2:-2]
    normed_two_own = normed_two[:, 2:-2]
    branch_one_own = branch_one[:, 2:-2]
    result = join_cols((hidden_own + gate_two * branch_two).astype(BF16))[None]
    grad_gate_two = item_sums(grad_own * branch_two)
    grad_down_bias = jnp.sum(grad_branch_two.astype(F32), axis=0)
    grad_scale_two = item_sums(grad_second * normed_two_own)
    grad_shift_two = item_sums(grad_second)
    grad_hidden = grad_own + layer_norm_back(
        grad_second * (1.0 + scale_two), normed_two_own, rate_two[:, 2:-2]
    )
    grad_gate_one = item_sums(grad_hidden * branch_one_own)
    grad_branch_one = (gate_one * grad_hidden).astype(BF16)
    flat_grad = grad_branch_one.reshape(-1, width)
    grad_out_bias = jnp.sum(flat_grad.astype(F32), axis=0)
    grad_attended = contract_cols(flat_grad, out_full).astype(BF16).reshape(own_shape)
    grad_unit = rows_to_unit(grad_attended)
    grad_out_weight = contract_rows(attended[:, 2:-2].reshape(-1, width), flat_grad)

    grad_parts, part_sums = attend_backward(
        projected, query_item, key_item, grad_unit, attended_unit, lse
    )
    grad_qkv = jnp.concatenate([contract_rows(mixed_unit, grad_parts[k]) for k in range(3)], axis=1)
    grad_qv_bias = jnp.stack([jnp.sum(part_sums[0], axis=0), jnp.sum(part_sums[2], axis=0)])
    grad_mixed_unit = sum(
        contract_cols(grad_parts[k], qkv_full[:, k * width : (k + 1) * width]) for k in range(3)
    ).astype(BF16)
    attn_grads = jnp.concatenate([grad_qkv, grad_out_weight], axis=1).astype(BF16)
    attn_grads = lax.psum_scatter(attn_grads, EVERY, scatter_dimension=0, tiled=True)
    grad_qkv = attn_grads[:, : 3 * width].astype(F32)
    grad_out_weight = attn_grads[:, 3 * width :].astype(F32)

    grad_mixed = unit_to_rows(grad_mixed_unit, half, rows, canvases)[:, 1:-1]
    grad_mixed = keep_item(grad_mixed, 1)
    own_mixed = grad_mixed[:, 1:-1].astype(F32)
    grad_attn_shift = jnp.sum(own_mixed, axis=(0, 1, 2, 3))
    grad_attn_kernel = tap_grads(first, own_mixed, big)
    grad_first = conv(grad_mixed, attn_kernel_full[::-1], big)
    normed_own = normed_one[:, 1:-1]
    grad_scale_one = item_sums(grad_first * normed_own)
    grad_shift_one = item_sums(grad_first)
    grad_inputs = grad_hidden + layer_norm_back(
        grad_first * (1.0 + scale_one), normed_own, rate_one[:, 1:-1]
    )
    grad_tokens = join_cols(grad_inputs.astype(BF16))[None]

    local_grad = jnp.concatenate(
        [
            grad_shift_one,
            grad_scale_one,
            grad_gate_one,
            grad_shift_two,
            grad_scale_two,
            grad_gate_two,
        ],
        axis=-1,
    )
    fsdp_bits = bits_of("fsdp")
    for axis, bit in fsdp_bits[:-1]:
        local_grad = local_grad + swap(local_grad, axis, bit)
    mod_grads = gather_small(local_grad, fsdp_bits[-1:] + bits_of("dp"))
    mod_grads = mod_grads.reshape(n_dp, 2, canvases, 2, 6 * width).transpose(0, 2, 1, 3, 4)
    mod_grads = mod_grads.reshape(n_dp * canvases * 4, 6 * width)
    grad_ada = jnp.dot(embedded.astype(F32).T, mod_grads, precision=lax.Precision.HIGHEST)
    bias_size = ada_bias.shape[0]
    grad_ada_bias = lax.dynamic_slice_in_dim(
        jnp.sum(mod_grads, axis=0), device * bias_size, bias_size
    )

    smalls = [
        grad_attn_kernel,
        grad_attn_shift,
        grad_qv_bias,
        grad_out_bias,
        grad_up_bias,
        grad_ffn_kernel,
        grad_ffn_shift,
        grad_down_bias,
    ]
    blocks = []
    for small in smalls:
        if small.ndim == 1:
            blocks.append(small.reshape(count, -1))
        else:
            lead = small.shape[0]
            blocks.append(small.reshape(lead, count, -1).swapaxes(0, 1).reshape(count, -1))
    summed = scatter_small(jnp.concatenate(blocks, axis=1), every_bit)[0]
    small_grads = []
    start = 0
    for small in smalls:
        size = math.prod(small.shape) // count
        piece = summed[start : start + size]
        small_grads.append(piece if small.ndim == 1 else piece.reshape(small.shape[0], -1))
        start += size
    (
        grad_attn_kernel,
        grad_attn_shift,
        grad_qv_bias,
        grad_out_bias,
        grad_up_bias,
        grad_ffn_kernel,
        grad_ffn_shift,
        grad_down_bias,
    ) = small_grads
    return (
        result,
        grad_tokens,
        grad_ada,
        grad_ada_bias,
        grad_attn_kernel,
        grad_attn_shift,
        grad_qkv,
        grad_qv_bias,
        grad_out_weight,
        grad_out_bias,
        grad_up,
        grad_up_bias,
        grad_ffn_kernel,
        grad_ffn_shift,
        grad_down,
        grad_down_bias,
    )


def solution(mesh):
    cells = P("dp", None, "fsdp", None, None)
    by_row = P(EVERY, None)
    by_col = P(None, EVERY)
    flat = P(EVERY)
    weights = (by_row, flat, by_col, flat, by_row, by_col, by_row, flat, by_row, flat, by_col, flat, by_row, flat)
    return jax.shard_map(
        per_device,
        mesh=mesh,
        in_specs=(cells, cells, P("dp", None), P("dp", None, None)) + weights,
        out_specs=(cells, cells) + weights,
        check_vma=False,
    )
```

time: 1720 us -> 706 us (0.41)
  waiting for transfers between devices: 853 us -> 208 us
  matrix products: 250 us -> 31.3 us
  Pallas kernels: 0 us -> 169 us
  blocking collectives: 162 us -> 0 us
  other arithmetic: 233 us -> 108 us
  local copies, waits for them, and re-layouts: 184 us -> 130 us
    reduce_scatter x6 -> x1, waiting for transfers between devices: 702 us -> 94 us  [per_device(): lax.psum_scatter(ff_grads, EVERY, scatter_dimension=0, tiled=True)[0]]
    pallas_call x0 -> x3, Pallas kernels: none -> 169 us  [the longest x1 96.1 us: feed_forward(): pl.pallas_call(body, grid=(hidden // block,), in_specs=[pl.BlockSpec(memo...]
    dot_general x12 -> x4, matrix products: 177 us -> 11.4 us  [the longest x3 10.1 us: matmul(): return jnp.dot(left_side, right_side, preferred_element_type=F32)]
    all_gather x3 -> x0, blocking collectives: 119 us -> none  [the longest x1 41.1 us: per_device(): lax.all_gather(ffn_kernel, ('dp', 'fsdp'), axis=1, tiled=True)]
    ppermute x8 -> x32, waiting for transfers between devices: 7.42 us -> 114 us  [the longest x30 114 us: swap(): return lax.ppermute(value, axis, [(i, i ^ bit) for i in range(size)])]
    unnamed x16 -> x5, waiting for transfers between devices: 104 us -> 0.07 us
    convert_element_type x22 -> x11, other arithmetic: 92.1 us -> 18.6 us  [the longest x1 6.36 us: per_device(): mixed = (conv(first, attn_kernel_full, big) + attn_shift_full).astype(BF16)]
    reduce_sum x16 -> x18, other arithmetic: 96.1 us -> 29.8 us  [the longest x9 18.1 us: item_sums(): return shaped.sum(axis=(1, 2, 4))]
  transfers between devices with their start and end apart: 22 -> 36, of which waited for: 12 -> 24; matrix products, arithmetic and copies ran while one was open for 24% -> 29% of each run, Pallas kernels for 0% -> 5%
where the time goes in v1:
time: 706 us; the launch traced here: 694 us
  waiting for transfers between devices  208 us (29%)
  Pallas kernels  169 us (24%)
  local copies, waits for them, and re-layouts  130 us (18%)
  other arithmetic  108 us (15%)
  matrix products  31.3 us (4%)
  starting transfers between devices  30.4 us (4%)
  between operations  17.4 us (2%)
    ppermute x30, waiting for transfers between devices, swap(): return lax.ppermute(value, axis, [(i, i ^ bit) for i in range(size)])  114 us
    pallas_call x1, Pallas kernels, feed_forward(): pl.pallas_call(body, grid=(hidden // block,), in_specs=[pl.BlockSpec(memo...  96.1 us
    reduce_scatter x1, waiting for transfers between devices, per_device(): lax.psum_scatter(ff_grads, EVERY, scatter_dimension=0, tiled=True)[0]  94 us
    pallas_call x1, Pallas kernels, attend_backward(): pl.pallas_call(functools.partial(attend_backward_wrap, 256), grid=(pairs,...  40 us
    pallas_call x1, Pallas kernels, attend_forward(): pl.pallas_call(functools.partial(attend_forward_body, 256), grid=(pairs,)...  32.9 us
    unnamed x244, local copies, waits for them, and re-layouts  30.6 us
    ppermute x30, starting transfers between devices, swap(): return lax.ppermute(value, axis, [(i, i ^ bit) for i in range(size)])  26.8 us
    reduce_sum x9, other arithmetic, item_sums(): return shaped.sum(axis=(1, 2, 4))  18.1 us
  transfers between devices with their start and end apart: 36, of which 24 were waited for; matrix products, arithmetic and copies ran while one was open for 29% of the time, Pallas kernels for 5%

profile of v1, /device:TPU:0, one launch (start us, length us, event | category | flops | bytes accessed | tf_op | source)
XLA Modules:
  0.0 694.4 jit_solution(17645806946741584947)
XLA Ops:
  12.7 4.1 concatenate.106
  16.8 4.1 collective-permute-start.2
  23.6 2.2 collective-permute-start
  36.7 3.6 collective-permute-start.5
  54.6 2.7 collective-permute-done.8
  58.5 10.5 %collective-permute-done.9 = f32[16,1152]{1,0:T(8,128)S(1)} collective-permute-done((f32[16,1152]{1,0:T(8,128)S(1)}, f32[16,1152]{1,0:T(8,128)S(1)}, u32[]{:S(2)}, u32[]{:S(2)}) %collective-permute-start.9) | collective-permute-done | bytes 73760 | tf_op jit(solution)/shard_map/ppermute | solution.py:31
  69.3 5.6 collective-permute-done.10
  76.0 2.8 collective-permute-done.11
  79.7 2.9 collective-permute-done.12
  88.6 2.2 fusion.26
  90.9 3.7 fusion.140
  94.7 6.4 fusion.33
  101.7 1.9 collective-permute-done.14
  107.0 22.8 %collective-permute-done.15 = bf16[1,2,8,32,768]{4,3,2,1,0:T(8,128)(2,1)} collective-permute-done((bf16[1,2,8,32,768]{4,3,2,1,0:T(8,128)(2,1)S(1)}, bf16[1,2,8,32,768]{4,3,2,1,0:T(8,128)(2,1)}, u32[]{:S(2)}, u32[]{:S(2)}) %collective-permute-start.15) | collective-permute-done | bytes 786464 | tf_op jit(solution)/shard_map/ppermute | solution.py:31
  132.5 6.1 add_convert_fusion.query_ref.key_ref.value_ref
  138.6 32.9 %attend_forward.1 = (bf16[1024,768]{1,0:T(8,128)(2,1)S(1)}, f32[6,8,1024]{2,1,0:T(8,128)S(1)}) custom-call(bf16[1024,2304]{1,0:T(8,128)(2,1)S(1)} %add_convert_fusion.query_ref.key_ref.value_ref, bf16[1024,2304]{1,0:T(8,128)(2,1)S(1)} %add_convert_fusion.query_ref.key_ref.value_ref, bf16[1024,2304]{1,0:T(8,128)(2,1)S(1)} %add_convert_fusion.query_ref.key_ref.value_ref, ...), custom_call_target="tpu_custom_call" | custom-call | flops 6442450944 | bytes 8388608 | tf_op jit(solution)/shard_map/attend_forward/pallas_call | solution.py:452
  172.2 2.6 collective-permute-done.16
  178.2 4.5 concatenate.116
  182.7 2.9 copy.353
  204.8 3.4 convert_bitcast_fusion.1
  211.6 3.7 convolution_add_fusion
  219.1 3.3 add_convert_fusion.1
  222.4 6.5 fusion.139
  228.9 2.3 copy.356
  231.3 3.3 copy.424
  234.5 96.1 %feed_forward.1 = (f32[1024,768]{1,0:T(8,128)}, f32[1024,768]{1,0:T(8,128)}, bf16[768,3072]{1,0:T(8,128)(2,1)}, bf16[3072,768]{1,0:T(8,128)(2,1)}, f32[16,3072]{1,0:T(8,128)}) custom-call(f32[1,3]{1,0:T(1,128)} %pad_maximum_fusion.26.flag_ref, bf16[1280,768]{1,0:T(8,128)(2,1)} %bitcast.390, bf16[1152,768]{1,0:T(8,128)(2,1)} %bitcast.377, ...), custom_call_target="tpu_custom_call" | custom-call | flops 28991029248 | bytes 41943040 | tf_op jit(solution)/shard_map/feed_forward/pallas_call | solution.py:373
  330.6 2.3 fusion.30
  333.5 3.5 multiply_reduce_fusion.8
  337.1 4.6 fusion.50
  343.6 3.4 convert_reduce_fusion.2
  347.0 2.7 convolution_convert_fusion
  350.0 2.3 collective-permute-done.18
  354.7 17.4 %collective-permute-done.19 = bf16[1,2,8,32,768]{4,3,2,1,0:T(8,128)(2,1)S(1)} collective-permute-done((bf16[1,2,8,32,768]{4,3,2,1,0:T(8,128)(2,1)S(1)}, bf16[1,2,8,32,768]{4,3,2,1,0:T(8,128)(2,1)S(1)}, u32[]{:S(2)}, u32[]{:S(2)}) %collective-permute-start.19) | collective-permute-done | bytes 786464 | tf_op jit(solution)/shard_map/ppermute | solution.py:31
  372.4 40.0 %attend_backward.1 = (bf16[3,1024,768]{2,1,0:T(8,128)(2,1)}, f32[3,8,768]{2,1,0:T(8,128)S(1)}) custom-call(bf16[1024,2304]{1,0:T(8,128)(2,1)} %copy-done.2, bf16[1024,2304]{1,0:T(8,128)(2,1)} %copy-done.2, bf16[1024,2304]{1,0:T(8,128)(2,1)} %copy-done.2, bf16[1024,128]{1,0:T(8,128)(2,1)S(1)} %fusion.92.query_item_ref, ...), custom_call_target="tpu_custom_call" | custom-call | flops 16106127360 | bytes 12582912 | tf_op jit(solution)/shard_map/attend_backward/pallas_call | solution.py:521
  412.4 3.0 fusion.63
  418.5 2.5 pad_maximum_fusion.1
  421.0 6.6 copy.404
  427.7 3.2 fusion.57
  430.9 3.2 fusion.61
  434.1 3.4 add_convert_fusion.3
  439.7 4.5 fusion.37
  445.2 10.2 %reshape.764 = bf16[32,24,4,768]{3,2,1,0:T(4,128)(2,1)} reshape(bf16[768,3072]{1,0:T(8,128)(2,1)} %get-tuple-element.32) | data formatting | bytes 9437184 | tf_op jit(solution)/shard_map/reshape | solution.py:742
  455.5 5.6 copy.395
  463.6 2.8 reduce_sum.336
  466.4 2.8 copy.358
  469.1 4.6 broadcast_in_dim_reshape.10
  476.9 7.7 %pad_maximum_fusion = bf16[32,192,768]{2,1,0:T(8,128)(2,1)} fusion(bf16[32,96,768]{2,1,0:T(8,128)(2,1)} %bitcast.380, bf16[32,96,768]{2,1,0:T(8,128)(2,1)} %bitcast.367), kind=kLoop, calls=%fused_computation | loop fusion | flops 18874368 | bytes 18874368 | tf_op jit(solution)/shard_map/concatenate | solution.py:744
  487.6 20.5 %collective-permute-done.21 = bf16[1,2,10,32,768]{4,3,1,0,2:T(8,128)(2,1)S(1)} collective-permute-done((bf16[1,2,10,32,768]{4,3,1,0,2:T(8,128)(2,1)}, bf16[1,2,10,32,768]{4,3,1,0,2:T(8,128)(2,1)S(1)}, u32[]{:S(2)}, u32[]{:S(2)}) %collective-permute-start.21) | collective-permute-done | bytes 983072 | tf_op jit(solution)/shard_map/ppermute | solution.py:31
  512.2 2.3 fusion.5
  515.3 2.1 multiply_reduce_fusion.2
  518.8 2.8 slice_bitcast_fusion.18
  521.5 3.4 slice_multiply_fusion.2
  528.8 1.9 fusion.46
  532.6 4.8 fusion.10
  539.7 7.7 %multiply_reduce_fusion.9 = (f32[32,768]{1,0:T(8,128)S(1)}, f32[16,2,32]{2,1,0:T(2,128)S(1)}, f32[16,2,32]{2,1,0:T(2,128)S(1)}, f32[32,768]{1,0:T(8,128)S(1)}, f32[1,16,2,32,768]{4,3,2,1,0:T(8,128)S(1)}) fusion(f32[1,18,2,32,768]{4,3,2,1,0:T(8,128)S(1)} %copy-done.13, f32[32,768]{1,0:T(8,128)S(1)} %bitcast.396, f32[768]{0:T(1024)S(1)} %copy-done.77, ...), kind=kLoop, calls=%fused_computation.98 | loop fusion | flops 18036736 | bytes 29028352 | tf_op jit(solution)/shard_map/reduce_sum | solution.py:149
  547.7 2.8 fusion.27
  555.5 1.9 collective-permute-done.23
  558.6 2.0 collective-permute-start.24
  560.6 1.8 collective-permute-done.28
  564.2 2.3 collective-permute-done.29
  567.9 2.4 collective-permute-done.30
  572.8 2.0 collective-permute-done.31
  579.1 5.0 collective-permute-done.26
  591.2 94.0 %reduce-scatter.5.cloned.1.call-done = bf16[1,192,768]{2,1,0:T(8,128)(2,1)} async-done(((bf16[32,192,768]{2,1,0:T(8,128)(2,1)}), bf16[1,192,768]{2,1,0:T(8,128)(2,1)}) %reduce-scatter.5.cloned.1.call-update) | async-done | bytes 294928 | tf_op jit(solution)/shard_map/reduce_scatter | solution.py:747
  (555 shorter events, 138.0 us)
Async XLA Ops:
  7.2 39.1 %copy-start = (bf16[24,4608]{1,0:T(8,128)(2,1)S(1)}, bf16[24,4608]{1,0:T(8,128)(2,1)}, u32[]{:S(2)}) copy-start(bf16[24,4608]{1,0:T(8,128)(2,1)} %param.22) | copy-start | bytes 663556
  7.2 33.3 %copy-start.36 = (bf16[1,1,16,64,768]{4,3,2,1,0:T(8,128)(2,1)S(1)}, bf16[1,1,16,64,768]{4,3,2,1,0:T(8,128)(2,1)}, u32[]{:S(2)}) copy-start(bf16[1,1,16,64,768]{4,3,2,1,0:T(8,128)(2,1)} %param.18) | copy-start | bytes 4718596
  7.2 23.3 %copy-start.60 = (bf16[96,768]{1,0:T(8,128)(2,1)S(1)}, bf16[96,768]{1,0:T(8,128)(2,1)}, u32[]{:S(2)}) copy-start(bf16[96,768]{1,0:T(8,128)(2,1)} %param.34) | copy-start | bytes 442372
  7.2 124.1 %all-gather.4.cloned.1.call-start = ((), (), s32[]{:S(2)}) async-start(), calls=%async_computation.2 | async-start | bytes 4866048 | tf_op jit(solution)/shard_map/all_gather | solution.py:592
  9.0 213.4 %all-gather.6.cloned.1.call-start = ((), (), s32[]{:S(2)}) async-start(), calls=%async_computation.4 | async-start | bytes 9732096 | tf_op jit(solution)/shard_map/all_gather | solution.py:598
  16.8 12.0 %collective-permute-start.2 = (f32[1541]{0:T(1024)S(1)}, f32[1541]{0:T(1024)S(1)}, u32[]{:S(2)}, u32[]{:S(2)}) collective-permute-start(f32[1541]{0:T(1024)S(1)} %concatenate.106), channel_id=1, source_target_pairs={{0,16},{4,20},{8,24},{12,28},{16,0},{20,4},{24,8},{28,12},{1,17},{... | collective-permute-start | bytes 18500 | tf_op jit(solution)/shard_map/ppermute | solution.py:31
  23.6 28.8 %collective-permute-start = (bf16[1,3,64,768]{3,2,1,0:T(8,128)(2,1)}, bf16[1,3,64,768]{3,2,1,0:T(8,128)(2,1)}, u32[]{:S(2)}, u32[]{:S(2)}) collective-permute-start(bf16[1,3,64,768]{3,2,1,0:T(8,128)(2,1)} %pad_maximum_fusion.12), channel_id=1, source_target_pairs={{0,1},{1,2},{2,3},{4,5},{5,6},{6,7},{8,9},{9,10},{10,11},{12,13},{... | collective-permute-start | bytes 884744 | tf_op jit(solution)/shard_map/ppermute | solution.py:682
  26.5 27.0 %collective-permute-start.1 = (bf16[1,3,64,768]{3,2,1,0:T(8,128)(2,1)}, bf16[1,3,64,768]{3,2,1,0:T(8,128)(2,1)}, u32[]{:S(2)}, u32[]{:S(2)}) collective-permute-start(bf16[1,3,64,768]{3,2,1,0:T(8,128)(2,1)} %pad_maximum_fusion.13), channel_id=1, source_target_pairs={{1,0},{2,1},{3,2},{5,4},{6,5},{7,6},{9,8},{10,9},{11,10},{13,12},{... | collective-permute-start | bytes 884744 | tf_op jit(solution)/shard_map/ppermute | solution.py:683
  28.9 3.8 collective-permute-start.3
  31.3 556.1 %reduce-scatter.7.cloned.1.call-start = ((), (), s32[]{:S(2)}) async-start(), calls=%async_computation.5 | async-start | bytes 4866048
  32.8 3.9 collective-permute-start.4
  36.7 6.7 collective-permute-start.5
  41.5 16.6 %copy-start.23 = (bf16[1,16,32,2,768]{4,2,3,1,0:T(8,128)(2,1)}, bf16[1,16,32,2,768]{4,2,3,1,0:T(8,128)(2,1)S(1)}, u32[]{:S(2)}) copy-start(bf16[1,16,32,2,768]{4,2,3,1,0:T(8,128)(2,1)S(1)} %copy.315) | copy-start | bytes 4718596
  43.5 1.4 collective-permute-start.6
  45.4 12.0 %copy-start.45 = (f32[32,1541]{1,0:T(8,128)}, f32[32,1541]{1,0:T(8,128)S(1)}, u32[]{:S(2)}) copy-start(f32[32,1541]{1,0:T(8,128)S(1)} %reshape.734) | copy-start | bytes 591748
  46.7 4.3 collective-permute-start.7
  47.9 39.5 %copy-start.72 = (f32[768]{0:T(1024)}, f32[768]{0:T(1024)S(1)}, u32[]{:S(2)}) copy-start(f32[768]{0:T(1024)S(1)} %mul.495) | copy-start | bytes 9220
  48.1 39.4 %copy-start.74 = (f32[768]{0:T(1024)}, f32[768]{0:T(1024)S(1)}, u32[]{:S(2)}) copy-start(f32[768]{0:T(1024)S(1)} %mul.504) | copy-start | bytes 9220
  49.8 44.8 %copy-start.76 = (f32[768]{0:T(1024)}, f32[768]{0:T(1024)S(1)}, u32[]{:S(2)}) copy-start(f32[768]{0:T(1024)S(1)} %mul.484) | copy-start | bytes 9220
  50.0 44.6 %copy-start.78 = (f32[768]{0:T(1024)}, f32[768]{0:T(1024)S(1)}, u32[]{:S(2)}) copy-start(f32[768]{0:T(1024)S(1)} %mul.487) | copy-start | bytes 9220
  50.1 44.5 %copy-start.80 = (f32[768]{0:T(1024)}, f32[768]{0:T(1024)S(1)}, u32[]{:S(2)}) copy-start(f32[768]{0:T(1024)S(1)} %mul.492) | copy-start | bytes 9220
  50.3 44.3 %copy-start.82 = (f32[768]{0:T(1024)}, f32[768]{0:T(1024)S(1)}, u32[]{:S(2)}) copy-start(f32[768]{0:T(1024)S(1)} %mul.501) | copy-start | bytes 9220
  51.1 6.2 collective-permute-start.8
  57.4 11.6 %collective-permute-start.9 = (f32[16,1152]{1,0:T(8,128)S(1)}, f32[16,1152]{1,0:T(8,128)S(1)}, u32[]{:S(2)}, u32[]{:S(2)}) collective-permute-start(f32[16,1152]{1,0:T(8,128)S(1)} %constant_dynamic-slice_fusion.17), channel_id=1, source_target_pairs={{0,16},{4,20},{8,24},{12,28},{16,0},{20,4},{24,8},{28,12},{1,17},{... | collective-permute-start | bytes 221192 | tf_op jit(solution)/shard_map/ppermute | solution.py:31
  58.5 26.2 %copy-start.5 = (f32[1,20,2,32,768]{4,3,2,1,0:T(8,128)}, f32[1,20,2,32,768]{4,3,2,1,0:T(8,128)S(1)}, u32[]{:S(2)}) copy-start(f32[1,20,2,32,768]{4,3,2,1,0:T(8,128)S(1)} %convert_bitcast_fusion) | copy-start | bytes 11796484
  69.0 6.0 collective-permute-start.10
  69.3 15.4 %copy-start.100 = (pred[18]{0:T(512)(128)(4,1)S(1)}, pred[18]{0:T(512)(128)(4,1)}, u32[]{:S(2)}) copy-start(pred[18]{0:T(512)(128)(4,1)} %fusion.128) | copy-start | bytes 58
  75.0 3.8 collective-permute-start.11
  76.0 9.6 %copy-start.54 = (f32[18,2,32]{2,1,0:T(2,128)}, f32[18,2,32]{2,1,0:T(2,128)S(1)}, u32[]{:S(2)}) copy-start(f32[18,2,32]{2,1,0:T(2,128)S(1)} %broadcast_multiply_fusion.2) | copy-start | bytes 13828
  78.8 3.8 collective-permute-start.12
  82.7 1.3 collective-permute-start.13
  86.5 8.2 %copy-start.17 = (f32[1,18,1,32,768]{4,3,2,1,0:T(8,128)}, f32[1,18,1,32,768]{4,3,2,1,0:T(8,128)S(1)}, u32[]{:S(2)}) copy-start(f32[1,18,1,32,768]{4,3,2,1,0:T(8,128)S(1)} %get-tuple-element.159) | copy-start | bytes 5308420
  87.4 7.2 %copy-start.15 = (f32[1,18,1,32,768]{4,3,2,1,0:T(8,128)}, f32[1,18,1,32,768]{4,3,2,1,0:T(8,128)S(1)}, u32[]{:S(2)}) copy-start(f32[1,18,1,32,768]{4,3,2,1,0:T(8,128)S(1)} %fusion.42) | copy-start | bytes 5308420
  101.2 2.4 collective-permute-start.14
  105.8 24.0 %collective-permute-start.15 = (bf16[1,2,8,32,768]{4,3,2,1,0:T(8,128)(2,1)S(1)}, bf16[1,2,8,32,768]{4,3,2,1,0:T(8,128)(2,1)}, u32[]{:S(2)}, u32[]{:S(2)}) collective-permute-start(bf16[1,2,8,32,768]{4,3,2,1,0:T(8,128)(2,1)S(1)} %fusion.89), channel_id=1, source_target_pairs={{0,2},{1,3},{2,0},{3,1},{4,6},{5,7},{6,4},{7,5},{8,10},{9,11},{10,... | collective-permute-start | bytes 2359304 | tf_op jit(solution)/shard_map/ppermute | solution.py:31
  138.5 32.9 %copy-start.2 = (bf16[1024,2304]{1,0:T(8,128)(2,1)}, bf16[1024,2304]{1,0:T(8,128)(2,1)S(1)}, u32[]{:S(2)}) copy-start(bf16[1024,2304]{1,0:T(8,128)(2,1)S(1)} %add_convert_fusion.query_ref.key_ref.value_ref) | copy-start | bytes 14155780
  172.1 2.6 collective-permute-start.16
  176.9 33.0 %collective-permute-start.17 = (bf16[1,2,10,32,768]{4,3,1,0,2:T(8,128)(2,1)}, bf16[1,2,10,32,768]{4,3,1,0,2:T(8,128)(2,1)}, u32[]{:S(2)}, u32[]{:S(2)}) collective-permute-start(bf16[1,2,10,32,768]{4,3,1,0,2:T(8,128)(2,1)} %fusion.85), channel_id=1, source_target_pairs={{0,2},{1,3},{2,0},{3,1},{4,6},{5,7},{6,4},{7,5},{8,10},{9,11},{10,... | collective-permute-start | bytes 2949128 | tf_op jit(solution)/shard_map/ppermute | solution.py:31
  197.6 10.7 %copy-start.94 = (f32[2,768]{1,0:T(2,128)S(1)}, f32[2,768]{1,0:T(2,128)}, u32[]{:S(2)}) copy-start(f32[2,768]{1,0:T(2,128)} %get-tuple-element.239) | copy-start | bytes 18436
  349.9 2.4 collective-permute-start.18
  352.5 19.6 %collective-permute-start.19 = (bf16[1,2,8,32,768]{4,3,2,1,0:T(8,128)(2,1)S(1)}, bf16[1,2,8,32,768]{4,3,2,1,0:T(8,128)(2,1)S(1)}, u32[]{:S(2)}, u32[]{:S(2)}) collective-permute-start(bf16[1,2,8,32,768]{4,3,2,1,0:T(8,128)(2,1)S(1)} %fusion.87), channel_id=1, source_target_pairs={{0,2},{1,3},{2,0},{3,1},{4,6},{5,7},{6,4},{7,5},{8,10},{9,11},{10,... | collective-permute-start | bytes 2359304 | tf_op jit(solution)/shard_map/ppermute | solution.py:31
  372.4 40.0 %copy-start.44 = (bf16[2,2,8,32,768]{4,3,2,1,0:T(8,128)(2,1)S(1)}, bf16[2,2,8,32,768]{4,3,2,1,0:T(8,128)(2,1)}, u32[]{:S(2)}) copy-start(bf16[2,2,8,32,768]{4,3,2,1,0:T(8,128)(2,1)} %copy-done.43) | copy-start | bytes 4718596
  427.6 257.6 %reduce-scatter.5.cloned.1.call-start = ((), (), s32[]{:S(2)}) async-start(), calls=%async_computation.3 | async-start | bytes 9732096 | tf_op jit(solution)/shard_map/reduce_scatter | solution.py:747
  439.1 34.7 %collective-permute-start.20 = (bf16[2,1,10,32,768]{4,3,1,0,2:T(8,128)(2,1)}, bf16[2,1,10,32,768]{4,3,1,0,2:T(8,128)(2,1)}, u32[]{:S(2)}, u32[]{:S(2)}) collective-permute-start(bf16[2,1,10,32,768]{4,3,1,0,2:T(8,128)(2,1)} %copy.415), channel_id=1, source_target_pairs={{0,1},{1,0},{2,3},{3,2},{4,5},{5,4},{6,7},{7,6},{8,9},{9,8},{10,11... | collective-permute-start | bytes 2949128 | tf_op jit(solution)/shard_map/ppermute | solution.py:31
  476.2 31.9 %collective-permute-start.21 = (bf16[1,2,10,32,768]{4,3,1,0,2:T(8,128)(2,1)}, bf16[1,2,10,32,768]{4,3,1,0,2:T(8,128)(2,1)S(1)}, u32[]{:S(2)}, u32[]{:S(2)}) collective-permute-start(bf16[1,2,10,32,768]{4,3,1,0,2:T(8,128)(2,1)} %fusion.83), channel_id=1, source_target_pairs={{0,2},{1,3},{2,0},{3,1},{4,6},{5,7},{6,4},{7,5},{8,10},{9,11},{10,... | collective-permute-start | bytes 2949128 | tf_op jit(solution)/shard_map/ppermute | solution.py:31
  521.5 7.2 %copy-start.109 = (f32[32]{0:T(128)S(1)}, f32[32]{0:T(128)}, u32[]{:S(2)}) copy-start(f32[32]{0:T(128)} %get-tuple-element.262) | copy-start | bytes 388
  532.5 7.1 %copy-start.30 = (f32[1,16,2,32,768]{4,3,1,2,0:T(8,128)S(1)}, f32[1,16,2,32,768]{4,3,1,2,0:T(8,128)}, u32[]{:S(2)}) copy-start(f32[1,16,2,32,768]{4,3,1,2,0:T(8,128)} %get-tuple-element.152) | copy-start | bytes 9437188
  532.5 7.1 %copy-start.42 = (f32[2,16,768]{2,1,0:T(8,128)S(1)}, f32[2,16,768]{2,1,0:T(8,128)}, u32[]{:S(2)}) copy-start(f32[2,16,768]{2,1,0:T(8,128)} %copy-done.41) | copy-start | bytes 294916
  539.7 7.8 %copy-start.27 = (f32[1280,768]{1,0:T(8,128)S(1)}, f32[1280,768]{1,0:T(8,128)}, u32[]{:S(2)}) copy-start(f32[1280,768]{1,0:T(8,128)} %copy-done.26) | copy-start | bytes 11796484
  539.7 7.8 %copy-start.71 = (f32[16,2,32]{2,1,0:T(2,128)S(1)}, f32[16,2,32]{2,1,0:T(2,128)}, u32[]{:S(2)}) copy-start(f32[16,2,32]{2,1,0:T(2,128)} %slice_bitcast_fusion.7) | copy-start | bytes 12292
  550.6 1.3 collective-permute-start.22
  551.9 5.5 collective-permute-start.23
  552.1 6.1 collective-permute-start.27
  558.4 4.1 collective-permute-start.28
  558.6 5.5 collective-permute-start.24
  562.5 3.9 collective-permute-start.29
  566.5 3.7 collective-permute-start.30
  570.3 4.6 collective-permute-start.31
  571.3 5.6 collective-permute-start.25
  577.0 9.1 %copy-start.99 = (f32[32]{0:T(128)S(1)}, f32[32]{0:T(128)}, u32[]{:S(2)}) copy-start(f32[32]{0:T(128)} %copy-done.98) | copy-start | bytes 388
  577.0 9.1 %copy-start.103 = (f32[24]{0:T(128)S(1)}, f32[24]{0:T(128)}, u32[]{:S(2)}) copy-start(f32[24]{0:T(128)} %copy-done.102) | copy-start | bytes 292
  577.0 9.1 %copy-start.105 = (pred[24]{0:T(512)(128)(4,1)S(1)}, pred[24]{0:T(512)(128)(4,1)}, u32[]{:S(2)}) copy-start(pred[24]{0:T(512)(128)(4,1)} %copy-done.104) | copy-start | bytes 76
  577.3 6.8 collective-permute-start.26
  585.0 102.7 %copy-start.1 = (bf16[24,4608]{1,0:T(8,128)(2,1)S(1)}, bf16[24,4608]{1,0:T(8,128)(2,1)}, u32[]{:S(2)}) copy-start(bf16[24,4608]{1,0:T(8,128)(2,1)} %param.22) | copy-start | bytes 663556
  (83 other events, 282.6 us)
Sparse Core Ops, SparseCore 0:
  10.9 67.1 all-gather.3
  81.6 82.3 all-gather.5
  427.8 116.5 reduce-scatter.6
  550.1 135.0 reduce-scatter.4

commit v2 on v1

--- a/solution.py
+++ b/solution.py
@@ -60,97 +60,6 @@
         keep, give = halves(value, flag, dim)
         value = keep + swap(give, axis, bit)
     return value.reshape(value.shape[len(bits):])
-
-
-def exchange(blocks, axis):
-    bits = bits_of(axis)
-    value = blocks.reshape([2] * len(bits) + list(blocks.shape[1:]))
-    for step, (name, bit) in enumerate(bits):
-        dim = len(bits) - 1 - step
-        flag = my_bit(name, bit)
-        keep, give = halves(value, flag, dim)
-        other = swap(give, name, bit)
-        value = by_bit(keep, other, flag, dim, jnp.concatenate)
-    return value.reshape(blocks.shape)
-
-
-def with_halo(cells, axis, dim, width):
-    count = lax.axis_size(axis)
-    ends = count - 1
-    head = lax.slice_in_dim(cells, 0, width, axis=dim)
-    tail = lax.slice_in_dim(cells, cells.shape[dim] - width, cells.shape[dim], axis=dim)
-    above = lax.ppermute(tail, axis, [(i, i + 1) for i in range(ends)])
-    below = lax.ppermute(head, axis, [(i + 1, i) for i in range(ends)])
-    return above, below
-
-
-def layer_norm(values):
-    centre = values - jnp.mean(values, axis=-1, keepdims=True)
-    spread = jnp.mean(centre * centre, axis=-1, keepdims=True)
-    rate = lax.rsqrt(spread + 1e-06)
-    return centre * rate, rate
-
-
-def layer_norm_back(grad, normed, rate):
-    mean_grad = jnp.mean(grad, axis=-1, keepdims=True)
-    mean_both = jnp.mean(grad * normed, axis=-1, keepdims=True)
-    return rate * (grad - mean_grad - normed * mean_both)
-
-
-def split_cols(values):
-    shape = values.shape
-    shaped = values.reshape(shape[:-2] + (shape[-2] // 2, 2, shape[-1]))
-    return jnp.swapaxes(shaped, -3, -2)
-
-
-def join_cols(values):
-    shape = values.shape
-    return jnp.swapaxes(values, -3, -2).reshape(shape[:-3] + (2 * shape[-2], shape[-1]))
-
-
-def side_cells(cells, big):
-    half = cells.shape[3]
-    even, odd = cells[:, :, 0], cells[:, :, 1]
-    spot = jnp.arange(half)[None, None, :, None]
-    same = big[:, None, None, None]
-    pad = ((0, 0), (0, 0), (1, 1), (0, 0))
-    odd_down = jnp.pad(odd, pad)[:, :, :half] * jnp.where(spot == half // 2, same, 1.0)
-    even_up = jnp.pad(even, pad)[:, :, 2:] * jnp.where(spot == half // 2 - 1, same, 1.0)
-    left = jnp.stack([odd_down, even], axis=2)
-    right = jnp.stack([odd, even_up], axis=2)
-    return left, right
-
-
-def conv(cells, kernel, big):
-    cells = cells.astype(F32)
-    rows = cells.shape[1] - 2
-    left, right = side_cells(cells, big)
-    total = 0.0
-    for down in range(3):
-        for across, part in enumerate((left, cells, right)):
-            total = total + part[:, down : down + rows] * kernel[3 * down + across]
-    return total
-
-
-def tap_grads(cells, grads, big):
-    cells = cells.astype(F32)
-    rows = cells.shape[1] - 2
-    left, right = side_cells(cells, big)
-    sums = []
-    for down in range(3):
-        for part in (left, cells, right):
-            sums.append(jnp.sum(part[:, down : down + rows] * grads, axis=(0, 1, 2, 3)))
-    return jnp.stack(sums)
-
-
-def item_sums(values):
-    half = values.shape[3] // 2
-    shaped = values.reshape(values.shape[:3] + (2, half, values.shape[-1]))
-    return shaped.sum(axis=(1, 2, 4))
-
-
-def spread_items(piece, grid):
-    return jnp.repeat(piece, grid // 4, axis=1)[:, None, None]
 
 
 def contract_rows(left_side, right_side):
@@ -191,12 +100,17 @@
     return even_sum, odd_sum
 
 
-def ffn_body(canvases, rows, half, lanes, flag_ref, second_ref, grad_ref, up_ref, up_bias_ref, kernel_ref, shift_ref,
-             down_ref, branch_ref, grad_second_ref, grad_up_ref, grad_down_ref, sums_ref,
-             cells, cells_side, grads, grads_side, active, grad_cells, second_t):
+def ffn_body(canvases, rows, half, lanes, flag_ref, second_ref, grad_ref, up_block, up_bias_ref, kernel_ref, shift_ref,
+             down_block, branch_ref, grad_second_ref, grad_up_block, grad_down_block, sums_ref,
+             cells, cells_side, grads, grads_side, active, grad_cells, second_t, up_ref, down_ref, grad_down_ref):
     step = pl.program_id(0)
     width = second_ref.shape[1]
     block = up_ref.shape[1]
+    shard, ff_shard = up_block.shape[1], down_block.shape[1]
+    for k in range(up_block.shape[0]):
+        up_ref[k * shard : (k + 1) * shard, :] = up_block[k]
+    for k in range(down_block.shape[0]):
+        down_ref[k * ff_shard : (k + 1) * ff_shard, :] = down_block[k]
     grid = 2 * half
     group = half // 8
     tile = 256
@@ -348,53 +262,70 @@
         def _(n):
             cols = pl.ds(pl.multiple_of(n * tile, tile), tile)
             part = contract_rows(active[act_rows, :, cols].reshape(own, tile), own_grad)
-            if canvases == 1:
-                grad_down_ref[cols, :] = part.astype(grad_down_ref.dtype)
-            elif c == 0:
-                grad_down_ref[cols, :] = part.astype(grad_down_ref.dtype)
+            if c == 0:
+                grad_down_ref[cols, :] = part
             else:
-                grad_down_ref[cols, :] += part.astype(grad_down_ref.dtype)
+                grad_down_ref[cols, :] += part
 
     @pl.loop(0, block // tile)
     def _(n):
         cols = pl.ds(pl.multiple_of(n * tile, tile), tile)
-        grad_up_ref[:, cols] = matmul(second_t[...], grad_cells[:, :, cols].reshape(-1, tile)).astype(grad_up_ref.dtype)
-
-
-def feed_forward(flags, second, grad_two, up, up_bias, kernel, shift, down, canvases, rows, half):
-    width, hidden = up.shape
-    block, lanes = 768, 128
+        part = matmul(second_t[...], grad_cells[:, :, cols].reshape(-1, tile))
+        grad_up_block[:, :, cols] = part.reshape(-1, shard, tile).astype(BF16)
+
+    for k in range(down_block.shape[0]):
+        grad_down_block[k] = grad_down_ref[k * ff_shard : (k + 1) * ff_shard, :].astype(BF16)
+
+
+def feed_forward(flags, second, grad_two, pair, up_bias, kernel, shift, canvases, rows, half):
+    count, both, width = pair.shape
+    ff_shard = both // 2
+    shard, hidden = width // count, ff_shard * count
+    block, lanes = width, 128
+    per_block = block // ff_shard
     grid = 2 * half
     ext, mid, own = [canvases * n * grid for n in (rows + 4, rows + 2, rows)]
     kernel = jnp.pad(kernel, ((0, 7), (0, 0)))
-    body = functools.partial(ffn_body, canvases, rows, half, lanes)
     fixed = lambda shape: pl.BlockSpec(shape, lambda i: (0, 0), pipeline_mode=pl.Buffered(1))
     cols = lambda n: pl.BlockSpec((n, block), lambda i: (0, i))
-    return pl.pallas_call(
-        body,
+    if shard % 8 == 0:
+        up, down = pair, pair
+        up_spec = pl.BlockSpec((count, shard, block), lambda i: (0, i, 0))
+        down_spec = pl.BlockSpec((per_block, ff_shard, width), lambda i: (i, 1, 0))
+        grad_spec = up_spec
+        grad_shape = (count, ff_shard, width)
+    else:
+        up = pair[:, :ff_shard].reshape(count, ff_shard // shard, shard, width).swapaxes(0, 1)
+        up, down = up.reshape(-1, width, width), pair[:, ff_shard:]
+        up_spec = pl.BlockSpec((1, width, block), lambda i: (i, 0, 0))
+        down_spec = pl.BlockSpec((per_block, ff_shard, width), lambda i: (i, 0, 0))
+        grad_spec = up_spec
+        grad_shape = (hidden // block, width, width)
+    outs = pl.pallas_call(
+        functools.partial(ffn_body, canvases, rows, half, lanes),
         grid=(hidden // block,),
         in_specs=[
             pl.BlockSpec(memory_space=pltpu.SMEM),
             fixed((ext, width)),
             fixed((mid, width)),
-            cols(width),
+            up_spec,
             cols(1),
             cols(16),
             cols(1),
-            pl.BlockSpec((block, width), lambda i: (i, 0)),
+            down_spec,
         ],
         out_specs=[
             pl.BlockSpec((own, width), lambda i: (0, 0)),
             pl.BlockSpec((own, width), lambda i: (0, 0)),
-            cols(width),
-            pl.BlockSpec((block, width), lambda i: (i, 0)),
+            grad_spec,
+            pl.BlockSpec((per_block, ff_shard, width), lambda i: (i, 0, 0)),
             cols(16),
         ],
         out_shape=[
             jax.ShapeDtypeStruct((own, width), F32),
             jax.ShapeDtypeStruct((own, width), F32),
-            jax.ShapeDtypeStruct((width, hidden), BF16),
-            jax.ShapeDtypeStruct((hidden, width), BF16 if canvases == 1 else F32),
+            jax.ShapeDtypeStruct(grad_shape, BF16),
+            jax.ShapeDtypeStruct((count, ff_shard, width), BF16),
             jax.ShapeDtypeStruct((16, hidden), F32),
         ],
         scratch_shapes=[
@@ -405,11 +336,18 @@
             pltpu.VMEM((mid // 8, 8, block), BF16),
             pltpu.VMEM((own // 8, 8, block), BF16),
             pltpu.VMEM((width, own), BF16),
+            pltpu.VMEM((width, block), BF16),
+            pltpu.VMEM((block, width), BF16),
+            pltpu.VMEM((block, width), F32),
         ],
         compiler_params=pltpu.CompilerParams(vmem_limit_bytes=60 << 20, dimension_semantics=("arbitrary",)),
-        cost_estimate=pl.CostEstimate(flops=36 * own * width * hidden // 3, bytes_accessed=40 << 20, transcendentals=own * hidden),
+        cost_estimate=pl.CostEstimate(flops=12 * own * width * hidden, bytes_accessed=40 << 20, transcendentals=own * hidden),
         name="feed_forward",
     )(flags, second, grad_two, up, up_bias[None], kernel, shift[None], down)
+    branch, grad_second, grad_up, grad_down, sums = outs
+    if shard % 8:
+        grad_up = grad_up.reshape(-1, count, shard, width).swapaxes(0, 1).reshape(count, ff_shard, width)
+    return branch, grad_second, jnp.concatenate([grad_up, grad_down], axis=1), sums
 
 
 def one_head(pair, head):
@@ -417,7 +355,7 @@
     return jnp.where((lane < HDIM) == (head == 0), pair, jnp.zeros_like(pair))
 
 
-def attend_forward_body(tile, query_ref, key_ref, value_ref, query_item_ref, key_item_ref, out_ref, lse_ref, key_wide):
+def attend_forward_body(tile, count, half, place_ref, query_ref, key_ref, value_ref, query_item_ref, key_item_ref, spread_ref, lse_ref, key_wide, out_ref):
     tokens = query_ref.shape[0]
     pair = query_ref.shape[1]
     scale = HDIM ** -0.5
@@ -441,37 +379,44 @@
         lane = lax.broadcasted_iota(jnp.int32, outs[0].shape, 1)
         out_ref[spots, :] = jnp.where(lane < HDIM, outs[0], outs[1]).astype(BF16)
 
-
-def attend_forward(projected, query_item, key_item):
+    spread_lines(spread_ref, out_ref[...], count, half, place_ref[0], slice(None))
+
+
+def attend_forward(place, projected, query_item, key_item, count, half):
     tokens = projected.shape[0]
     width = projected.shape[1] // 3
     pair = 2 * HDIM
     pairs = width // pair
+    lines = tokens // count + 2 * half
     block = lambda k: pl.BlockSpec((tokens, pair), lambda i: (0, i + k * pairs))
     fixed = pl.BlockSpec((tokens, 128), lambda i: (0, 0))
     return pl.pallas_call(
-        functools.partial(attend_forward_body, 256),
+        functools.partial(attend_forward_body, 256, count, half),
         grid=(pairs,),
-        in_specs=[block(0), block(1), block(2), fixed, fixed],
-        out_specs=[block(0), pl.BlockSpec((1, 8, tokens), lambda i: (i, 0, 0))],
-        out_shape=[jax.ShapeDtypeStruct((tokens, width), BF16), jax.ShapeDtypeStruct((pairs, 8, tokens), F32)],
-        scratch_shapes=[pltpu.VMEM((tokens, 2 * pair), BF16)],
+        in_specs=[pl.BlockSpec(memory_space=pltpu.SMEM), block(0), block(1), block(2), fixed, fixed],
+        out_specs=[pl.BlockSpec((count, lines, pair), lambda i: (0, 0, i)), pl.BlockSpec((1, 8, tokens), lambda i: (i, 0, 0))],
+        out_shape=[jax.ShapeDtypeStruct((count, lines, width), BF16), jax.ShapeDtypeStruct((pairs, 8, tokens), F32)],
+        scratch_shapes=[pltpu.VMEM((tokens, 2 * pair), BF16), pltpu.VMEM((tokens, pair), BF16)],
         compiler_params=pltpu.CompilerParams(vmem_limit_bytes=40 << 20, dimension_semantics=("arbitrary",)),
         cost_estimate=pl.CostEstimate(flops=8 * tokens * tokens * width, bytes_accessed=8 << 20, transcendentals=tokens * tokens * width // HDIM),
         name="attend_forward",
-    )(projected, projected, projected, query_item, key_item)
-
-
-def attend_backward_body(tile, query_ref, key_ref, value_ref, query_item_ref, key_item_ref, grad_ref, out_ref, lse_ref,
-                         result_ref, key_wide, key_t, query_t):
+    )(place, projected, projected, projected, query_item, key_item)
+
+
+def attend_backward_body(tile, count, half, query_ref, key_ref, value_ref, query_item_ref, key_item_ref, spread_ref, lse_ref, *refs):
+    blocks = refs[:count]
+    final_ref, sums_ref, result_ref, key_wide, key_t, query_t, grad_ref, out_ref = refs[count:]
     tokens = query_ref.shape[0]
     pair = query_ref.shape[1]
+    size = tokens // count
     scale = HDIM ** -0.5
     key_wide[:, :pair] = key_ref[...]
     key_wide[:, pair:] = key_item_ref[...]
     key_t[...] = key_ref[...].T
-
-    grad_key = [jnp.zeros((), F32)] * 2
+    for k in range(count):
+        grad_ref[k * size : (k + 1) * size, :] = blocks[k][...]
+        out_ref[k * size : (k + 1) * size, :] = spread_ref[k, half : half + size, :]
+
     result_ref[1] = jnp.zeros_like(result_ref[1])
     result_ref[2] = jnp.zeros_like(result_ref[2])
 
@@ -500,62 +445,553 @@
         query_t[:, spots] = jnp.concatenate(queries_new, axis=0)
 
     result_ref[0] = query_t[...].T * scale
-
-
-def attend_backward_wrap(tile, query_ref, key_ref, value_ref, query_item_ref, key_item_ref, grad_ref, out_ref, lse_ref,
-                         final_ref, sums_ref, result, key_wide, key_t, query_t):
-    attend_backward_body(tile, query_ref, key_ref, value_ref, query_item_ref, key_item_ref, grad_ref, out_ref, lse_ref,
-                         result, key_wide, key_t, query_t)
-    final_ref[...] = result[...].astype(BF16)
+    final_ref[...] = result_ref[...].astype(BF16)
     for k in range(3):
-        sums_ref[k] = jnp.sum(result[k].reshape(-1, 8, result.shape[2]), axis=0)
-
-
-def attend_backward(projected, query_item, key_item, grad, out, lse):
+        sums_ref[k] = jnp.sum(fold(result_ref[k]), axis=0)
+
+
+def attend_backward(projected, query_item, key_item, blocks, spread, lse, half):
     tokens = projected.shape[0]
     width = projected.shape[1] // 3
     pair = 2 * HDIM
     pairs = width // pair
+    count = len(blocks)
+    lines = tokens // count + 2 * half
     block = lambda k: pl.BlockSpec((tokens, pair), lambda i: (0, i + k * pairs))
     fixed = pl.BlockSpec((tokens, 128), lambda i: (0, 0))
     return pl.pallas_call(
-        functools.partial(attend_backward_wrap, 256),
+        functools.partial(attend_backward_body, 256, count, half),
         grid=(pairs,),
-        in_specs=[block(0), block(1), block(2), fixed, fixed, block(0), block(0), pl.BlockSpec((1, 8, tokens), lambda i: (i, 0, 0))],
+        in_specs=[block(0), block(1), block(2), fixed, fixed]
+        + [pl.BlockSpec((count, lines, pair), lambda i: (0, 0, i)), pl.BlockSpec((1, 8, tokens), lambda i: (i, 0, 0))]
+        + [pl.BlockSpec((tokens // count, pair), lambda i: (0, i))] * count,
         out_specs=[pl.BlockSpec((3, tokens, pair), lambda i: (0, 0, i)), pl.BlockSpec((3, 8, pair), lambda i: (0, 0, i))],
         out_shape=[jax.ShapeDtypeStruct((3, tokens, width), BF16), jax.ShapeDtypeStruct((3, 8, width), F32)],
-        scratch_shapes=[pltpu.VMEM((3, tokens, pair), F32), pltpu.VMEM((tokens, 2 * pair), BF16), pltpu.VMEM((pair, tokens), BF16), pltpu.VMEM((pair, tokens), F32)],
+        scratch_shapes=[pltpu.VMEM((3, tokens, pair), F32), pltpu.VMEM((tokens, 2 * pair), BF16), pltpu.VMEM((pair, tokens), BF16), pltpu.VMEM((pair, tokens), F32)] + [pltpu.VMEM((tokens, pair), BF16)] * 2,
         compiler_params=pltpu.CompilerParams(vmem_limit_bytes=48 << 20, dimension_semantics=("arbitrary",)),
         cost_estimate=pl.CostEstimate(flops=20 * tokens * tokens * width, bytes_accessed=12 << 20, transcendentals=tokens * tokens * width // HDIM),
         name="attend_backward",
-    )(projected, projected, projected, query_item, key_item, grad, out, lse)
-
-
-def to_units(cells):
-    canvases, rows, two, half, width = cells.shape
-    shaped = cells.reshape(canvases, rows // 2, 2, two, half, width)
-    return shaped.transpose(0, 2, 3, 1, 4, 5).reshape(canvases * 4, rows // 2, half, width)
-
-
-def from_units(blocks, canvases):
-    units, count, half, width = blocks.shape
-    shaped = blocks.reshape(canvases, 2, 2, count, half, width)
-    return shaped.transpose(0, 3, 1, 2, 4, 5).reshape(canvases, 2 * count, 2, half, width)
-
-
-def unit_to_rows(values, half, rows, canvases):
-    width = values.shape[-1]
-    own = rows // 2
-    padded = jnp.pad(values.reshape(half, half, width), ((1, 1), (0, 0), (0, 0)))
-    blocks = jnp.stack(
-        [padded[own * k : own * k + own + 2] for k in range(half // own)]
-    )
-    return from_units(exchange(blocks, "fsdp"), canvases)
-
-
-def rows_to_unit(cells):
-    blocks = exchange(to_units(cells), "fsdp")
-    return blocks.reshape(-1, cells.shape[-1])
+    )(projected, projected, projected, query_item, key_item, spread, lse, *blocks)
+
+
+def column_order(size, grid, back):
+    here = lax.broadcasted_iota(jnp.int32, (size, size), 1 if back else 0)
+    there = lax.broadcasted_iota(jnp.int32, (size, size), 0 if back else 1)
+    spot = here % grid
+    source = here - spot + 2 * (spot % (grid // 2)) + spot // (grid // 2)
+    return (source == there).astype(BF16)
+
+
+def rows_at(row, grid):
+    return pl.ds(pl.multiple_of(row * grid, grid), grid)
+
+
+def normalise(values):
+    centre = values - jnp.mean(values, axis=-1, keepdims=True)
+    rate = lax.rsqrt(jnp.mean(centre * centre, axis=-1, keepdims=True) + 1e-06)
+    return centre * rate, rate
+
+
+def normalise_back(grad, normed, rate):
+    mean_grad = jnp.mean(grad, axis=-1, keepdims=True)
+    mean_both = jnp.mean(grad * normed, axis=-1, keepdims=True)
+    return rate * (grad - mean_grad - normed * mean_both)
+
+
+def fold(values):
+    return values.reshape(-1, 8, values.shape[-1])
+
+
+def half_sums(values):
+    parts = values.reshape(2, 2, -1, 8, values.shape[-1])
+    return jnp.sum(parts, axis=(0, 2))
+
+
+def edge_masks(flag_ref, c, half, lanes):
+    shape = (half // 8, 8, lanes)
+    spot = lax.broadcasted_iota(jnp.int32, shape, 0) * 8 + lax.broadcasted_iota(jnp.int32, shape, 1)
+    big = flag_ref[c, 0]
+    down_mask = jnp.where(spot == 0, 0.0, jnp.where(spot == half // 2, big, 1.0))
+    up_mask = jnp.where(spot == half - 1, 0.0, jnp.where(spot == half // 2 - 1, big, 1.0))
+    return down_mask, up_mask
+
+
+def fill_sides(cells, side, down_mask, up_mask, base, chunks, lanes):
+    group = down_mask.shape[0]
+    for k in range(chunks):
+        cols = slice(k * lanes, (k + 1) * lanes)
+        even = cells[pl.ds(base, group), :, cols]
+        odd = cells[pl.ds(base + group, group), :, cols]
+        side[pl.ds(base, group), :, cols] = shifted(odd, down_mask, 1)
+        side[pl.ds(base + group, group), :, cols] = shifted(even, up_mask, -1)
+
+
+def load_row(cells, side, base, group, cols):
+    return (
+        cells[pl.ds(base, group), :, cols],
+        cells[pl.ds(base + group, group), :, cols],
+        side[pl.ds(base, group), :, cols],
+        side[pl.ds(base + group, group), :, cols],
+    )
+
+
+def spread_tap(ref, row, cols, lanes):
+    return jnp.broadcast_to(ref[pl.ds(row, 1), cols][None], (1, 8, lanes))
+
+
+def whole_call(body, inputs, outputs, scratch, name, flops, limit=60, scalars=1):
+    moved = sum(math.prod(v.shape) * v.dtype.itemsize for v in list(inputs) + list(outputs))
+    vmem = pl.BlockSpec(memory_space=pltpu.VMEM)
+    smem = pl.BlockSpec(memory_space=pltpu.SMEM)
+    return pl.pallas_call(
+        body,
+        in_specs=[smem] * scalars + [vmem] * (len(inputs) - scalars),
+        out_specs=[vmem] * len(outputs),
+        out_shape=list(outputs),
+        scratch_shapes=scratch,
+        compiler_params=pltpu.CompilerParams(vmem_limit_bytes=limit << 20),
+        cost_estimate=pl.CostEstimate(flops=flops, bytes_accessed=moved, transcendentals=0),
+        name=name,
+    )(*inputs)
+
+
+def sorted_rows(source, dest, count, grid, back):
+    size = 2 * grid
+    order = column_order(size, grid, back)
+
+    @pl.loop(0, count // 2)
+    def _(n):
+        spots = pl.ds(pl.multiple_of(n * size, size), size)
+        dest[spots, :] = matmul(order, source[spots, :]).astype(BF16)
+
+
+def prepare_body(canvases, rows, half, flag_ref, place_ref, inputs_ref, grad_ref, kernel_ref, sorted_ref, grad_sorted_ref, out_ref, cells, side):
+    grid, lanes = 2 * half, 128
+    width = inputs_ref.shape[1]
+    group, per_row, chunks = half // 8, grid // 8, width // lanes
+    ext, mid = rows + 4, rows + 2
+    me = place_ref[0]
+    sorted_rows(inputs_ref, sorted_ref, canvases * ext, grid, False)
+    for c in range(canvases):
+        down_mask, up_mask = edge_masks(flag_ref, c, half, lanes)
+
+        @pl.loop(0, mid)
+        def _(r):
+            normed, _ = normalise(sorted_ref[rows_at(c * ext + r + 1, grid), :].astype(F32))
+            keep = jnp.where(r == 0, flag_ref[c, 1], jnp.where(r == mid - 1, flag_ref[c, 2], 1.0))
+            base = (c * mid + r) * per_row
+            cells[pl.ds(base, per_row)] = fold(normed * keep)
+            fill_sides(cells, side, down_mask, up_mask, base, chunks, lanes)
+
+        @pl.loop(0, chunks)
+        def _(k):
+            cols = pl.ds(pl.multiple_of(k * lanes, lanes), lanes)
+            taps = [spread_tap(kernel_ref, t, cols, lanes) for t in range(9)]
+
+            @pl.loop(0, rows // 2)
+            def _(i):
+                spots = pl.ds(pl.multiple_of(i * half, half), half)
+                for a in range(2):
+                    load = lambda down: load_row(cells, side, (c * mid + 2 * i + a + down) * per_row, group, cols)
+                    sums = conv_row(load, taps)
+                    for b in range(2):
+                        unit = jnp.bitwise_xor(c * 4 + a * 2 + b, me)
+                        out_ref[unit, spots, cols] = sums[b].reshape(half, lanes).astype(BF16)
+
+    sorted_rows(grad_ref, grad_sorted_ref, canvases * mid, grid, False)
+
+
+def prepare(flags, place, inputs, grad_out, kernel, canvases, rows, half):
+    width = inputs.shape[1]
+    mid = canvases * (rows + 2) * half * 2
+    return whole_call(
+        functools.partial(prepare_body, canvases, rows, half),
+        (flags, place, inputs, grad_out, kernel),
+        (
+            jax.ShapeDtypeStruct(inputs.shape, BF16),
+            jax.ShapeDtypeStruct(grad_out.shape, BF16),
+            jax.ShapeDtypeStruct((canvases * 4, rows // 2 * half, width), BF16),
+        ),
+        [pltpu.VMEM((mid // 8, 8, width), F32)] * 2,
+        "prepare",
+        30 * inputs.shape[0] * width,
+        scalars=2,
+    )
+
+
+def project_body(count, half, place_ref, *refs):
+    blocks, (scale_ref, add_ref, weight_ref, bias_ref, mixed_ref, out_ref) = refs[:count], refs[count:]
+    me, odd_row = place_ref[0], place_ref[1]
+    size = blocks[0].shape[0]
+    lines = size // half
+
+    @pl.when(pl.program_id(0) == 0)
+    def _():
+        for k in range(count):
+            owner = jnp.bitwise_xor(k, me)
+            side = owner // (count // 2)
+
+            @pl.loop(0, lines)
+            def _(i):
+                at_edge = jnp.where(odd_row == 0, jnp.where(i == 0, place_ref[2 + owner], 0), jnp.where(i == lines - 1, place_ref[2 + count + owner], 0))
+                spots = pl.ds(pl.multiple_of(i * half, half), half)
+                value = blocks[k][spots, :].astype(F32) * scale_ref[side] + add_ref[at_edge * 2 + side]
+                mixed_ref[pl.ds(pl.multiple_of(k * size + i * half, half), half), :] = value.astype(BF16)
+
+    out_ref[...] = (matmul(mixed_ref[...], weight_ref[...]) + bias_ref[...]).astype(BF16)
+
+
+def project(place, blocks, scale, add, weight, bias, half):
+    count = len(blocks)
+    size, width = blocks[0].shape
+    tokens, tile = count * size, 256
+    fixed = lambda value: pl.BlockSpec(value.shape, lambda i: (0,) * value.ndim, pipeline_mode=pl.Buffered(1))
+    cols = lambda n: pl.BlockSpec((n, tile), lambda i: (0, i))
+    return pl.pallas_call(
+        functools.partial(project_body, count, half),
+        grid=(3 * width // tile,),
+        in_specs=[pl.BlockSpec(memory_space=pltpu.SMEM)] + [fixed(block) for block in blocks] + [fixed(scale), fixed(add), cols(width), cols(1)],
+        out_specs=[pl.BlockSpec((tokens, width), lambda i: (0, 0)), cols(tokens)],
+        out_shape=[jax.ShapeDtypeStruct((tokens, width), BF16), jax.ShapeDtypeStruct((tokens, 3 * width), BF16)],
+        compiler_params=pltpu.CompilerParams(vmem_limit_bytes=40 << 20, dimension_semantics=("arbitrary",)),
+        cost_estimate=pl.CostEstimate(flops=6 * tokens * width * width, bytes_accessed=12 << 20, transcendentals=0),
+        name="project",
+    )(place, *blocks, scale, add, weight, bias)
+
+
+def middle_body(canvases, rows, half, count, flag_ref, place_ref, *refs):
+    blocks = refs[:count]
+    inputs_ref, weight_ref, bias_ref, mods_ref, second_ref, hidden_ref, branch_ref, attended_ref, wide, product = refs[count:]
+    grid = 2 * half
+    width = inputs_ref.shape[1]
+    ext = rows + 4
+    me = place_ref[0]
+    lines = rows // 2 + 2
+    tile = 256
+    for k in range(count):
+        unit = jnp.bitwise_xor(k, me)
+        canvas, a, b = unit // 4, (unit // 2) % 2, unit % 2
+
+        @pl.loop(0, lines)
+        def _(i):
+            start = (canvas * ext + 2 * i + a) * grid + b * half
+            wide[pl.ds(pl.multiple_of(start, half), half), :] = blocks[k][pl.ds(pl.multiple_of(i * half, half), half), :]
+
+    @pl.loop(0, width // tile)
+    def _(n):
+        cols = pl.ds(pl.multiple_of(n * tile, tile), tile)
+        product[:, cols] = matmul(wide[...], weight_ref[:, cols]) + bias_ref[:, cols]
+
+    for c in range(canvases):
+        own = slice((c * ext + 2) * grid, (c * ext + 2 + rows) * grid)
+        attended_ref[c * rows * grid : (c + 1) * rows * grid, :] = wide[own, :]
+
+        def line(r):
+            spots = rows_at(c * ext + r, grid)
+            branch = product[spots, :]
+            hidden = inputs_ref[spots, :].astype(F32) + mods_ref[c, 2] * branch
+            normed, _ = normalise(hidden)
+            second_ref[spots, :] = (normed * (1.0 + mods_ref[c, 4]) + mods_ref[c, 3]).astype(BF16)
+            return branch, hidden
+
+        for r in (0, 1, rows + 2, rows + 3):
+            line(r)
+
+        @pl.loop(0, rows)
+        def _(r):
+            branch, hidden = line(r + 2)
+            spots = rows_at(c * rows + r, grid)
+            branch_ref[spots, :] = branch
+            hidden_ref[spots, :] = hidden
+
+
+def middle(flags, place, blocks, inputs, weight, bias, mods, canvases, rows, half):
+    width = inputs.shape[1]
+    own = canvases * rows * 2 * half
+    return whole_call(
+        functools.partial(middle_body, canvases, rows, half, len(blocks)),
+        (flags, place, *blocks, inputs, weight, bias, mods),
+        (
+            jax.ShapeDtypeStruct(inputs.shape, BF16),
+            jax.ShapeDtypeStruct((own, width), F32),
+            jax.ShapeDtypeStruct((own, width), F32),
+            jax.ShapeDtypeStruct((own, width), BF16),
+        ),
+        [pltpu.VMEM(inputs.shape, BF16), pltpu.VMEM(inputs.shape, F32)],
+        "middle",
+        2 * inputs.shape[0] * width * width,
+        scalars=2,
+    )
+
+
+def turn_body(canvases, rows, half, place_ref, branch_two_ref, grad_second_ref, hidden_ref, branch_ref, grad_out_ref, weight_ref, bias_ref,
+              mods_ref, out_ref, grad_hidden_ref, grad_branch_ref, blocks_ref, half_ref, bias_sums_ref, result):
+    grid = 2 * half
+    width = hidden_ref.shape[1]
+    me = place_ref[0]
+    tile = 256
+    half_ref[...] = jnp.zeros_like(half_ref)
+    bias_sums_ref[...] = jnp.zeros_like(bias_sums_ref)
+    for c in range(canvases):
+
+        @pl.loop(0, rows)
+        def _(r):
+            spots = rows_at(c * rows + r, grid)
+            grad_out = grad_out_ref[rows_at(c * (rows + 2) + r + 1, grid), :].astype(F32)
+            branch_two = branch_two_ref[spots, :] + bias_ref[...]
+            hidden = hidden_ref[spots, :]
+            result[spots, :] = (hidden + mods_ref[c, 5] * branch_two).astype(BF16)
+            normed, rate = normalise(hidden)
+            grad = grad_second_ref[spots, :]
+            grad_hidden = grad_out + normalise_back(grad * (1.0 + mods_ref[c, 4]), normed, rate)
+            grad_hidden_ref[spots, :] = grad_hidden
+            grad_branch = (mods_ref[c, 2] * grad_hidden).astype(BF16)
+            grad_branch_ref[spots, :] = grad_branch
+            half_ref[c, 0] += half_sums(grad_hidden * branch_ref[spots, :])
+            half_ref[c, 1] += half_sums(grad)
+            half_ref[c, 2] += half_sums(grad * normed)
+            half_ref[c, 3] += half_sums(grad_out * branch_two)
+            bias_sums_ref[0] += jnp.sum(fold(grad_branch.astype(F32)), axis=0)
+            low = (mods_ref[c, 5] * grad_out).astype(BF16).astype(F32)
+            bias_sums_ref[1] += jnp.sum(fold(low), axis=0)
+
+    @pl.loop(0, width // tile)
+    def _(n):
+        cols = pl.ds(pl.multiple_of(n * tile, tile), tile)
+        product = contract_cols(grad_branch_ref[...], weight_ref[cols, :]).astype(BF16)
+        for c in range(canvases):
+            for r in range(rows):
+                for b in range(2):
+                    unit = jnp.bitwise_xor(c * 4 + r % 2 * 2 + b, me)
+                    start = (c * rows + r) * grid + b * half
+                    line = r // 2 * half
+                    blocks_ref[unit, line : line + half, cols] = product[start : start + half]
+
+    sorted_rows(result, out_ref, canvases * rows, grid, True)
+
+
+def turn(place, branch_two, grad_second, hidden, branch, grad_out, weight, bias, mods, canvases, rows, half):
+    own, width = hidden.shape
+    return whole_call(
+        functools.partial(turn_body, canvases, rows, half),
+        (place, branch_two, grad_second, hidden, branch, grad_out, weight, bias, mods),
+        (
+            jax.ShapeDtypeStruct((own, width), BF16),
+            jax.ShapeDtypeStruct((own, width), F32),
+            jax.ShapeDtypeStruct((own, width), BF16),
+            jax.ShapeDtypeStruct((canvases * 4, rows // 2 * half, width), BF16),
+            jax.ShapeDtypeStruct((canvases, 4, 2, 8, width), F32),
+            jax.ShapeDtypeStruct((2, 8, width), F32),
+        ),
+        [pltpu.VMEM((own, width), BF16)],
+        "turn",
+        2 * own * width * width,
+    )
+
+
+def spread_lines(out_ref, value, count, half, me, cols):
+    size = value.shape[0] // count
+    for k in range(count):
+        owner = jnp.bitwise_xor(k, me)
+        block = value[k * size : (k + 1) * size]
+        out_ref[k, half : half + size, cols] = block
+
+        @pl.when(owner + 1 < count)
+        def _():
+            out_ref[jnp.bitwise_xor(owner + 1, me), :half, cols] = block[size - half :]
+
+        @pl.when(owner > 0)
+        def _():
+            out_ref[jnp.bitwise_xor(owner - 1, me), half + size :, cols] = block[:half]
+
+        @pl.when(owner == 0)
+        def _():
+            out_ref[k, :half, cols] = jnp.zeros_like(block[:half])
+
+        @pl.when(owner + 1 == count)
+        def _():
+            out_ref[k, half + size :, cols] = jnp.zeros_like(block[:half])
+
+
+def project_back_body(count, half, place_ref, parts_ref, weight_ref, out_ref):
+    width = parts_ref.shape[2]
+    total = contract_cols(parts_ref[0], weight_ref[:, :width])
+    for k in (1, 2):
+        total += contract_cols(parts_ref[k], weight_ref[:, k * width : (k + 1) * width])
+    spread_lines(out_ref, total.astype(BF16), count, half, place_ref[0], slice(None))
+
+
+def project_back(place, parts, weight, count, half):
+    _, tokens, width = parts.shape
+    tile = 256
+    lines = tokens // count + 2 * half
+    return pl.pallas_call(
+        functools.partial(project_back_body, count, half),
+        grid=(width // tile,),
+        in_specs=[
+            pl.BlockSpec(memory_space=pltpu.SMEM),
+            pl.BlockSpec((3, tokens, width), lambda i: (0, 0, 0), pipeline_mode=pl.Buffered(1)),
+            pl.BlockSpec((tile, 3 * width), lambda i: (i, 0)),
+        ],
+        out_specs=pl.BlockSpec((count, lines, tile), lambda i: (0, 0, i)),
+        out_shape=jax.ShapeDtypeStruct((count, lines, width), BF16),
+        compiler_params=pltpu.CompilerParams(vmem_limit_bytes=40 << 20, dimension_semantics=("arbitrary",)),
+        cost_estimate=pl.CostEstimate(flops=6 * tokens * width * width, bytes_accessed=12 << 20, transcendentals=0),
+        name="project_back",
+    )(place, parts, weight)
+
+
+def finish_body(canvases, rows, half, count, flag_ref, place_ref, *refs):
+    blocks = refs[:count]
+    inputs_ref, grad_hidden_ref, kernel_ref, mods_ref, out_ref, half_ref, sums_ref, cells, side, grads, grads_side, back, result = refs[count:]
+    grid, lanes = 2 * half, 128
+    width = inputs_ref.shape[1]
+    group, per_row, chunks = half // 8, grid // 8, width // lanes
+    ext, mid = rows + 4, rows + 2
+    me = place_ref[0]
+    for k in range(count):
+        unit = jnp.bitwise_xor(k, me)
+        canvas, a, b = unit // 4, (unit // 2) % 2, unit % 2
+
+        @pl.loop(0, rows // 2 + 2)
+        def _(i):
+            start = (canvas * ext + 2 * i + a) * per_row + b * group
+            grads[pl.ds(start, group)] = fold(blocks[k][pl.ds(pl.multiple_of(i * half, half), half), :].astype(F32))
+
+    half_ref[...] = jnp.zeros_like(half_ref)
+    for c in range(canvases):
+        down_mask, up_mask = edge_masks(flag_ref, c, half, lanes)
+        for row, flag in ((1, 1), (mid, 2)):
+
+            @pl.when(flag_ref[c, flag] == 0)
+            def _():
+                grads[pl.ds((c * ext + row) * per_row, per_row)] = jnp.zeros((per_row, 8, width), F32)
+
+        @pl.loop(0, mid)
+        def _(r):
+            normed, _ = normalise(inputs_ref[rows_at(c * ext + r + 1, grid), :].astype(F32))
+            first = (normed * (1.0 + mods_ref[c, 1]) + mods_ref[c, 0]).astype(BF16).astype(F32)
+            keep = jnp.where(r == 0, flag_ref[c, 1], jnp.where(r == mid - 1, flag_ref[c, 2], 1.0))
+            base = (c * mid + r) * per_row
+            cells[pl.ds(base, per_row)] = fold(first * keep)
+            fill_sides(cells, side, down_mask, up_mask, base, chunks, lanes)
+            fill_sides(grads, grads_side, down_mask, up_mask, (c * ext + r + 1) * per_row, chunks, lanes)
+
+        @pl.loop(0, chunks)
+        def _(k):
+            cols = pl.ds(pl.multiple_of(k * lanes, lanes), lanes)
+            taps = [spread_tap(kernel_ref, 8 - t, cols, lanes) for t in range(9)]
+
+            def row_step(r, sums):
+                load_grads = lambda down: load_row(grads, grads_side, (c * ext + r + 1 + down) * per_row, group, cols)
+                back_even, back_odd = conv_row(load_grads, taps)
+                here = (c * rows + r) * per_row
+                back[pl.ds(here, group), :, cols] = back_even
+                back[pl.ds(here + group, group), :, cols] = back_odd
+                mine = (c * ext + r + 2) * per_row
+                g_even = grads[pl.ds(mine, group), :, cols]
+                g_odd = grads[pl.ds(mine + group, group), :, cols]
+                new = []
+                for down in range(3):
+                    even, odd, odd_down, even_up = load_row(cells, side, (c * mid + r + down) * per_row, group, cols)
+                    for for_even, for_odd in ((odd_down, even), (even, odd), (odd, even_up)):
+                        new.append(jnp.sum(for_even * g_even + for_odd * g_odd, axis=0))
+                new.append(jnp.sum(g_even + g_odd, axis=0))
+                return tuple(s + v for s, v in zip(sums, new))
+
+            sums = lax.fori_loop(0, rows, row_step, (jnp.zeros((8, lanes), F32),) * 10)
+            for t in range(10):
+                total = jnp.sum(sums[t], axis=0, keepdims=True)
+                if c == 0:
+                    sums_ref[pl.ds(t, 1), cols] = total
+                else:
+                    sums_ref[pl.ds(t, 1), cols] += total
+
+        @pl.loop(0, rows)
+        def _(r):
+            normed, rate = normalise(inputs_ref[rows_at(c * ext + r + 2, grid), :].astype(F32))
+            grad = back[pl.ds((c * rows + r) * per_row, per_row)].reshape(grid, width)
+            half_ref[c, 0] += half_sums(grad)
+            half_ref[c, 1] += half_sums(grad * normed)
+            spots = rows_at(c * rows + r, grid)
+            total = grad_hidden_ref[spots, :] + normalise_back(grad * (1.0 + mods_ref[c, 1]), normed, rate)
+            result[spots, :] = total.astype(BF16)
+
+    sorted_rows(result, out_ref, canvases * rows, grid, True)
+
+
+def finish(flags, place, blocks, inputs, grad_hidden, kernel, mods, canvases, rows, half):
+    own, width = grad_hidden.shape
+    grid = 2 * half
+    sizes = [canvases * n * grid // 8 for n in (rows + 2, rows + 4, rows)]
+    return whole_call(
+        functools.partial(finish_body, canvases, rows, half, len(blocks)),
+        (flags, place, *blocks, inputs, grad_hidden, kernel, mods),
+        (
+            jax.ShapeDtypeStruct((own, width), BF16),
+            jax.ShapeDtypeStruct((canvases, 2, 2, 8, width), F32),
+            jax.ShapeDtypeStruct((16, width), F32),
+        ),
+        [pltpu.VMEM((sizes[0], 8, width), F32)] * 2
+        + [pltpu.VMEM((sizes[1], 8, width), F32)] * 2
+        + [pltpu.VMEM((sizes[2], 8, width), F32), pltpu.VMEM((own, width), BF16)],
+        "finish",
+        60 * own * width,
+        scalars=2,
+    )
+
+
+def trade(blocks):
+    size = lax.axis_size("fsdp")
+    parts = [blocks[k] for k in range(size)]
+    moved = {}
+    for k in list(range(size - 1, 0, -1)):
+        moved[k] = lax.ppermute(parts[k], "fsdp", [(i, i ^ k) for i in range(size)])
+    return [parts[0]] + [moved[k] for k in range(1, size)]
+
+
+def attention_grads_body(mixed_ref, part_ref, attended_ref, grad_ref, out_ref, left):
+    step = pl.program_id(0)
+    split = pl.num_programs(0) * 3 // 4
+
+    @pl.when(step == 0)
+    def _():
+        left[...] = mixed_ref[...].T
+
+    @pl.when(step == split)
+    def _():
+        left[...] = attended_ref[...].T
+
+    @pl.when(step < split)
+    def _():
+        out_ref[...] = matmul(left[...], part_ref[0]).astype(BF16)
+
+    @pl.when(step >= split)
+    def _():
+        out_ref[...] = matmul(left[...], grad_ref[...]).astype(BF16)
+
+
+def attention_grads(mixed, parts, attended, grad_branch):
+    tokens, width = mixed.shape
+    tile = 256
+    per = width // tile
+    whole = pl.BlockSpec((tokens, width), lambda i: (0, 0), pipeline_mode=pl.Buffered(1))
+    return pl.pallas_call(
+        attention_grads_body,
+        grid=(4 * per,),
+        in_specs=[
+            whole,
+            pl.BlockSpec((1, tokens, tile), lambda i: (jnp.minimum(i // per, 2), 0, i % per)),
+            whole,
+            pl.BlockSpec((tokens, tile), lambda i: (0, jnp.maximum(i - 3 * per, 0))),
+        ],
+        out_specs=pl.BlockSpec((width, tile), lambda i: (0, i)),
+        out_shape=jax.ShapeDtypeStruct((width, 4 * width), BF16),
+        scratch_shapes=[pltpu.VMEM((width, tokens), BF16)],
+        compiler_params=pltpu.CompilerParams(vmem_limit_bytes=32 << 20, dimension_semantics=("arbitrary",)),
+        cost_estimate=pl.CostEstimate(flops=8 * tokens * width * width, bytes_accessed=14 << 20, transcendentals=0),
+        name="attention_grads",
+    )(mixed, parts, attended, grad_branch)
 
 
 def per_device(
@@ -592,16 +1028,12 @@
     first_pair = lax.all_gather(
         jnp.concatenate([qkv_weight, out_weight], axis=1), EVERY, axis=0, tiled=True
     )
-    qkv_full, out_full = first_pair[:, : 3 * width], first_pair[:, 3 * width :]
+    out_full = first_pair[:, 3 * width :]
     up_rows = up_weight.reshape(shard, ff_shard * count // width, width).transpose(1, 0, 2)
     up_rows = up_rows.reshape(ff_shard, width)
     second_pair = lax.all_gather(
         jnp.concatenate([up_rows, down_weight], axis=0)[None], EVERY, axis=0, tiled=True
     )
-    up_full = second_pair[:, :ff_shard].reshape(count, ff_shard // shard, shard, width)
-    up_full = up_full.transpose(0, 2, 1, 3).reshape(width, hidden_units)
-    down_full = second_pair[:, ff_shard:].reshape(hidden_units, width)
-
     parts = [
         ada_bias,
         attn_kernel,
@@ -669,9 +1101,9 @@
     first_row = fsdp_index * rows
     row_half = (first_row >= half).astype(jnp.int32)
     local_mod = lax.dynamic_slice_in_dim(modulation, 2 * row_half, 2, axis=1)
-    shift_one, scale_one, gate_one, shift_two, scale_two, gate_two = [
-        spread_items(local_mod[:, :, k * width : (k + 1) * width], grid) for k in range(6)
-    ]
+    mods = local_mod.reshape(canvases, 2, 6, width).swapaxes(1, 2)
+    mods = jnp.repeat(mods[:, :, None], 2, axis=2)
+    mods = jnp.repeat(mods, half // 2, axis=3).reshape(canvases, 6, grid, width)
 
     big_item = size_tags[0] == 1
     big = big_item.astype(F32)
@@ -681,130 +1113,124 @@
     ends = n_fsdp - 1
     above = lax.ppermute(edge[0], "fsdp", [(i, i + 1) for i in range(ends)])
     below = lax.ppermute(edge[1], "fsdp", [(i + 1, i) for i in range(ends)])
-    inputs = split_cols(jnp.concatenate([above[:, :2], tokens[0], below[:, :2]], axis=1))
-    grad_out = split_cols(jnp.concatenate([above[:, 2:], cotangent[0], below[:, 2:]], axis=1))
-    inputs = inputs.astype(F32)
-    grad_out = grad_out.astype(F32)
+    inputs = jnp.concatenate([above[:, :2], tokens[0], below[:, :2]], axis=1).reshape(-1, width)
+    grad_out = jnp.concatenate([above[:, 2:], cotangent[0], below[:, 2:]], axis=1).reshape(-1, width)
     crosses_top = jnp.logical_and(first_row == half, jnp.logical_not(big_item))
     crosses_end = jnp.logical_and(first_row + rows == half, jnp.logical_not(big_item))
     top_ok = jnp.where(jnp.logical_or(fsdp_index == 0, crosses_top), 0.0, 1.0)
     end_ok = jnp.where(jnp.logical_or(fsdp_index == n_fsdp - 1, crosses_end), 0.0, 1.0)
 
-    def keep_item(cells, extra):
-        spot = jnp.arange(cells.shape[1])[None, :]
-        flag = jnp.where(spot < extra, top_ok[:, None], 1.0)
-        flag = jnp.where(spot >= cells.shape[1] - extra, end_ok[:, None], flag)
-        return jnp.where(flag[:, :, None, None, None] > 0, cells, jnp.zeros_like(cells))
-
-    normed_one, rate_one = layer_norm(inputs[:, 1:-1])
-    first = keep_item((normed_one * (1.0 + scale_one) + shift_one).astype(BF16), 1)
-    mixed = (conv(first, attn_kernel_full, big) + attn_shift_full).astype(BF16)
-    mixed_unit = rows_to_unit(mixed)
-    bias_row = jnp.concatenate([qv_bias_full[0], jnp.zeros((width,), F32), qv_bias_full[1]])
-    projected = (matmul(mixed_unit, qkv_full) + bias_row).astype(BF16)
-    unit_canvas = fsdp_index // 4
+    flags = jnp.stack([big, top_ok, end_ok], axis=1)
+
+    unit_canvas, row_parity, col_parity = fsdp_index // 4, (fsdp_index // 2) % 2, fsdp_index % 2
     unit_big = jnp.take(big_item, unit_canvas)
-    side = (jnp.arange(half) >= half // 2).astype(jnp.int32)
-    quad = (2 * side[:, None] + side[None, :]).reshape(-1)
+    owners = jnp.arange(n_fsdp)
+    middle_split = jnp.logical_not(unit_big)
+    top_edge = jnp.logical_or(owners == 0, jnp.logical_and(owners == n_fsdp // 2, middle_split))
+    end_edge = jnp.logical_or(
+        owners == n_fsdp - 1, jnp.logical_and(owners == n_fsdp // 2 - 1, middle_split)
+    )
+    place = jnp.concatenate([jnp.stack([fsdp_index, row_parity]), top_edge, end_edge]).astype(jnp.int32)
+    spots = jnp.arange(half)
+    right_side = (spots >= half // 2).astype(jnp.int32)
+    block_side = (jnp.bitwise_xor(owners, fsdp_index) >= n_fsdp // 2).astype(jnp.int32)
+    quad = jnp.broadcast_to(
+        (2 * block_side[:, None, None] + right_side), (n_fsdp, rows // 2, half)
+    ).reshape(-1)
     lane = jnp.arange(128)[None]
     hot = quad[:, None] == lane
     query_item = hot.astype(BF16)
     open_keys = jnp.logical_or(unit_big, jnp.logical_or(hot, lane >= 4))
     key_item = jnp.where(open_keys, 0.0, -1e30).astype(BF16)
-    attended_unit, lse = attend_forward(projected, query_item, key_item)
-    attended = unit_to_rows(attended_unit, half, rows, canvases)
-    flat = attended.reshape(-1, width)
-    branch_one = (matmul(flat, out_full) + out_bias_full).reshape(attended.shape)
-    hidden = inputs + gate_one * branch_one
-    normed_two, rate_two = layer_norm(hidden)
-    second = (normed_two * (1.0 + scale_two) + shift_two).astype(BF16)
-
-    own_shape = (canvases, rows, 2, half, width)
-    grad_two_ext = (gate_two * grad_out).astype(BF16)
-    grad_branch_two = grad_two_ext[:, 1:-1].reshape(-1, width)
-    flags = jnp.stack([big, top_ok, end_ok], axis=1)
-    branch_two, grad_second, grad_up, grad_down, ff_sums = feed_forward(
+
+    attn_taps = jnp.pad(attn_kernel_full, ((0, 7), (0, 0)))
+    inputs, grad_out, blocks = prepare(flags, place, inputs, grad_out, attn_taps, canvases, rows, half)
+    blocks = trade(blocks)
+    unit_mod = jnp.take(modulation, unit_canvas, axis=0).reshape(2, 2, 6, width)
+    unit_mod = jnp.repeat(unit_mod, half // 2, axis=1)
+    unit_shift, unit_scale = unit_mod[:, :, 0], 1.0 + unit_mod[:, :, 1]
+    tap_grid = attn_kernel_full.reshape(3, 3, width)
+    lost_row = jnp.take(tap_grid, 2 * row_parity, axis=0)
+    at_side = jnp.where(
+        col_parity == 0,
+        jnp.logical_or(spots == 0, jnp.logical_and(spots == half // 2, middle_split)),
+        jnp.logical_or(spots == half - 1, jnp.logical_and(spots == half // 2 - 1, middle_split)),
+    )
+
+    def taps_left(grid_part):
+        lost = jnp.take(grid_part, 2 * col_parity, axis=1).sum(axis=0)
+        return grid_part.sum(axis=(0, 1)) - jnp.where(at_side[:, None], lost, 0.0)
+
+    full_taps = taps_left(tap_grid)
+    edge_taps = full_taps - taps_left(lost_row[None])
+    taps_here = jnp.stack([full_taps, edge_taps])
+    unit_add = unit_shift[None] * taps_here[:, None] + attn_shift_full
+    bias_row = jnp.concatenate([qv_bias_full[0], jnp.zeros((width,), F32), qv_bias_full[1]])
+    mixed_unit, projected = project(
+        place, blocks, unit_scale, unit_add.reshape(4, half, width), first_pair, bias_row[None], half
+    )
+    attended_unit, lse = attend_forward(place, projected, query_item, key_item, n_fsdp, half)
+    second, hidden, branch_one, attended = middle(
+        flags, place, trade(attended_unit), inputs, out_full, out_bias_full[None], mods, canvases, rows, half
+    )
+
+    gate_two = mods[:, 5][:, None]
+    grad_two = (gate_two * grad_out.reshape(canvases, rows + 2, grid, width).astype(F32)).astype(BF16)
+    branch_two, grad_second, ff_grads, ff_sums = feed_forward(
         flags,
-        second.reshape(-1, width),
-        grad_two_ext.reshape(-1, width),
-        up_full,
+        second,
+        grad_two.reshape(-1, width),
+        second_pair,
         up_bias_full,
         ffn_kernel_full,
         ffn_shift_full,
-        down_full,
         canvases,
         rows,
         half,
     )
-    branch_two = (branch_two + down_bias_full).reshape(own_shape)
-    grad_second = grad_second.reshape(own_shape)
     grad_ffn_kernel, grad_ffn_shift, grad_up_bias = ff_sums[:9], ff_sums[9], ff_sums[10]
-    grad_up_rows = grad_up.astype(BF16).reshape(count, shard, ff_shard // shard, width)
-    grad_up_rows = grad_up_rows.transpose(0, 2, 1, 3).reshape(count, ff_shard, width)
-    ff_grads = jnp.concatenate(
-        [grad_up_rows, grad_down.astype(BF16).reshape(count, ff_shard, width)], axis=1
-    )
     ff_grads = lax.psum_scatter(ff_grads, EVERY, scatter_dimension=0, tiled=True)[0]
     grad_up = ff_grads[:ff_shard].reshape(ff_shard // shard, shard, width)
     grad_up = grad_up.transpose(1, 0, 2).reshape(shard, hidden_units).astype(F32)
     grad_down = ff_grads[ff_shard:].astype(F32)
 
-    grad_own = grad_out[:, 1:-1]
-    hidden_own = hidden[:, 2:-2]
-    normed_two_own = normed_two[:, 2:-2]
-    branch_one_own = branch_one[:, 2:-2]
-    result = join_cols((hidden_own + gate_two * branch_two).astype(BF16))[None]
-    grad_gate_two = item_sums(grad_own * branch_two)
-    grad_down_bias = jnp.sum(grad_branch_two.astype(F32), axis=0)
-    grad_scale_two = item_sums(grad_second * normed_two_own)
-    grad_shift_two = item_sums(grad_second)
-    grad_hidden = grad_own + layer_norm_back(
-        grad_second * (1.0 + scale_two), normed_two_own, rate_two[:, 2:-2]
-    )
-    grad_gate_one = item_sums(grad_hidden * branch_one_own)
-    grad_branch_one = (gate_one * grad_hidden).astype(BF16)
-    flat_grad = grad_branch_one.reshape(-1, width)
-    grad_out_bias = jnp.sum(flat_grad.astype(F32), axis=0)
-    grad_attended = contract_cols(flat_grad, out_full).astype(BF16).reshape(own_shape)
-    grad_unit = rows_to_unit(grad_attended)
-    grad_out_weight = contract_rows(attended[:, 2:-2].reshape(-1, width), flat_grad)
-
+    result, grad_hidden, grad_branch, blocks, late_sums, bias_sums = turn(
+        place,
+        branch_two,
+        grad_second,
+        hidden,
+        branch_one,
+        grad_out,
+        out_full,
+        down_bias_full[None],
+        mods,
+        canvases,
+        rows,
+        half,
+    )
+    bias_sums = jnp.sum(bias_sums, axis=1)
+    grad_out_bias, grad_down_bias = bias_sums[0], bias_sums[1]
     grad_parts, part_sums = attend_backward(
-        projected, query_item, key_item, grad_unit, attended_unit, lse
-    )
-    grad_qkv = jnp.concatenate([contract_rows(mixed_unit, grad_parts[k]) for k in range(3)], axis=1)
-    grad_qv_bias = jnp.stack([jnp.sum(part_sums[0], axis=0), jnp.sum(part_sums[2], axis=0)])
-    grad_mixed_unit = sum(
-        contract_cols(grad_parts[k], qkv_full[:, k * width : (k + 1) * width]) for k in range(3)
-    ).astype(BF16)
-    attn_grads = jnp.concatenate([grad_qkv, grad_out_weight], axis=1).astype(BF16)
+        projected, query_item, key_item, trade(blocks), attended_unit, lse, half
+    )
+    part_sums = jnp.sum(part_sums, axis=1)
+    grad_qv_bias = jnp.stack([part_sums[0], part_sums[2]])
+    blocks = trade(project_back(place, grad_parts, first_pair, n_fsdp, half))
+    attn_grads = attention_grads(mixed_unit, grad_parts, attended, grad_branch)
     attn_grads = lax.psum_scatter(attn_grads, EVERY, scatter_dimension=0, tiled=True)
     grad_qkv = attn_grads[:, : 3 * width].astype(F32)
     grad_out_weight = attn_grads[:, 3 * width :].astype(F32)
-
-    grad_mixed = unit_to_rows(grad_mixed_unit, half, rows, canvases)[:, 1:-1]
-    grad_mixed = keep_item(grad_mixed, 1)
-    own_mixed = grad_mixed[:, 1:-1].astype(F32)
-    grad_attn_shift = jnp.sum(own_mixed, axis=(0, 1, 2, 3))
-    grad_attn_kernel = tap_grads(first, own_mixed, big)
-    grad_first = conv(grad_mixed, attn_kernel_full[::-1], big)
-    normed_own = normed_one[:, 1:-1]
-    grad_scale_one = item_sums(grad_first * normed_own)
-    grad_shift_one = item_sums(grad_first)
-    grad_inputs = grad_hidden + layer_norm_back(
-        grad_first * (1.0 + scale_one), normed_own, rate_one[:, 1:-1]
-    )
-    grad_tokens = join_cols(grad_inputs.astype(BF16))[None]
-
+    grad_inputs, early_sums, tap_sums = finish(
+        flags, place, blocks, inputs, grad_hidden, attn_taps, mods, canvases, rows, half
+    )
+    grad_attn_kernel, grad_attn_shift = tap_sums[:9], tap_sums[9]
+    result = result.reshape(tokens.shape)
+    grad_tokens = grad_inputs.reshape(tokens.shape)
+
+    early_sums = jnp.sum(early_sums, axis=3)
+    late_sums = jnp.sum(late_sums, axis=3)
     local_grad = jnp.concatenate(
-        [
-            grad_shift_one,
-            grad_scale_one,
-            grad_gate_one,
-            grad_shift_two,
-            grad_scale_two,
-            grad_gate_two,
-        ],
+        [early_sums[:, 0], early_sums[:, 1], late_sums[:, 0], late_sums[:, 1], late_sums[:, 2], late_sums[:, 3]],
         axis=-1,
     )
     fsdp_bits = bits_of("fsdp")

time: 706 us -> 651 us (0.922); the launches traced: 694 us -> 650 us
  Pallas kernels: 169 us -> 259 us
  local copies, waits for them, and re-layouts: 130 us -> 49.2 us
  other arithmetic: 108 us -> 28.3 us
  waiting for transfers between devices: 208 us -> 261 us
  matrix products: 31.3 us -> 1.65 us
    pallas_call x3 -> x10, Pallas kernels: 169 us -> 259 us  [the longest x1 96.8 us: feed_forward(): pl.pallas_call(functools.partial(ffn_body, canvases, rows, half, lanes),...]
    ppermute x0 -> x12, waiting for transfers between devices: none -> 78.1 us  [trade(): moved[k] = lax.ppermute(parts[k], 'fsdp', [(i, i ^ k) for i in range(size)])]
    ppermute x30 -> x22, waiting for transfers between devices: 114 us -> 40.7 us  [swap(): return lax.ppermute(value, axis, [(i, i ^ bit) for i in range(size)])]
    reduce_scatter x1, waiting for transfers between devices: 94 us -> 138 us  [per_device(): lax.psum_scatter(ff_grads, EVERY, scatter_dimension=0, tiled=True)[0]]
    reduce_sum x19 -> x7, other arithmetic: 30.6 us -> 1.13 us  [the longest x1 0.93 us: per_device(): early_sums = jnp.sum(early_sums, axis=3)]
    dot_general x8 -> x0, matrix products: 19.9 us -> none  [the longest x4 12.4 us: contract_cols(): lax.dot_general(left_side, right_side, (((1,), (1,)), ((), ())), preferre...]
    unnamed x244 -> x60, local copies, waits for them, and re-layouts: 30.6 us -> 15.6 us
    concatenate x13 -> x1, local copies, waits for them, and re-layouts: 14.2 us -> 0.01 us  [per_device(): jnp.concatenate([early_sums[:, 0], early_sums[:, 1], late_sums[:, 0], lat...]
  transfers between devices with their start and end apart: 36 -> 40, of which waited for: 24 -> 25; matrix products, arithmetic and copies ran while one was open for 29% -> 9% of each run, Pallas kernels for 5% -> 14%
where the time goes in v2:
time: 651 us; the launch traced here: 650 us
  waiting for transfers between devices  261 us (40%)
  Pallas kernels  259 us (40%)
  local copies, waits for them, and re-layouts  49.2 us (8%)
  starting transfers between devices  35.9 us (6%)
  other arithmetic  28.3 us (4%)
  between operations  15.6 us (2%)
    reduce_scatter x1, waiting for transfers between devices, per_device(): lax.psum_scatter(ff_grads, EVERY, scatter_dimension=0, tiled=True)[0]  138 us
    pallas_call x1, Pallas kernels, feed_forward(): pl.pallas_call(functools.partial(ffn_body, canvases, rows, half, lanes),...  96.8 us
    ppermute x12, waiting for transfers between devices, trade(): moved[k] = lax.ppermute(parts[k], 'fsdp', [(i, i ^ k) for i in range(size)])  78.1 us
    pallas_call x4, Pallas kernels, whole_call(): pl.pallas_call(body, in_specs=[smem] * scalars + [vmem] * (len(inputs) -...  65.8 us
    ppermute x22, waiting for transfers between devices, swap(): return lax.ppermute(value, axis, [(i, i ^ bit) for i in range(size)])  40.7 us
    pallas_call x1, Pallas kernels, attend_backward(): pl.pallas_call(functools.partial(attend_backward_body, 256, count, half),...  40.4 us
    pallas_call x1, Pallas kernels, attend_forward(): pl.pallas_call(functools.partial(attend_forward_body, 256, count, half),...  33.4 us
    ppermute x22, starting transfers between devices, swap(): return lax.ppermute(value, axis, [(i, i ^ bit) for i in range(size)])  22.8 us
  transfers between devices with their start and end apart: 40, of which 25 were waited for; matrix products, arithmetic and copies ran while one was open for 9% of the time, Pallas kernels for 14%

profile of v2, /device:TPU:0, one launch (start us, length us, event | category | flops | bytes accessed | tf_op | source)
XLA Modules:
  0.0 650.0 jit_solution(11494355703769443950)
XLA Ops:
  7.3 1.7 pad_maximum_fusion.10
  10.0 1.7 pad_maximum_fusion.6
  15.3 4.1 concatenate.77
  19.4 4.1 collective-permute-start.2
  25.2 1.3 collective-permute-start.1
  27.3 3.8 collective-permute-start
  31.7 1.6 collective-permute-start.3
  33.4 2.1 collective-permute-done.3
  35.6 1.6 collective-permute-start.4
  37.1 2.3 collective-permute-done.4
  41.1 2.7 collective-permute-done.5
  48.6 1.2 collective-permute-done.10
  50.8 5.0 collective-permute-done.11
  56.5 8.1 %collective-permute-done.12 = f32[16,1152]{1,0:T(8,128)S(1)} collective-permute-done((f32[16,1152]{1,0:T(8,128)S(1)}, f32[16,1152]{1,0:T(8,128)S(1)}, u32[]{:S(2)}, u32[]{:S(2)}) %collective-permute-start.12) | collective-permute-done | bytes 73760 | tf_op jit(solution)/shard_map/ppermute | solution.py:31
  70.5 2.4 collective-permute-start.14
  72.9 1.6 pad_maximum_fusion.1
  75.6 1.4 pad_maximum_fusion.2
  77.0 14.2 %prepare.1 = (bf16[1280,768]{1,0:T(8,128)(2,1)}, bf16[1152,768]{1,0:T(8,128)(2,1)}, bf16[4,256,768]{2,1,0:T(8,128)(2,1)}) custom-call(f32[1,3]{1,0:T(1,128)} %pad_maximum_fusion.20.flag_ref, s32[10]{0:T(128)} %pad_add_fusion.place_ref, bf16[1280,768]{1,0:T(8,128)(2,1)} %bitcast.193, bf16[1152,768]{1,0:T(8,128)(2,1)} %bitcast.194, ...), custom_call_target="tpu_custom_call" | custom-call | flops 29491200 | bytes 9093172 | tf_op jit(solution)/shard_map/prepare/pallas_call | solution.py:546
  91.3 2.3 slice_bitcast_fusion.12
  93.7 2.1 collective-permute-start.9
  96.3 9.3 %collective-permute-done.9.refs_3_ = bf16[256,768]{1,0:T(8,128)(2,1)S(1)} collective-permute-done((bf16[256,768]{1,0:T(8,128)(2,1)}, bf16[256,768]{1,0:T(8,128)(2,1)S(1)}, u32[]{:S(2)}, u32[]{:S(2)}) %collective-permute-start.9) | collective-permute-done | bytes 393248 | tf_op jit(solution)/shard_map/ppermute | solution.py:949
  105.6 12.7 %collective-permute-done.8.refs_2_ = bf16[256,768]{1,0:T(8,128)(2,1)S(1)} collective-permute-done((bf16[256,768]{1,0:T(8,128)(2,1)}, bf16[256,768]{1,0:T(8,128)(2,1)S(1)}, u32[]{:S(2)}, u32[]{:S(2)}) %collective-permute-start.8) | collective-permute-done | bytes 393248 | tf_op jit(solution)/shard_map/ppermute | solution.py:949
  118.3 2.3 copy-done.3
  120.7 7.3 %project.1 = (bf16[1024,768]{1,0:T(8,128)(2,1)S(1)}, bf16[1024,2304]{1,0:T(8,128)(2,1)S(1)}) custom-call(s32[10]{0:T(128)S(1)} %copy-done.5, bf16[256,768]{1,0:T(8,128)(2,1)S(1)} %get-tuple-element.126.refs_0_, bf16[256,768]{1,0:T(8,128)(2,1)S(1)} %collective-permute-done.7.refs_1_, bf16[256,768]{1,0:T(8,128)(2,1)S(1)} %collective-permute-done.8.refs_2_, ...), custom_call_target="tpu_custom_call" | custom-call | flops 3623878656 | bytes 12582912 | tf_op jit(solution)/shard_map/project/pallas_call | solution.py:650
  128.0 33.4 %attend_forward.1 = (bf16[4,320,768]{2,1,0:T(8,128)(2,1)S(1)}, f32[6,8,1024]{2,1,0:T(8,128)S(1)}) custom-call(s32[10]{0:T(128)S(1)} %copy-done.5, bf16[1024,2304]{1,0:T(8,128)(2,1)S(1)} %get-tuple-element.44.query_ref.key_ref.value_ref, bf16[1024,2304]{1,0:T(8,128)(2,1)S(1)} %get-tuple-element.44.query_ref.key_ref.value_ref, ...), custom_call_target="tpu_custom_call" | custom-call | flops 6442450944 | bytes 8388608 | tf_op jit(solution)/shard_map/attend_forward/pallas_call | solution.py:393
  165.4 1.6 fusion.grad_ref
  167.1 2.4 slice.357.refs_5_.weight_ref
  169.4 6.3 collective-permute-done.19.refs_3_
  175.7 10.7 %collective-permute-done.18.refs_2_ = bf16[320,768]{1,0:T(8,128)(2,1)S(1)} collective-permute-done((bf16[320,768]{1,0:T(8,128)(2,1)S(1)}, bf16[320,768]{1,0:T(8,128)(2,1)S(1)}, u32[]{:S(2)}, u32[]{:S(2)}) %collective-permute-start.18) | collective-permute-done | bytes 491552 | tf_op jit(solution)/shard_map/ppermute | solution.py:949
  187.4 12.8 %middle.1 = (bf16[1280,768]{1,0:T(8,128)(2,1)}, f32[1024,768]{1,0:T(8,128)}, f32[1024,768]{1,0:T(8,128)}, bf16[1024,768]{1,0:T(8,128)(2,1)}) custom-call(f32[1,3]{1,0:T(1,128)} %pad_maximum_fusion.20.flag_ref, s32[10]{0:T(128)} %pad_add_fusion.place_ref, bf16[320,768]{1,0:T(8,128)(2,1)} %get-tuple-element.118.refs_0_, bf16[320,768]{1,0:T(8,128)(2,1)} %copy-done.23, ...), custom_call_target="tpu_custom_call" | custom-call | flops 1509949440 | bytes 16124980 | tf_op jit(solution)/shard_map/middle/pallas_call | solution.py:546
  200.2 96.8 %feed_forward.1 = (f32[1024,768]{1,0:T(8,128)}, f32[1024,768]{1,0:T(8,128)}, bf16[32,96,768]{2,1,0:T(8,128)(2,1)}, bf16[32,96,768]{2,1,0:T(8,128)(2,1)}, f32[16,3072]{1,0:T(8,128)}) custom-call(f32[1,3]{1,0:T(1,128)} %pad_maximum_fusion.20.flag_ref, bf16[1280,768]{1,0:T(8,128)(2,1)} %get-tuple-element.47.second_ref, bf16[1152,768]{1,0:T(8,128)(2,1)} %fusion.grad_ref, ...), custom_call_target="tpu_custom_call" | custom-call | flops 28991029248 | bytes 41943040 | tf_op jit(solution)/shard_map/feed_forward/pallas_call | solution.py:304
  297.0 18.2 %turn.1 = (bf16[1024,768]{1,0:T(8,128)(2,1)}, f32[1024,768]{1,0:T(8,128)}, bf16[1024,768]{1,0:T(8,128)(2,1)}, bf16[4,256,768]{2,1,0:T(8,128)(2,1)}, f32[1,4,2,8,768]{4,3,2,1,0:T(8,128)}, /*index=5*/f32[2,8,768]{2,1,0:T(8,128)}) custom-call(s32[10]{0:T(128)} %pad_add_fusion.place_ref, f32[1024,768]{1,0:T(8,128)} %get-tuple-element.49.branch_two_ref, ...), custom_call_target="tpu_custom_call" | custom-call | flops 1207959552 | bytes 24824872 | tf_op jit(solution)/shard_map/turn/pallas_call | solution.py:546
  315.2 1.5 slice_bitcast_fusion.8
  318.6 9.6 %collective-permute-done.22.refs_3_ = bf16[256,768]{1,0:T(8,128)(2,1)S(1)} collective-permute-done((bf16[256,768]{1,0:T(8,128)(2,1)S(1)}, bf16[256,768]{1,0:T(8,128)(2,1)S(1)}, u32[]{:S(2)}, u32[]{:S(2)}) %collective-permute-start.22) | collective-permute-done | bytes 393248 | tf_op jit(solution)/shard_map/ppermute | solution.py:949
  328.1 8.4 %collective-permute-done.21.refs_2_ = bf16[256,768]{1,0:T(8,128)(2,1)S(1)} collective-permute-done((bf16[256,768]{1,0:T(8,128)(2,1)S(1)}, bf16[256,768]{1,0:T(8,128)(2,1)S(1)}, u32[]{:S(2)}, u32[]{:S(2)}) %collective-permute-start.21) | collective-permute-done | bytes 393248 | tf_op jit(solution)/shard_map/ppermute | solution.py:949
  336.5 40.4 %attend_backward.1 = (bf16[3,1024,768]{2,1,0:T(8,128)(2,1)}, f32[3,8,768]{2,1,0:T(8,128)S(1)}) custom-call(bf16[1024,2304]{1,0:T(8,128)(2,1)} %copy-done.13, bf16[1024,2304]{1,0:T(8,128)(2,1)} %copy-done.13, bf16[1024,2304]{1,0:T(8,128)(2,1)} %copy-done.13, bf16[1024,128]{1,0:T(8,128)(2,1)S(1)} %fusion.2.query_item_ref, ...), custom_call_target="tpu_custom_call" | custom-call | flops 16106127360 | bytes 12582912 | tf_op jit(solution)/shard_map/attend_backward/pallas_call | solution.py:462
  376.9 2.3 copy-done.9
  379.2 9.5 %attention_grads.1 = bf16[768,3072]{1,0:T(8,128)(2,1)S(1)} custom-call(bf16[1024,768]{1,0:T(8,128)(2,1)S(1)} %copy-done.12, bf16[3,1024,768]{2,1,0:T(8,128)(2,1)S(1)} %copy-done.9, bf16[1024,768]{1,0:T(8,128)(2,1)S(1)} %copy-done.7, bf16[1024,768]{1,0:T(8,128)(2,1)S(1)} %copy-done.8), custom_call_target="tpu_custom_call" | custom-call | flops 4831838208 | bytes 14680064 | tf_op jit(solution)/shard_map/attention_grads/pallas_call | solution.py:979
  388.8 2.1 copy-done.2
  391.7 7.6 %pad_maximum_fusion = bf16[32,192,768]{2,1,0:T(8,128)(2,1)} fusion(bf16[32,96,768]{2,1,0:T(8,128)(2,1)} %get-tuple-element.69, bf16[32,96,768]{2,1,0:T(8,128)(2,1)} %get-tuple-element.68), kind=kLoop, calls=%fused_computation | loop fusion | flops 18874368 | bytes 18874368 | tf_op jit(solution)/shard_map/concatenate | solution.py:350
  399.4 2.5 copy-done.4
  401.8 2.5 copy-done.10
  404.3 5.4 project_back.1
  411.1 1.5 collective-permute-start.24
  414.0 10.3 %collective-permute-done.25.refs_3_ = bf16[320,768]{1,0:T(8,128)(2,1)S(1)} collective-permute-done((bf16[320,768]{1,0:T(8,128)(2,1)}, bf16[320,768]{1,0:T(8,128)(2,1)S(1)}, u32[]{:S(2)}, u32[]{:S(2)}) %collective-permute-start.25) | collective-permute-done | bytes 491552 | tf_op jit(solution)/shard_map/ppermute | solution.py:949
  424.3 10.8 %collective-permute-done.24.refs_2_ = bf16[320,768]{1,0:T(8,128)(2,1)S(1)} collective-permute-done((bf16[320,768]{1,0:T(8,128)(2,1)S(1)}, bf16[320,768]{1,0:T(8,128)(2,1)S(1)}, u32[]{:S(2)}, u32[]{:S(2)}) %collective-permute-start.24) | collective-permute-done | bytes 491552 | tf_op jit(solution)/shard_map/ppermute | solution.py:949
  436.1 20.6 %finish.1 = (bf16[1024,768]{1,0:T(8,128)(2,1)}, f32[1,2,2,8,768]{4,3,2,1,0:T(8,128)}, f32[16,768]{1,0:T(8,128)}) custom-call(f32[1,3]{1,0:T(1,128)} %pad_maximum_fusion.20.flag_ref, s32[10]{0:T(128)} %pad_add_fusion.place_ref, bf16[320,768]{1,0:T(8,128)(2,1)} %get-tuple-element.114.refs_0_, bf16[320,768]{1,0:T(8,128)(2,1)} %copy-done.20, ...), custom_call_target="tpu_custom_call" | custom-call | flops 47185920 | bytes 10027060 | tf_op jit(solution)/shard_map/finish/pallas_call | solution.py:546
  461.7 4.1 collective-permute-start.27
  466.0 1.1 collective-permute-start.32
  467.1 1.2 collective-permute-done.27
  468.3 2.7 collective-permute-done.32
  471.1 1.2 collective-permute-start.33
  472.4 2.5 collective-permute-done.33
  475.1 3.2 collective-permute-done.28
  479.3 1.3 collective-permute-start.29
  480.6 2.8 collective-permute-done.35
  485.8 1.3 collective-permute-start.30
  488.4 4.7 collective-permute-done.30
  494.8 1.3 fusion.21
  496.1 3.8 reduce-scatter.3.cloned.1.call-done
  500.0 1.4 slice_convert_fusion.1
  501.4 1.6 slice_convert_fusion
  503.0 138.0 %reduce-scatter.5.cloned.1.call-done = bf16[1,192,768]{2,1,0:T(8,128)(2,1)} async-done(((bf16[32,192,768]{2,1,0:T(8,128)(2,1)}), bf16[1,192,768]{2,1,0:T(8,128)(2,1)}) %reduce-scatter.5.cloned.1.call-update) | async-done | bytes 294928 | tf_op jit(solution)/shard_map/reduce_scatter | solution.py:1192
  641.0 1.7 fusion.5
  (276 shorter events, 46.2 us)
Async XLA Ops:
  7.2 40.5 %copy-start = (bf16[24,4608]{1,0:T(8,128)(2,1)S(1)}, bf16[24,4608]{1,0:T(8,128)(2,1)}, u32[]{:S(2)}) copy-start(bf16[24,4608]{1,0:T(8,128)(2,1)} %param.22) | copy-start | bytes 663556
  7.2 17.2 %copy-start.16 = (bf16[1,1,16,64,768]{4,3,2,1,0:T(8,128)(2,1)S(1)}, bf16[1,1,16,64,768]{4,3,2,1,0:T(8,128)(2,1)}, u32[]{:S(2)}) copy-start(bf16[1,1,16,64,768]{4,3,2,1,0:T(8,128)(2,1)} %param.18) | copy-start | bytes 4718596
  7.2 111.1 %all-gather.4.cloned.1.call-start = ((), (), s32[]{:S(2)}) async-start(), calls=%async_computation.2 | async-start | bytes 4866048 | tf_op jit(solution)/shard_map/all_gather | solution.py:1028
  9.0 191.2 %all-gather.6.cloned.1.call-start = ((), (), s32[]{:S(2)}) async-start(), calls=%async_computation.5 | async-start | bytes 9732096 | tf_op jit(solution)/shard_map/all_gather | solution.py:1034
  11.6 488.3 %reduce-scatter.3.cloned.1.call-start = ((), (), s32[]{:S(2)}) async-start(), calls=%async_computation.3 | async-start | bytes 4866048 | tf_op jit(solution)/shard_map/reduce_scatter | solution.py:1220
  19.4 12.3 %collective-permute-start.2 = (f32[1541]{0:T(1024)S(1)}, f32[1541]{0:T(1024)S(1)}, u32[]{:S(2)}, u32[]{:S(2)}) collective-permute-start(f32[1541]{0:T(1024)S(1)} %concatenate.77), channel_id=1, source_target_pairs={{0,16},{4,20},{8,24},{12,28},{16,0},{20,4},{24,8},{28,12},{1,17},{... | collective-permute-start | bytes 18500 | tf_op jit(solution)/shard_map/ppermute | solution.py:31
  25.2 44.3 %collective-permute-start.1 = (bf16[1,3,64,768]{3,2,1,0:T(8,128)(2,1)}, bf16[1,3,64,768]{3,2,1,0:T(8,128)(2,1)S(1)}, u32[]{:S(2)}, u32[]{:S(2)}) collective-permute-start(bf16[1,3,64,768]{3,2,1,0:T(8,128)(2,1)} %pad_maximum_fusion.5), channel_id=1, source_target_pairs={{1,0},{2,1},{3,2},{5,4},{6,5},{7,6},{9,8},{10,9},{11,10},{13,12},{... | collective-permute-start | bytes 884744 | tf_op jit(solution)/shard_map/ppermute | solution.py:1115
  27.3 42.3 %collective-permute-start = (bf16[1,3,64,768]{3,2,1,0:T(8,128)(2,1)}, bf16[1,3,64,768]{3,2,1,0:T(8,128)(2,1)}, u32[]{:S(2)}, u32[]{:S(2)}) collective-permute-start(bf16[1,3,64,768]{3,2,1,0:T(8,128)(2,1)} %pad_maximum_fusion.4), channel_id=1, source_target_pairs={{0,1},{1,2},{2,3},{4,5},{5,6},{6,7},{8,9},{9,10},{10,11},{12,13},{... | collective-permute-start | bytes 884744 | tf_op jit(solution)/shard_map/ppermute | solution.py:1114
  31.7 3.8 collective-permute-start.3
  35.6 3.9 collective-permute-start.4
  39.5 4.3 collective-permute-start.5
  43.9 1.4 collective-permute-start.6
  48.1 1.6 collective-permute-start.10
  49.8 6.0 collective-permute-start.11
  55.9 8.7 %collective-permute-start.12 = (f32[16,1152]{1,0:T(8,128)S(1)}, f32[16,1152]{1,0:T(8,128)S(1)}, u32[]{:S(2)}, u32[]{:S(2)}) collective-permute-start(f32[16,1152]{1,0:T(8,128)S(1)} %constant_dynamic-slice_fusion.9), channel_id=1, source_target_pairs={{0,16},{4,20},{8,24},{12,28},{16,0},{20,4},{24,8},{28,12},{1,17},{... | collective-permute-start | bytes 221192 | tf_op jit(solution)/shard_map/ppermute | solution.py:31
  64.6 5.8 collective-permute-start.13
  70.5 5.0 copy-start.17
  70.5 4.9 collective-permute-start.14
  75.5 15.8 %collective-permute-start.15 = (f32[4,1152]{1,0:T(4,128)S(1)}, f32[4,1152]{1,0:T(4,128)S(1)}, u32[]{:S(2)}, u32[]{:S(2)}) collective-permute-start(f32[4,1152]{1,0:T(4,128)S(1)} %dynamic-slice_add_fusion.7), channel_id=1, source_target_pairs={{0,2},{1,3},{2,0},{3,1},{4,6},{5,7},{6,4},{7,5},{8,10},{9,11},{10,... | collective-permute-start | bytes 55304 | tf_op jit(solution)/shard_map/ppermute | solution.py:31
  91.3 4.6 collective-permute-start.16
  93.7 11.9 %collective-permute-start.9 = (bf16[256,768]{1,0:T(8,128)(2,1)}, bf16[256,768]{1,0:T(8,128)(2,1)S(1)}, u32[]{:S(2)}, u32[]{:S(2)}) collective-permute-start(bf16[256,768]{1,0:T(8,128)(2,1)} %get-tuple-element.123), channel_id=1, source_target_pairs={{0,3},{1,2},{2,1},{3,0},{4,7},{5,6},{6,5},{7,4},{8,11},{9,10},{10,... | collective-permute-start | bytes 1179656 | tf_op jit(solution)/shard_map/ppermute | solution.py:949
  95.8 22.5 %collective-permute-start.8 = (bf16[256,768]{1,0:T(8,128)(2,1)}, bf16[256,768]{1,0:T(8,128)(2,1)S(1)}, u32[]{:S(2)}, u32[]{:S(2)}) collective-permute-start(bf16[256,768]{1,0:T(8,128)(2,1)} %get-tuple-element.124), channel_id=1, source_target_pairs={{0,2},{1,3},{2,0},{3,1},{4,6},{5,7},{6,4},{7,5},{8,10},{9,11},{10,... | collective-permute-start | bytes 1179656 | tf_op jit(solution)/shard_map/ppermute | solution.py:949
  95.8 22.5 %collective-permute-start.7 = (bf16[256,768]{1,0:T(8,128)(2,1)S(1)}, bf16[256,768]{1,0:T(8,128)(2,1)S(1)}, u32[]{:S(2)}, u32[]{:S(2)}) collective-permute-start(bf16[256,768]{1,0:T(8,128)(2,1)S(1)} %get-tuple-element.125), channel_id=1, source_target_pairs={{0,1},{1,0},{2,3},{3,2},{4,5},{5,4},{6,7},{7,6},{8,9},{9,8},{10,11... | collective-permute-start | bytes 1179656 | tf_op jit(solution)/shard_map/ppermute | solution.py:949
  95.9 22.3 %copy-start.5 = (s32[10]{0:T(128)S(1)}, s32[10]{0:T(128)}, u32[]{:S(2)}) copy-start(s32[10]{0:T(128)} %pad_add_fusion.place_ref) | copy-start | bytes 124
  118.3 2.4 copy-start.3
  128.0 33.4 %copy-start.11 = (bf16[1024,768]{1,0:T(8,128)(2,1)}, bf16[1024,768]{1,0:T(8,128)(2,1)S(1)}, u32[]{:S(2)}) copy-start(bf16[1024,768]{1,0:T(8,128)(2,1)S(1)} %get-tuple-element.65.mixed_ref) | copy-start | bytes 4718596
  128.0 33.4 %copy-start.13 = (bf16[1024,2304]{1,0:T(8,128)(2,1)}, bf16[1024,2304]{1,0:T(8,128)(2,1)S(1)}, u32[]{:S(2)}) copy-start(bf16[1024,2304]{1,0:T(8,128)(2,1)S(1)} %get-tuple-element.44.query_ref.key_ref.value_ref) | copy-start | bytes 14155780
  161.5 4.0 copy-start.15
  162.4 13.4 %collective-permute-start.19 = (bf16[320,768]{1,0:T(8,128)(2,1)S(1)}, bf16[320,768]{1,0:T(8,128)(2,1)S(1)}, u32[]{:S(2)}, u32[]{:S(2)}) collective-permute-start(bf16[320,768]{1,0:T(8,128)(2,1)S(1)} %get-tuple-element.115), channel_id=1, source_target_pairs={{0,3},{1,2},{2,1},{3,0},{4,7},{5,6},{6,5},{7,4},{8,11},{9,10},{10,... | collective-permute-start | bytes 1474568 | tf_op jit(solution)/shard_map/ppermute | solution.py:949
  163.2 23.3 %collective-permute-start.18 = (bf16[320,768]{1,0:T(8,128)(2,1)S(1)}, bf16[320,768]{1,0:T(8,128)(2,1)S(1)}, u32[]{:S(2)}, u32[]{:S(2)}) collective-permute-start(bf16[320,768]{1,0:T(8,128)(2,1)S(1)} %get-tuple-element.116), channel_id=1, source_target_pairs={{0,2},{1,3},{2,0},{3,1},{4,6},{5,7},{6,4},{7,5},{8,10},{9,11},{10,... | collective-permute-start | bytes 1474568 | tf_op jit(solution)/shard_map/ppermute | solution.py:949
  164.0 22.5 %collective-permute-start.17 = (bf16[320,768]{1,0:T(8,128)(2,1)S(1)}, bf16[320,768]{1,0:T(8,128)(2,1)S(1)}, u32[]{:S(2)}, u32[]{:S(2)}) collective-permute-start(bf16[320,768]{1,0:T(8,128)(2,1)S(1)} %get-tuple-element.117), channel_id=1, source_target_pairs={{0,1},{1,0},{2,3},{3,2},{4,5},{5,4},{6,7},{7,6},{8,9},{9,8},{10,11... | collective-permute-start | bytes 1474568 | tf_op jit(solution)/shard_map/ppermute | solution.py:949
  164.4 1.1 copy-start.14
  175.7 11.5 %copy-start.21 = (bf16[320,768]{1,0:T(8,128)(2,1)}, bf16[320,768]{1,0:T(8,128)(2,1)S(1)}, u32[]{:S(2)}) copy-start(bf16[320,768]{1,0:T(8,128)(2,1)S(1)} %collective-permute-done.19.refs_3_) | copy-start | bytes 1474564
  186.4 1.0 copy-start.22
  316.6 11.5 %collective-permute-start.22 = (bf16[256,768]{1,0:T(8,128)(2,1)S(1)}, bf16[256,768]{1,0:T(8,128)(2,1)S(1)}, u32[]{:S(2)}, u32[]{:S(2)}) collective-permute-start(bf16[256,768]{1,0:T(8,128)(2,1)S(1)} %get-tuple-element.119), channel_id=1, source_target_pairs={{0,3},{1,2},{2,1},{3,0},{4,7},{5,6},{6,5},{7,4},{8,11},{9,10},{10,... | collective-permute-start | bytes 1179656 | tf_op jit(solution)/shard_map/ppermute | solution.py:949
  317.5 18.9 %collective-permute-start.21 = (bf16[256,768]{1,0:T(8,128)(2,1)S(1)}, bf16[256,768]{1,0:T(8,128)(2,1)S(1)}, u32[]{:S(2)}, u32[]{:S(2)}) collective-permute-start(bf16[256,768]{1,0:T(8,128)(2,1)S(1)} %get-tuple-element.120), channel_id=1, source_target_pairs={{0,2},{1,3},{2,0},{3,1},{4,6},{5,7},{6,4},{7,5},{8,10},{9,11},{10,... | collective-permute-start | bytes 1179656 | tf_op jit(solution)/shard_map/ppermute | solution.py:949
  318.1 18.4 %collective-permute-start.20 = (bf16[256,768]{1,0:T(8,128)(2,1)S(1)}, bf16[256,768]{1,0:T(8,128)(2,1)S(1)}, u32[]{:S(2)}, u32[]{:S(2)}) collective-permute-start(bf16[256,768]{1,0:T(8,128)(2,1)S(1)} %get-tuple-element.121), channel_id=1, source_target_pairs={{0,1},{1,0},{2,3},{3,2},{4,5},{5,4},{6,7},{7,6},{8,9},{9,8},{10,11... | collective-permute-start | bytes 1179656 | tf_op jit(solution)/shard_map/ppermute | solution.py:949
  336.5 40.4 %copy-start.7 = (bf16[1024,768]{1,0:T(8,128)(2,1)S(1)}, bf16[1024,768]{1,0:T(8,128)(2,1)}, u32[]{:S(2)}) copy-start(bf16[1024,768]{1,0:T(8,128)(2,1)} %get-tuple-element.66.attended_ref) | copy-start | bytes 4718596
  336.5 40.4 %copy-start.8 = (bf16[1024,768]{1,0:T(8,128)(2,1)S(1)}, bf16[1024,768]{1,0:T(8,128)(2,1)}, u32[]{:S(2)}) copy-start(bf16[1024,768]{1,0:T(8,128)(2,1)} %get-tuple-element.67.grad_ref) | copy-start | bytes 4718596
  336.5 40.4 %copy-start.12 = (bf16[1024,768]{1,0:T(8,128)(2,1)S(1)}, bf16[1024,768]{1,0:T(8,128)(2,1)}, u32[]{:S(2)}) copy-start(bf16[1024,768]{1,0:T(8,128)(2,1)} %copy-done.11) | copy-start | bytes 4718596
  376.9 2.3 copy-start.9
  388.8 2.1 copy-start.2
  390.9 250.1 %reduce-scatter.5.cloned.1.call-start = ((), (), s32[]{:S(2)}) async-start(), calls=%async_computation.4 | async-start | bytes 9732096 | tf_op jit(solution)/shard_map/reduce_scatter | solution.py:1192
  391.7 7.6 %copy-start.6 = (s32[10]{0:T(128)S(1)}, s32[10]{0:T(128)}, u32[]{:S(2)}) copy-start(s32[10]{0:T(128)} %pad_add_fusion.place_ref) | copy-start | bytes 124
  399.4 2.5 copy-start.4
  401.8 2.5 copy-start.10
  409.7 3.2 copy-start.25
  409.7 3.3 copy-start.24
  410.8 13.5 %collective-permute-start.25 = (bf16[320,768]{1,0:T(8,128)(2,1)}, bf16[320,768]{1,0:T(8,128)(2,1)S(1)}, u32[]{:S(2)}, u32[]{:S(2)}) collective-permute-start(bf16[320,768]{1,0:T(8,128)(2,1)} %get-tuple-element.111), channel_id=1, source_target_pairs={{0,3},{1,2},{2,1},{3,0},{4,7},{5,6},{6,5},{7,4},{8,11},{9,10},{10,... | collective-permute-start | bytes 1474568 | tf_op jit(solution)/shard_map/ppermute | solution.py:949
  411.1 24.0 %collective-permute-start.24 = (bf16[320,768]{1,0:T(8,128)(2,1)S(1)}, bf16[320,768]{1,0:T(8,128)(2,1)S(1)}, u32[]{:S(2)}, u32[]{:S(2)}) collective-permute-start(bf16[320,768]{1,0:T(8,128)(2,1)S(1)} %get-tuple-element.112), channel_id=1, source_target_pairs={{0,2},{1,3},{2,0},{3,1},{4,6},{5,7},{6,4},{7,5},{8,10},{9,11},{10,... | collective-permute-start | bytes 1474568 | tf_op jit(solution)/shard_map/ppermute | solution.py:949
  412.6 22.5 %collective-permute-start.23 = (bf16[320,768]{1,0:T(8,128)(2,1)S(1)}, bf16[320,768]{1,0:T(8,128)(2,1)S(1)}, u32[]{:S(2)}, u32[]{:S(2)}) collective-permute-start(bf16[320,768]{1,0:T(8,128)(2,1)S(1)} %get-tuple-element.113), channel_id=1, source_target_pairs={{0,1},{1,0},{2,3},{3,2},{4,5},{5,4},{6,7},{7,6},{8,9},{9,8},{10,11... | collective-permute-start | bytes 1474568 | tf_op jit(solution)/shard_map/ppermute | solution.py:949
  424.3 10.8 %copy-start.18 = (bf16[320,768]{1,0:T(8,128)(2,1)}, bf16[320,768]{1,0:T(8,128)(2,1)S(1)}, u32[]{:S(2)}) copy-start(bf16[320,768]{1,0:T(8,128)(2,1)S(1)} %collective-permute-done.25.refs_3_) | copy-start | bytes 1474564
  435.1 1.0 copy-start.20
  460.1 5.7 collective-permute-start.31
  460.3 1.4 collective-permute-start.26
  461.7 6.6 %collective-permute-start.27 = (f32[1,2,4608]{2,1,0:T(2,128)S(1)}, f32[1,2,4608]{2,1,0:T(2,128)S(1)}, u32[]{:S(2)}, u32[]{:S(2)}) collective-permute-start(f32[1,2,4608]{2,1,0:T(2,128)S(1)} %add.297), channel_id=1, source_target_pairs={{0,16},{4,20},{8,24},{12,28},{16,0},{20,4},{24,8},{28,12},{1,17},{... | collective-permute-start | bytes 110600 | tf_op jit(solution)/shard_map/ppermute | solution.py:31
  466.0 5.1 collective-permute-start.32
  471.1 3.9 collective-permute-start.33
  472.4 6.0 collective-permute-start.28
  475.0 3.7 collective-permute-start.34
  478.8 4.6 collective-permute-start.35
  479.3 6.2 collective-permute-start.29
  485.8 7.3 %collective-permute-start.30 = (f32[2,2,2,1,2,4608]{5,4,2,1,0,3:T(2,128)S(1)}, f32[2,2,2,1,2,4608]{5,4,2,1,0,3:T(2,128)S(1)}, u32[]{:S(2)}, u32[]{:S(2)}) collective-permute-start(f32[2,2,2,1,2,4608]{5,4,2,1,0,3:T(2,128)S(1)} %pad_maximum_fusion.7), channel_id=1, source_target_pairs={{0,2},{1,3},{2,0},{3,1},{4,6},{5,7},{6,4},{7,5},{8,10},{9,11},{10,... | collective-permute-start | bytes 884744 | tf_op jit(solution)/shard_map/ppermute | solution.py:31
  493.5 150.0 %copy-start.1 = (bf16[24,4608]{1,0:T(8,128)(2,1)S(1)}, bf16[24,4608]{1,0:T(8,128)(2,1)}, u32[]{:S(2)}) copy-start(bf16[24,4608]{1,0:T(8,128)(2,1)} %param.22) | copy-start | bytes 663556
  (3 other events, 2.4 us)
Sparse Core Ops, SparseCore 0:
  10.9 66.3 all-gather.3
  80.2 82.1 all-gather.5
  391.1 108.8 reduce-scatter.2
  505.7 135.2 reduce-scatter.4
